TPU v7x, 32 devices: a whole 2x2x4 slice. The times are simulated.
32 devices in a mesh: section: 4 (over y, x), row: 2 (over core), col: 4 (over z).
Axes of the slice: x: 2, y: 2, z: 4, core: 2. Of those that a mesh axis runs over, the one named last changes fastest.
Arguments:
- cotangent: float32 [4, 128, 4096], P('section', None, ('row', 'col')), may hold values from -6 to 6
- incoming: float32 [4, 128, 4096], P('section', None, ('row', 'col')), may hold values from -6 to 6
- upd_u: float32 [4, 8, 128, 4096], P('section', None, None, ('row', 'col')), may hold values from -4 to 4
- upd_v: float32 [4, 8, 128, 4096], P('section', None, None, ('row', 'col')), may hold values from -0.0078125 to 0.0078125
- saved_x: bfloat16 [4, 4, 128, 4096], P('section', None, None, ('row', 'col')), may hold values from -6 to 6
- saved_h: bfloat16 [4, 4, 2, 128, 14336], P('section', None, None, None, 'col'), may hold values from -6 to 6
- norm_gain: float32 [4, 4096], P('section', ('row', 'col')), may hold values from 0.25 to 1.75
- w_gate: bfloat16 [4, 4096, 14336], P('section', 'row', 'col'), may hold values from -0.09375 to 0.09375
- w_up: bfloat16 [4, 4096, 14336], P('section', 'row', 'col'), may hold values from -0.09375 to 0.09375
- w_down: bfloat16 [4, 14336, 4096], P('section', 'col', 'row'), may hold values from -0.046875 to 0.046875
Outputs:
- new_cotangent: float32 [4, 128, 4096], P('section', None, ('row', 'col'))
- residual_out: float32 [4, 128, 4096], P('section', None, ('row', 'col'))
All inputs are finite; a program needn't handle non-finite values.
Results may differ from a plain program's by a relative error of at most 0.014.
Values may be sent and summed in bfloat16 or wider, within the bound.
No kernel may reach another device: no remote copies, remote signals or barrier semaphores. Data moves between devices by JAX's collectives and lax.ppermute only.
A program may use at most 128 MiB of HBM per device.

v0:
```python
import jax
import jax.numpy as jnp
from jax import lax
from jax.sharding import PartitionSpec as P

D = 4096


eps = 1e-05


def shifted(x, axis, by):
    devices = lax.axis_size(axis)
    return lax.ppermute(x, axis, [(i, (i + by) % devices) for i in range(devices)])


def rotate(carry):
    return shifted(carry, "section", -1)


def shards(cotangent, incoming, upd_u, upd_v, saved_x, saved_h, norm_gain, w_gate, w_up, w_down):
    sections = lax.axis_size("section")
    section_idx = lax.axis_index("section")
    inputs_all = saved_x[0].astype(jnp.float32)
    hidden_all = saved_h[0]
    gain = norm_gain[0]
    wg = w_gate[0]
    wu = w_up[0]
    wd = w_down[0]

    def layer_step(step, carry):
        carry = rotate(carry)
        micro = (section_idx + step + 1) % sections
        xf = lax.dynamic_index_in_dim(inputs_all, micro, 0, keepdims=False)
        hpair = lax.dynamic_index_in_dim(hidden_all, micro, 0, keepdims=False)
        sumsq = lax.psum(jnp.sum(xf * xf, axis=1), ("row", "col"))
        gy = carry.astype(jnp.bfloat16)
        wide = lax.all_gather(gy, "col", axis=1, tiled=True)
        ga_part = lax.dot_general(
            wide, wd, (((1,), (1,)), ((), ())), preferred_element_type=jnp.float32
        )
        ga = lax.psum_scatter(ga_part, "row", scatter_dimension=1, tiled=True)
        width = ga.shape[1]
        offset = lax.axis_index("row") * width
        hg = lax.dynamic_slice_in_dim(hpair[0], offset, width, 1).astype(jnp.float32)
        hu = lax.dynamic_slice_in_dim(hpair[1], offset, width, 1).astype(jnp.float32)
        sig = jax.nn.sigmoid(hg)
        part_gate = (ga * hu * sig * (1.0 + hg * (1.0 - sig))).astype(jnp.bfloat16)
        part_up = (ga * hg * sig).astype(jnp.bfloat16)
        grad_gate, grad_up = (
            lax.all_gather(part_gate, "row", axis=1, tiled=True),
            lax.all_gather(part_up, "row", axis=1, tiled=True),
        )
        first = lax.dot_general(
            wg, grad_gate, (((1,), (1,)), ((), ())), preferred_element_type=jnp.float32
        )
        second = lax.dot_general(
            wu, grad_up, (((1,), (1,)), ((), ())), preferred_element_type=jnp.float32
        )
        normgrad = lax.psum_scatter(first + second, "col", scatter_dimension=0, tiled=True).T
        rstd = lax.rsqrt(sumsq / D + eps)[:, None]
        scaled = gain * normgrad
        inner = lax.psum(jnp.sum(scaled * xf, axis=1), ("row", "col"))[:, None] / D
        updated = carry + rstd * scaled - xf * (rstd * rstd * rstd) * inner
        active = jnp.logical_and(step >= micro, step - micro < sections)
        return jnp.where(active, updated, carry)

    pulled = lax.fori_loop(0, 2 * sections - 1, layer_step, cotangent[0])
    pulled = rotate(pulled)
    resid = pulled + incoming[0] - cotangent[0]
    local_dots = jnp.einsum("urd,rd->u", upd_v[0], resid, precision=lax.Precision.HIGHEST)
    dots = lax.psum(local_dots, ("row", "col"))
    update = jnp.einsum("u,urd->rd", dots, upd_u[0], precision=lax.Precision.HIGHEST)
    fresh = cotangent[0] + resid - update
    return (fresh[None], resid[None])


def solution(mesh):
    placed = (
        P("section", None, ("row", "col")),
        P("section", None, ("row", "col")),
        P("section", None, None, ("row", "col")),
        P("section", None, None, ("row", "col")),
        P("section", None, None, ("row", "col")),
        P("section", None, None, None, "col"),
        P("section", ("row", "col")),
        P("section", "row", "col"),
        P("section", "row", "col"),
        P("section", "col", "row"),
    )
    return jax.shard_map(
        shards,
        mesh=mesh,
        in_specs=placed,
        out_specs=(P("section", None, ("row", "col")), P("section", None, ("row", "col"))),
        check_vma=False,
    )
```

profile of v0, /device:TPU:0, one launch (start us, length us, event | category | flops | bytes accessed | tf_op | source)
XLA Modules:
  0.0 880.5 jit_solution(12553855589407518897)
XLA Ops:
  10.2 832.8 %while.15 = (s32[]{:T(128)}, f32[128,512]{1,0:T(8,128)}, s32[]{:T(128)}, f32[4,128,512]{2,1,0:T(8,128)S(1)}, f32[1,512]{1,0:T(1,128)}, /*index=5*/bf16[3584,2048...) while((s32[]{:T(128)}, f32[128,512]{1,0:T(8,128)}, ...), condition=%wide.region_7.8_spmd, body=%wide.region_0.7_spmd.sunk | while | flops 5641699840 | bytes 72765032 | solution.py:68
  20.1 15.1 %all_gather.33 = bf16[128,2048]{1,0:T(8,128)(2,1)S(1)} all-gather(bf16[128,512]{1,0:T(8,128)(2,1)S(1)} %convert_element_type.72), channel_id=1, replica_groups=mesh['section'=4,'row'=2,'col'=4] {'col'}, dimensions={1}, use_global_device_ids=true | all-gather | bytes 655360 | tf_op jit(solution)/shard_map/while/body/eval_jaxpr/all_gather | solution.py:38
  35.3 11.4 %fusion.48 = f32[128,3584]{1,0:T(8,128)} fusion(bf16[128,2048]{1,0:T(8,128)(2,1)S(1)} %all_gather.33, bf16[3584,2048]{1,0:T(8,128)(2,1)} %get-tuple-element.365), kind=kOutput, calls=%fused_computation.40.clone.1 | convolution fusion | flops 1879048192 | bytes 17039360 | tf_op jit(solution)/shard_map/while/body/eval_jaxpr/dot_general | solution.py:39
  46.7 12.0 %reduce-scatter.3.cloned.1.call-done = f32[128,1792]{1,0:T(8,128)} async-done(((f32[128,3584]{1,0:T(8,128)}), f32[128,1792]{1,0:T(8,128)}) %reduce-scatter.3.cloned.1.call-update) | async-done | bytes 917520 | tf_op jit(solution)/shard_map/while/body/eval_jaxpr/reduce_scatter | solution.py:42
  65.5 9.9 %fusion.50 = f32[128,2048]{1,0:T(8,128)S(1)} fusion(bf16[128,3584]{1,0:T(8,128)(2,1)S(1)} %all_gather.34, bf16[2048,3584]{1,0:T(8,128)(2,1)} %get-tuple-element.367), kind=kOutput, calls=%fused_computation.41.clone.1 | convolution fusion | flops 1879048192 | bytes 16646144 | tf_op jit(solution)/shard_map/while/body/eval_jaxpr/dot_general | solution.py:54
  75.4 10.9 %fusion.51 = f32[2048,128]{0,1:T(8,128)} fusion(f32[128,2048]{1,0:T(8,128)S(1)} %fusion.50, bf16[128,3584]{1,0:T(8,128)(2,1)S(1)} %all_gather.35, bf16[2048,3584]{1,0:T(8,128)(2,1)} %get-tuple-element.368), kind=kOutput, calls=%fused_computation.1.clone.1 | convolution fusion | flops 1879310336 | bytes 17694720 | tf_op jit(solution)/shard_map/while/body/eval_jaxpr/dot_general | solution.py:57
  86.4 28.7 %reduce-scatter.5.cloned.1.call-done = f32[512,128]{0,1:T(8,128)} async-done(((f32[2048,128]{0,1:T(8,128)}), f32[512,128]{0,1:T(8,128)}) %reduce-scatter.5.cloned.1.call-update) | async-done | bytes 262160 | tf_op jit(solution)/shard_map/while/body/eval_jaxpr/reduce_scatter | solution.py:60
  116.2 13.7 %all-reduce.2 = (f32[128]{0:T(128)S(1)}, f32[128]{0:T(128)S(1)}) all-reduce(f32[128]{0:T(128)S(1)} %get-tuple-element.317, f32[128]{0:T(128)S(1)} %get-tuple-element.318), channel_id=1, replica_groups=mesh['section'=4,'row'=2,'col'=4] {'row','col'}, use_global_device_ids=true, to_apply=%region_6.6 | all-reduce | flops 256 | bytes 2048 | tf_op jit(solution)/shard_map/while/body/eval_jaxpr/psum | solution.py:63
  141.1 16.1 %all_gather.33 = bf16[128,2048]{1,0:T(8,128)(2,1)S(1)} all-gather(bf16[128,512]{1,0:T(8,128)(2,1)S(1)} %convert_element_type.72), channel_id=1, replica_groups=mesh['section'=4,'row'=2,'col'=4] {'col'}, dimensions={1}, use_global_device_ids=true | all-gather | bytes 655360 | tf_op jit(solution)/shard_map/while/body/eval_jaxpr/all_gather | solution.py:38
  157.2 11.3 %fusion.48 = f32[128,3584]{1,0:T(8,128)} fusion(bf16[128,2048]{1,0:T(8,128)(2,1)S(1)} %all_gather.33, bf16[3584,2048]{1,0:T(8,128)(2,1)} %get-tuple-element.365), kind=kOutput, calls=%fused_computation.40.clone.1 | convolution fusion | flops 1879048192 | bytes 17039360 | tf_op jit(solution)/shard_map/while/body/eval_jaxpr/dot_general | solution.py:39
  168.7 8.6 reduce-scatter.3.cloned.1.call-done
  184.1 9.9 %fusion.50 = f32[128,2048]{1,0:T(8,128)S(1)} fusion(bf16[128,3584]{1,0:T(8,128)(2,1)S(1)} %all_gather.34, bf16[2048,3584]{1,0:T(8,128)(2,1)} %get-tuple-element.367), kind=kOutput, calls=%fused_computation.41.clone.1 | convolution fusion | flops 1879048192 | bytes 16646144 | tf_op jit(solution)/shard_map/while/body/eval_jaxpr/dot_general | solution.py:54
  194.0 10.9 %fusion.51 = f32[2048,128]{0,1:T(8,128)} fusion(f32[128,2048]{1,0:T(8,128)S(1)} %fusion.50, bf16[128,3584]{1,0:T(8,128)(2,1)S(1)} %all_gather.35, bf16[2048,3584]{1,0:T(8,128)(2,1)} %get-tuple-element.368), kind=kOutput, calls=%fused_computation.1.clone.1 | convolution fusion | flops 1879310336 | bytes 17694720 | tf_op jit(solution)/shard_map/while/body/eval_jaxpr/dot_general | solution.py:57
  205.0 28.7 %reduce-scatter.5.cloned.1.call-done = f32[512,128]{0,1:T(8,128)} async-done(((f32[2048,128]{0,1:T(8,128)}), f32[512,128]{0,1:T(8,128)}) %reduce-scatter.5.cloned.1.call-update) | async-done | bytes 262160 | tf_op jit(solution)/shard_map/while/body/eval_jaxpr/reduce_scatter | solution.py:60
  234.8 13.7 %all-reduce.2 = (f32[128]{0:T(128)S(1)}, f32[128]{0:T(128)S(1)}) all-reduce(f32[128]{0:T(128)S(1)} %get-tuple-element.317, f32[128]{0:T(128)S(1)} %get-tuple-element.318), channel_id=1, replica_groups=mesh['section'=4,'row'=2,'col'=4] {'row','col'}, use_global_device_ids=true, to_apply=%region_6.6 | all-reduce | flops 256 | bytes 2048 | tf_op jit(solution)/shard_map/while/body/eval_jaxpr/psum | solution.py:63
  259.7 16.2 %all_gather.33 = bf16[128,2048]{1,0:T(8,128)(2,1)S(1)} all-gather(bf16[128,512]{1,0:T(8,128)(2,1)S(1)} %convert_element_type.72), channel_id=1, replica_groups=mesh['section'=4,'row'=2,'col'=4] {'col'}, dimensions={1}, use_global_device_ids=true | all-gather | bytes 655360 | tf_op jit(solution)/shard_map/while/body/eval_jaxpr/all_gather | solution.py:38
  275.8 11.3 %fusion.48 = f32[128,3584]{1,0:T(8,128)} fusion(bf16[128,2048]{1,0:T(8,128)(2,1)S(1)} %all_gather.33, bf16[3584,2048]{1,0:T(8,128)(2,1)} %get-tuple-element.365), kind=kOutput, calls=%fused_computation.40.clone.1 | convolution fusion | flops 1879048192 | bytes 17039360 | tf_op jit(solution)/shard_map/while/body/eval_jaxpr/dot_general | solution.py:39
  287.3 8.5 reduce-scatter.3.cloned.1.call-done
  302.6 9.9 %fusion.50 = f32[128,2048]{1,0:T(8,128)S(1)} fusion(bf16[128,3584]{1,0:T(8,128)(2,1)S(1)} %all_gather.34, bf16[2048,3584]{1,0:T(8,128)(2,1)} %get-tuple-element.367), kind=kOutput, calls=%fused_computation.41.clone.1 | convolution fusion | flops 1879048192 | bytes 16646144 | tf_op jit(solution)/shard_map/while/body/eval_jaxpr/dot_general | solution.py:54
  312.6 10.9 %fusion.51 = f32[2048,128]{0,1:T(8,128)} fusion(f32[128,2048]{1,0:T(8,128)S(1)} %fusion.50, bf16[128,3584]{1,0:T(8,128)(2,1)S(1)} %all_gather.35, bf16[2048,3584]{1,0:T(8,128)(2,1)} %get-tuple-element.368), kind=kOutput, calls=%fused_computation.1.clone.1 | convolution fusion | flops 1879310336 | bytes 17694720 | tf_op jit(solution)/shard_map/while/body/eval_jaxpr/dot_general | solution.py:57
  323.5 28.7 %reduce-scatter.5.cloned.1.call-done = f32[512,128]{0,1:T(8,128)} async-done(((f32[2048,128]{0,1:T(8,128)}), f32[512,128]{0,1:T(8,128)}) %reduce-scatter.5.cloned.1.call-update) | async-done | bytes 262160 | tf_op jit(solution)/shard_map/while/body/eval_jaxpr/reduce_scatter | solution.py:60
  353.3 13.7 %all-reduce.2 = (f32[128]{0:T(128)S(1)}, f32[128]{0:T(128)S(1)}) all-reduce(f32[128]{0:T(128)S(1)} %get-tuple-element.317, f32[128]{0:T(128)S(1)} %get-tuple-element.318), channel_id=1, replica_groups=mesh['section'=4,'row'=2,'col'=4] {'row','col'}, use_global_device_ids=true, to_apply=%region_6.6 | all-reduce | flops 256 | bytes 2048 | tf_op jit(solution)/shard_map/while/body/eval_jaxpr/psum | solution.py:63
  378.2 16.2 %all_gather.33 = bf16[128,2048]{1,0:T(8,128)(2,1)S(1)} all-gather(bf16[128,512]{1,0:T(8,128)(2,1)S(1)} %convert_element_type.72), channel_id=1, replica_groups=mesh['section'=4,'row'=2,'col'=4] {'col'}, dimensions={1}, use_global_device_ids=true | all-gather | bytes 655360 | tf_op jit(solution)/shard_map/while/body/eval_jaxpr/all_gather | solution.py:38
  394.4 11.3 %fusion.48 = f32[128,3584]{1,0:T(8,128)} fusion(bf16[128,2048]{1,0:T(8,128)(2,1)S(1)} %all_gather.33, bf16[3584,2048]{1,0:T(8,128)(2,1)} %get-tuple-element.365), kind=kOutput, calls=%fused_computation.40.clone.1 | convolution fusion | flops 1879048192 | bytes 17039360 | tf_op jit(solution)/shard_map/while/body/eval_jaxpr/dot_general | solution.py:39
  421.2 9.9 %fusion.50 = f32[128,2048]{1,0:T(8,128)S(1)} fusion(bf16[128,3584]{1,0:T(8,128)(2,1)S(1)} %all_gather.34, bf16[2048,3584]{1,0:T(8,128)(2,1)} %get-tuple-element.367), kind=kOutput, calls=%fused_computation.41.clone.1 | convolution fusion | flops 1879048192 | bytes 16646144 | tf_op jit(solution)/shard_map/while/body/eval_jaxpr/dot_general | solution.py:54
  431.1 10.9 %fusion.51 = f32[2048,128]{0,1:T(8,128)} fusion(f32[128,2048]{1,0:T(8,128)S(1)} %fusion.50, bf16[128,3584]{1,0:T(8,128)(2,1)S(1)} %all_gather.35, bf16[2048,3584]{1,0:T(8,128)(2,1)} %get-tuple-element.368), kind=kOutput, calls=%fused_computation.1.clone.1 | convolution fusion | flops 1879310336 | bytes 17694720 | tf_op jit(solution)/shard_map/while/body/eval_jaxpr/dot_general | solution.py:57
  442.0 28.7 %reduce-scatter.5.cloned.1.call-done = f32[512,128]{0,1:T(8,128)} async-done(((f32[2048,128]{0,1:T(8,128)}), f32[512,128]{0,1:T(8,128)}) %reduce-scatter.5.cloned.1.call-update) | async-done | bytes 262160 | tf_op jit(solution)/shard_map/while/body/eval_jaxpr/reduce_scatter | solution.py:60
  471.8 13.7 %all-reduce.2 = (f32[128]{0:T(128)S(1)}, f32[128]{0:T(128)S(1)}) all-reduce(f32[128]{0:T(128)S(1)} %get-tuple-element.317, f32[128]{0:T(128)S(1)} %get-tuple-element.318), channel_id=1, replica_groups=mesh['section'=4,'row'=2,'col'=4] {'row','col'}, use_global_device_ids=true, to_apply=%region_6.6 | all-reduce | flops 256 | bytes 2048 | tf_op jit(solution)/shard_map/while/body/eval_jaxpr/psum | solution.py:63
  496.7 16.2 %all_gather.33 = bf16[128,2048]{1,0:T(8,128)(2,1)S(1)} all-gather(bf16[128,512]{1,0:T(8,128)(2,1)S(1)} %convert_element_type.72), channel_id=1, replica_groups=mesh['section'=4,'row'=2,'col'=4] {'col'}, dimensions={1}, use_global_device_ids=true | all-gather | bytes 655360 | tf_op jit(solution)/shard_map/while/body/eval_jaxpr/all_gather | solution.py:38
  512.9 11.3 %fusion.48 = f32[128,3584]{1,0:T(8,128)} fusion(bf16[128,2048]{1,0:T(8,128)(2,1)S(1)} %all_gather.33, bf16[3584,2048]{1,0:T(8,128)(2,1)} %get-tuple-element.365), kind=kOutput, calls=%fused_computation.40.clone.1 | convolution fusion | flops 1879048192 | bytes 17039360 | tf_op jit(solution)/shard_map/while/body/eval_jaxpr/dot_general | solution.py:39
  539.7 9.9 %fusion.50 = f32[128,2048]{1,0:T(8,128)S(1)} fusion(bf16[128,3584]{1,0:T(8,128)(2,1)S(1)} %all_gather.34, bf16[2048,3584]{1,0:T(8,128)(2,1)} %get-tuple-element.367), kind=kOutput, calls=%fused_computation.41.clone.1 | convolution fusion | flops 1879048192 | bytes 16646144 | tf_op jit(solution)/shard_map/while/body/eval_jaxpr/dot_general | solution.py:54
  549.6 10.9 %fusion.51 = f32[2048,128]{0,1:T(8,128)} fusion(f32[128,2048]{1,0:T(8,128)S(1)} %fusion.50, bf16[128,3584]{1,0:T(8,128)(2,1)S(1)} %all_gather.35, bf16[2048,3584]{1,0:T(8,128)(2,1)} %get-tuple-element.368), kind=kOutput, calls=%fused_computation.1.clone.1 | convolution fusion | flops 1879310336 | bytes 17694720 | tf_op jit(solution)/shard_map/while/body/eval_jaxpr/dot_general | solution.py:57
  560.6 28.7 %reduce-scatter.5.cloned.1.call-done = f32[512,128]{0,1:T(8,128)} async-done(((f32[2048,128]{0,1:T(8,128)}), f32[512,128]{0,1:T(8,128)}) %reduce-scatter.5.cloned.1.call-update) | async-done | bytes 262160 | tf_op jit(solution)/shard_map/while/body/eval_jaxpr/reduce_scatter | solution.py:60
  590.4 13.7 %all-reduce.2 = (f32[128]{0:T(128)S(1)}, f32[128]{0:T(128)S(1)}) all-reduce(f32[128]{0:T(128)S(1)} %get-tuple-element.317, f32[128]{0:T(128)S(1)} %get-tuple-element.318), channel_id=1, replica_groups=mesh['section'=4,'row'=2,'col'=4] {'row','col'}, use_global_device_ids=true, to_apply=%region_6.6 | all-reduce | flops 256 | bytes 2048 | tf_op jit(solution)/shard_map/while/body/eval_jaxpr/psum | solution.py:63
  615.3 16.2 %all_gather.33 = bf16[128,2048]{1,0:T(8,128)(2,1)S(1)} all-gather(bf16[128,512]{1,0:T(8,128)(2,1)S(1)} %convert_element_type.72), channel_id=1, replica_groups=mesh['section'=4,'row'=2,'col'=4] {'col'}, dimensions={1}, use_global_device_ids=true | all-gather | bytes 655360 | tf_op jit(solution)/shard_map/while/body/eval_jaxpr/all_gather | solution.py:38
  631.5 11.3 %fusion.48 = f32[128,3584]{1,0:T(8,128)} fusion(bf16[128,2048]{1,0:T(8,128)(2,1)S(1)} %all_gather.33, bf16[3584,2048]{1,0:T(8,128)(2,1)} %get-tuple-element.365), kind=kOutput, calls=%fused_computation.40.clone.1 | convolution fusion | flops 1879048192 | bytes 17039360 | tf_op jit(solution)/shard_map/while/body/eval_jaxpr/dot_general | solution.py:39
  642.9 8.5 reduce-scatter.3.cloned.1.call-done
  658.2 9.9 %fusion.50 = f32[128,2048]{1,0:T(8,128)S(1)} fusion(bf16[128,3584]{1,0:T(8,128)(2,1)S(1)} %all_gather.34, bf16[2048,3584]{1,0:T(8,128)(2,1)} %get-tuple-element.367), kind=kOutput, calls=%fused_computation.41.clone.1 | convolution fusion | flops 1879048192 | bytes 16646144 | tf_op jit(solution)/shard_map/while/body/eval_jaxpr/dot_general | solution.py:54
  668.1 10.9 %fusion.51 = f32[2048,128]{0,1:T(8,128)} fusion(f32[128,2048]{1,0:T(8,128)S(1)} %fusion.50, bf16[128,3584]{1,0:T(8,128)(2,1)S(1)} %all_gather.35, bf16[2048,3584]{1,0:T(8,128)(2,1)} %get-tuple-element.368), kind=kOutput, calls=%fused_computation.1.clone.1 | convolution fusion | flops 1879310336 | bytes 17694720 | tf_op jit(solution)/shard_map/while/body/eval_jaxpr/dot_general | solution.py:57
  679.1 28.7 %reduce-scatter.5.cloned.1.call-done = f32[512,128]{0,1:T(8,128)} async-done(((f32[2048,128]{0,1:T(8,128)}), f32[512,128]{0,1:T(8,128)}) %reduce-scatter.5.cloned.1.call-update) | async-done | bytes 262160 | tf_op jit(solution)/shard_map/while/body/eval_jaxpr/reduce_scatter | solution.py:60
  708.9 13.7 %all-reduce.2 = (f32[128]{0:T(128)S(1)}, f32[128]{0:T(128)S(1)}) all-reduce(f32[128]{0:T(128)S(1)} %get-tuple-element.317, f32[128]{0:T(128)S(1)} %get-tuple-element.318), channel_id=1, replica_groups=mesh['section'=4,'row'=2,'col'=4] {'row','col'}, use_global_device_ids=true, to_apply=%region_6.6 | all-reduce | flops 256 | bytes 2048 | tf_op jit(solution)/shard_map/while/body/eval_jaxpr/psum | solution.py:63
  733.8 16.2 %all_gather.33 = bf16[128,2048]{1,0:T(8,128)(2,1)S(1)} all-gather(bf16[128,512]{1,0:T(8,128)(2,1)S(1)} %convert_element_type.72), channel_id=1, replica_groups=mesh['section'=4,'row'=2,'col'=4] {'col'}, dimensions={1}, use_global_device_ids=true | all-gather | bytes 655360 | tf_op jit(solution)/shard_map/while/body/eval_jaxpr/all_gather | solution.py:38
  750.0 11.3 %fusion.48 = f32[128,3584]{1,0:T(8,128)} fusion(bf16[128,2048]{1,0:T(8,128)(2,1)S(1)} %all_gather.33, bf16[3584,2048]{1,0:T(8,128)(2,1)} %get-tuple-element.365), kind=kOutput, calls=%fused_computation.40.clone.1 | convolution fusion | flops 1879048192 | bytes 17039360 | tf_op jit(solution)/shard_map/while/body/eval_jaxpr/dot_general | solution.py:39
  776.7 9.9 %fusion.50 = f32[128,2048]{1,0:T(8,128)S(1)} fusion(bf16[128,3584]{1,0:T(8,128)(2,1)S(1)} %all_gather.34, bf16[2048,3584]{1,0:T(8,128)(2,1)} %get-tuple-element.367), kind=kOutput, calls=%fused_computation.41.clone.1 | convolution fusion | flops 1879048192 | bytes 16646144 | tf_op jit(solution)/shard_map/while/body/eval_jaxpr/dot_general | solution.py:54
  786.7 10.9 %fusion.51 = f32[2048,128]{0,1:T(8,128)} fusion(f32[128,2048]{1,0:T(8,128)S(1)} %fusion.50, bf16[128,3584]{1,0:T(8,128)(2,1)S(1)} %all_gather.35, bf16[2048,3584]{1,0:T(8,128)(2,1)} %get-tuple-element.368), kind=kOutput, calls=%fused_computation.1.clone.1 | convolution fusion | flops 1879310336 | bytes 17694720 | tf_op jit(solution)/shard_map/while/body/eval_jaxpr/dot_general | solution.py:57
  797.6 28.7 %reduce-scatter.5.cloned.1.call-done = f32[512,128]{0,1:T(8,128)} async-done(((f32[2048,128]{0,1:T(8,128)}), f32[512,128]{0,1:T(8,128)}) %reduce-scatter.5.cloned.1.call-update) | async-done | bytes 262160 | tf_op jit(solution)/shard_map/while/body/eval_jaxpr/reduce_scatter | solution.py:60
  827.4 13.7 %all-reduce.2 = (f32[128]{0:T(128)S(1)}, f32[128]{0:T(128)S(1)}) all-reduce(f32[128]{0:T(128)S(1)} %get-tuple-element.317, f32[128]{0:T(128)S(1)} %get-tuple-element.318), channel_id=1, replica_groups=mesh['section'=4,'row'=2,'col'=4] {'row','col'}, use_global_device_ids=true, to_apply=%region_6.6 | all-reduce | flops 256 | bytes 2048 | tf_op jit(solution)/shard_map/while/body/eval_jaxpr/psum | solution.py:63
  855.4 14.0 %psum.35 = f32[8]{0:T(128)S(1)} all-reduce(f32[8]{0:T(128)S(1)} %fusion.16), channel_id=1, replica_groups=mesh['section'=4,'row'=2,'col'=4] {'row','col'}, use_global_device_ids=true, to_apply=%region_8.9 | all-reduce | flops 8 | bytes 64 | tf_op jit(solution)/shard_map/psum | solution.py:72
  (120 shorter events, 180.1 us)
Async XLA Ops:
  7.2 862.2 %copy-start = (f32[1,8,128,512]{3,2,1,0:T(8,128)S(1)}, f32[1,8,128,512]{3,2,1,0:T(8,128)}, u32[]{:S(2)}) copy-start(f32[1,8,128,512]{3,2,1,0:T(8,128)} %param.14) | copy-start | bytes 6291460
  10.2 48.5 %reduce-scatter.3.cloned.1.call-start = ((), (), s32[]{:S(2)}) async-start(), calls=%async_computation.2 | async-start | bytes 2752512 | tf_op jit(solution)/shard_map/while/body/eval_jaxpr/reduce_scatter | solution.py:42
  10.2 9.9 %collective-permute-start = (f32[128,512]{1,0:T(8,128)}, f32[128,512]{1,0:T(8,128)S(1)}, u32[]{:S(2)}, u32[]{:S(2)}) collective-permute-start(f32[128,512]{1,0:T(8,128)} %get-tuple-element.343), channel_id=1, source_target_pairs={{0,24},{8,0},{16,8},{24,16},{1,25},{9,1},{17,9},{25,17},{2,26},{10... | collective-permute-start | bytes 786440 | tf_op jit(solution)/shard_map/while/body/eval_jaxpr/ppermute | solution.py:14
  46.6 68.5 %reduce-scatter.5.cloned.1.call-start = ((), (), s32[]{:S(2)}) async-start(), calls=%async_computation.3 | async-start | bytes 1310720 | tf_op jit(solution)/shard_map/while/body/eval_jaxpr/reduce_scatter | solution.py:60
  75.4 39.7 %copy-start.2 = (f32[1,512]{1,0:T(1,128)S(1)}, f32[1,512]{1,0:T(1,128)}, u32[]{:S(2)}) copy-start(f32[1,512]{1,0:T(1,128)} %get-tuple-element.364) | copy-start | bytes 6148 | tf_op jit(solution)/shard_map/while
  131.7 45.6 %reduce-scatter.3.cloned.1.call-start = ((), (), s32[]{:S(2)}) async-start(), calls=%async_computation.2 | async-start | bytes 2752512 | tf_op jit(solution)/shard_map/while/body/eval_jaxpr/reduce_scatter | solution.py:42
  131.7 9.4 %collective-permute-start = (f32[128,512]{1,0:T(8,128)}, f32[128,512]{1,0:T(8,128)S(1)}, u32[]{:S(2)}, u32[]{:S(2)}) collective-permute-start(f32[128,512]{1,0:T(8,128)} %get-tuple-element.343), channel_id=1, source_target_pairs={{0,24},{8,0},{16,8},{24,16},{1,25},{9,1},{17,9},{25,17},{2,26},{10... | collective-permute-start | bytes 786440 | tf_op jit(solution)/shard_map/while/body/eval_jaxpr/ppermute | solution.py:14
  168.6 65.1 %reduce-scatter.5.cloned.1.call-start = ((), (), s32[]{:S(2)}) async-start(), calls=%async_computation.3 | async-start | bytes 1310720 | tf_op jit(solution)/shard_map/while/body/eval_jaxpr/reduce_scatter | solution.py:60
  194.0 39.7 %copy-start.2 = (f32[1,512]{1,0:T(1,128)S(1)}, f32[1,512]{1,0:T(1,128)}, u32[]{:S(2)}) copy-start(f32[1,512]{1,0:T(1,128)} %get-tuple-element.364) | copy-start | bytes 6148 | tf_op jit(solution)/shard_map/while
  250.3 45.6 %reduce-scatter.3.cloned.1.call-start = ((), (), s32[]{:S(2)}) async-start(), calls=%async_computation.2 | async-start | bytes 2752512 | tf_op jit(solution)/shard_map/while/body/eval_jaxpr/reduce_scatter | solution.py:42
  250.3 9.4 %collective-permute-start = (f32[128,512]{1,0:T(8,128)}, f32[128,512]{1,0:T(8,128)S(1)}, u32[]{:S(2)}, u32[]{:S(2)}) collective-permute-start(f32[128,512]{1,0:T(8,128)} %get-tuple-element.343), channel_id=1, source_target_pairs={{0,24},{8,0},{16,8},{24,16},{1,25},{9,1},{17,9},{25,17},{2,26},{10... | collective-permute-start | bytes 786440 | tf_op jit(solution)/shard_map/while/body/eval_jaxpr/ppermute | solution.py:14
  287.2 65.0 %reduce-scatter.5.cloned.1.call-start = ((), (), s32[]{:S(2)}) async-start(), calls=%async_computation.3 | async-start | bytes 1310720 | tf_op jit(solution)/shard_map/while/body/eval_jaxpr/reduce_scatter | solution.py:60
  312.6 39.7 %copy-start.2 = (f32[1,512]{1,0:T(1,128)S(1)}, f32[1,512]{1,0:T(1,128)}, u32[]{:S(2)}) copy-start(f32[1,512]{1,0:T(1,128)} %get-tuple-element.364) | copy-start | bytes 6148 | tf_op jit(solution)/shard_map/while
  368.8 45.5 %reduce-scatter.3.cloned.1.call-start = ((), (), s32[]{:S(2)}) async-start(), calls=%async_computation.2 | async-start | bytes 2752512 | tf_op jit(solution)/shard_map/while/body/eval_jaxpr/reduce_scatter | solution.py:42
  368.8 9.4 %collective-permute-start = (f32[128,512]{1,0:T(8,128)}, f32[128,512]{1,0:T(8,128)S(1)}, u32[]{:S(2)}, u32[]{:S(2)}) collective-permute-start(f32[128,512]{1,0:T(8,128)} %get-tuple-element.343), channel_id=1, source_target_pairs={{0,24},{8,0},{16,8},{24,16},{1,25},{9,1},{17,9},{25,17},{2,26},{10... | collective-permute-start | bytes 786440 | tf_op jit(solution)/shard_map/while/body/eval_jaxpr/ppermute | solution.py:14
  405.8 65.0 %reduce-scatter.5.cloned.1.call-start = ((), (), s32[]{:S(2)}) async-start(), calls=%async_computation.3 | async-start | bytes 1310720 | tf_op jit(solution)/shard_map/while/body/eval_jaxpr/reduce_scatter | solution.py:60
  431.1 39.7 %copy-start.2 = (f32[1,512]{1,0:T(1,128)S(1)}, f32[1,512]{1,0:T(1,128)}, u32[]{:S(2)}) copy-start(f32[1,512]{1,0:T(1,128)} %get-tuple-element.364) | copy-start | bytes 6148 | tf_op jit(solution)/shard_map/while
  487.4 45.5 %reduce-scatter.3.cloned.1.call-start = ((), (), s32[]{:S(2)}) async-start(), calls=%async_computation.2 | async-start | bytes 2752512 | tf_op jit(solution)/shard_map/while/body/eval_jaxpr/reduce_scatter | solution.py:42
  487.4 9.4 %collective-permute-start = (f32[128,512]{1,0:T(8,128)}, f32[128,512]{1,0:T(8,128)S(1)}, u32[]{:S(2)}, u32[]{:S(2)}) collective-permute-start(f32[128,512]{1,0:T(8,128)} %get-tuple-element.343), channel_id=1, source_target_pairs={{0,24},{8,0},{16,8},{24,16},{1,25},{9,1},{17,9},{25,17},{2,26},{10... | collective-permute-start | bytes 786440 | tf_op jit(solution)/shard_map/while/body/eval_jaxpr/ppermute | solution.py:14
  524.3 65.0 %reduce-scatter.5.cloned.1.call-start = ((), (), s32[]{:S(2)}) async-start(), calls=%async_computation.3 | async-start | bytes 1310720 | tf_op jit(solution)/shard_map/while/body/eval_jaxpr/reduce_scatter | solution.py:60
  549.6 39.7 %copy-start.2 = (f32[1,512]{1,0:T(1,128)S(1)}, f32[1,512]{1,0:T(1,128)}, u32[]{:S(2)}) copy-start(f32[1,512]{1,0:T(1,128)} %get-tuple-element.364) | copy-start | bytes 6148 | tf_op jit(solution)/shard_map/while
  605.9 45.5 %reduce-scatter.3.cloned.1.call-start = ((), (), s32[]{:S(2)}) async-start(), calls=%async_computation.2 | async-start | bytes 2752512 | tf_op jit(solution)/shard_map/while/body/eval_jaxpr/reduce_scatter | solution.py:42
  605.9 9.4 %collective-permute-start = (f32[128,512]{1,0:T(8,128)}, f32[128,512]{1,0:T(8,128)S(1)}, u32[]{:S(2)}, u32[]{:S(2)}) collective-permute-start(f32[128,512]{1,0:T(8,128)} %get-tuple-element.343), channel_id=1, source_target_pairs={{0,24},{8,0},{16,8},{24,16},{1,25},{9,1},{17,9},{25,17},{2,26},{10... | collective-permute-start | bytes 786440 | tf_op jit(solution)/shard_map/while/body/eval_jaxpr/ppermute | solution.py:14
  642.8 65.0 %reduce-scatter.5.cloned.1.call-start = ((), (), s32[]{:S(2)}) async-start(), calls=%async_computation.3 | async-start | bytes 1310720 | tf_op jit(solution)/shard_map/while/body/eval_jaxpr/reduce_scatter | solution.py:60
  668.1 39.7 %copy-start.2 = (f32[1,512]{1,0:T(1,128)S(1)}, f32[1,512]{1,0:T(1,128)}, u32[]{:S(2)}) copy-start(f32[1,512]{1,0:T(1,128)} %get-tuple-element.364) | copy-start | bytes 6148 | tf_op jit(solution)/shard_map/while
  724.4 45.5 %reduce-scatter.3.cloned.1.call-start = ((), (), s32[]{:S(2)}) async-start(), calls=%async_computation.2 | async-start | bytes 2752512 | tf_op jit(solution)/shard_map/while/body/eval_jaxpr/reduce_scatter | solution.py:42
  724.4 9.4 %collective-permute-start = (f32[128,512]{1,0:T(8,128)}, f32[128,512]{1,0:T(8,128)S(1)}, u32[]{:S(2)}, u32[]{:S(2)}) collective-permute-start(f32[128,512]{1,0:T(8,128)} %get-tuple-element.343), channel_id=1, source_target_pairs={{0,24},{8,0},{16,8},{24,16},{1,25},{9,1},{17,9},{25,17},{2,26},{10... | collective-permute-start | bytes 786440 | tf_op jit(solution)/shard_map/while/body/eval_jaxpr/ppermute | solution.py:14
  761.3 65.0 %reduce-scatter.5.cloned.1.call-start = ((), (), s32[]{:S(2)}) async-start(), calls=%async_computation.3 | async-start | bytes 1310720 | tf_op jit(solution)/shard_map/while/body/eval_jaxpr/reduce_scatter | solution.py:60
  786.6 39.7 %copy-start.2 = (f32[1,512]{1,0:T(1,128)S(1)}, f32[1,512]{1,0:T(1,128)}, u32[]{:S(2)}) copy-start(f32[1,512]{1,0:T(1,128)} %get-tuple-element.364) | copy-start | bytes 6148 | tf_op jit(solution)/shard_map/while
  842.9 9.4 %collective-permute-start.1 = (f32[128,512]{1,0:T(8,128)}, f32[128,512]{1,0:T(8,128)S(1)}, u32[]{:S(2)}, u32[]{:S(2)}) collective-permute-start(f32[128,512]{1,0:T(8,128)} %get-tuple-element.223), channel_id=1, source_target_pairs={{0,24},{8,0},{16,8},{24,16},{1,25},{9,1},{17,9},{25,17},{2,26},{10... | collective-permute-start | bytes 786440 | tf_op jit(solution)/shard_map/ppermute | solution.py:14
  853.4 20.6 %copy-start.1 = (f32[128,512]{1,0:T(8,128)}, f32[128,512]{1,0:T(8,128)S(1)}, u32[]{:S(2)}) copy-start(f32[128,512]{1,0:T(8,128)S(1)} %fusion.20) | copy-start | bytes 786436
Sparse Core Ops, SparseCore 0:
  46.7 11.8 reduce-scatter.2
  86.5 28.5 reduce-scatter.4
  168.7 8.5 reduce-scatter.2
  205.1 28.5 reduce-scatter.4
  287.3 8.4 reduce-scatter.2
  323.6 28.5 reduce-scatter.4
  405.9 8.4 reduce-scatter.2
  442.2 28.5 reduce-scatter.4
  524.4 8.4 reduce-scatter.2
  560.7 28.5 reduce-scatter.4
  642.9 8.4 reduce-scatter.2
  679.2 28.5 reduce-scatter.4
  761.5 8.4 reduce-scatter.2
  797.7 28.5 reduce-scatter.4
where the time goes:
time: 882 us; the launch traced here: 881 us
  waiting for transfers between devices  319 us (36%)
  blocking collectives  256 us (29%)
  matrix products  228 us (26%)
  other arithmetic  39.4 us (4%)
  starting transfers between devices  21 us (2%)
  between operations  13.7 us (2%)
    reduce_scatter x7, waiting for transfers between devices, layer_step(): lax.psum_scatter(first + second, 'col', scatter_dimension=0, tiled=True)  201 us
    all_gather x7, blocking collectives, layer_step(): wide = lax.all_gather(gy, 'col', axis=1, tiled=True)  112 us
    psum x7, blocking collectives, layer_step(): inner = lax.psum(jnp.sum(scaled * xf, axis=1), ('row', 'col'))[:, None] / D  95.9 us
    dot_general x7, matrix products, layer_step(): lax.dot_general(wide, wd, (((1,), (1,)), ((), ())), preferred_element_typ...  79.4 us
    dot_general x7, matrix products, layer_step(): lax.dot_general(wu, grad_up, (((1,), (1,)), ((), ())), preferred_element_...  76.5 us
    dot_general x7, matrix products, layer_step(): lax.dot_general(wg, grad_gate, (((1,), (1,)), ((), ())), preferred_elemen...  69.4 us
    reduce_scatter x7, waiting for transfers between devices, layer_step(): ga = lax.psum_scatter(ga_part, 'row', scatter_dimension=1, tiled=True)  63.1 us
    ppermute x8, waiting for transfers between devices, shifted(): lax.ppermute(x, axis, [(i, (i + by) % devices) for i in range(devices)])  54.8 us
  transfers between devices with their start and end apart: 22, of which 22 were waited for; matrix products, arithmetic and copies ran while one was open for 0% of the time, Pallas kernels for 0%

commit v1 on v0

--- a/solution.py
+++ b/solution.py
@@ -1,12 +1,20 @@
+import functools
+
 import jax
 import jax.numpy as jnp
 from jax import lax
+from jax.experimental import pallas as pl
+from jax.experimental.pallas import tpu as pltpu
 from jax.sharding import PartitionSpec as P
 
 D = 4096
 
 
 eps = 1e-05
+
+NT = (((1,), (1,)), ((), ()))
+VMEM = pl.BlockSpec(memory_space=pltpu.VMEM)
+ANY = pl.BlockSpec(memory_space=pl.ANY)
 
 
 def shifted(x, axis, by):
@@ -18,7 +26,196 @@
     return shifted(carry, "section", -1)
 
 
+def spread(x, by):
+    sections, cols = lax.axis_size("section"), lax.axis_size("col")
+    pairs = [
+        (s * cols + c, ((s - 1) % sections) * cols + (c + by) % cols)
+        for s in range(sections)
+        for c in range(cols)
+    ]
+    return lax.ppermute(x, ("section", "col"), pairs)
+
+
+def group_sum(x):
+    rows, cols = lax.axis_size("row"), lax.axis_size("col")
+    total = x
+    for r in range(rows):
+        for c in range(cols):
+            if r == 0 and c == 0:
+                continue
+            pairs = [
+                (i * cols + j, ((i + r) % rows) * cols + (j + c) % cols)
+                for i in range(rows)
+                for j in range(cols)
+            ]
+            total = total + lax.ppermute(x, ("row", "col"), pairs)
+    return total
+
+
+def down_kernel(cols, depth, tile, *refs):
+    pieces, w_ref, o_ref = refs[:cols], refs[cols], refs[cols + 1]
+    buf, gy, sem = refs[cols + 2 :]
+    tiles = w_ref.shape[0] // tile
+    chunk = gy.shape[1] // cols
+
+    def fetch(i):
+        return pltpu.make_async_copy(
+            w_ref.at[pl.ds(i * tile, tile)], buf.at[i % depth], sem.at[i % depth]
+        )
+
+    for i in range(min(depth, tiles)):
+        fetch(i).start()
+    col = lax.axis_index("col")
+    for j in range(cols):
+        source = lax.rem(col + cols - j, cols)
+        gy[:, pl.ds(pl.multiple_of(source * chunk, chunk), chunk)] = pieces[j][...]
+    for i in range(tiles):
+        fetch(i).wait()
+        o_ref[:, i * tile : (i + 1) * tile] = lax.dot_general(
+            gy[...], buf[i % depth], NT, preferred_element_type=jnp.float32
+        ).astype(o_ref.dtype)
+        if i + depth < tiles:
+            fetch(i + depth).start()
+
+
+def down(pieces, wd):
+    cols = len(pieces)
+    rows = pieces[0].shape[0]
+    width, feats = wd.shape
+    tile, depth = 512, 5
+    return pl.pallas_call(
+        functools.partial(down_kernel, cols, depth, tile),
+        in_specs=[VMEM] * cols + [ANY],
+        out_specs=VMEM,
+        out_shape=jax.ShapeDtypeStruct((rows, width), jnp.bfloat16),
+        scratch_shapes=[
+            pltpu.VMEM((depth, tile, feats), wd.dtype),
+            pltpu.VMEM((rows, feats), jnp.bfloat16),
+            pltpu.SemaphoreType.DMA((depth,)),
+        ],
+        compiler_params=pltpu.CompilerParams(vmem_limit_bytes=24 << 20),
+        cost_estimate=pl.CostEstimate(
+            flops=2 * rows * width * feats, bytes_accessed=2 * width * feats, transcendentals=0
+        ),
+    )(*pieces, wd)
+
+
+def up_kernel(step, cols, depth, tile, ga_ref, gb_ref, h_ref, wg_ref, wu_ref, *refs):
+    outs = refs[:cols]
+    hbuf, gate, upper, gbuf, ubuf, hsem, sem = refs[cols:]
+    feats, width = wg_ref.shape
+    chunk = feats // cols
+    parts = chunk // tile
+    sections = h_ref.shape[1]
+    micro = lax.rem(lax.axis_index("section") + step + 1, sections)
+    col = lax.axis_index("col")
+    order = [(j, p) for j in list(range(1, cols)) + [0] for p in range(parts)]
+
+    def fetch(i):
+        j, p = order[i]
+        dest = lax.rem(col + j, cols)
+        first = pl.multiple_of(dest * chunk + p * tile, tile)
+        s = i % depth
+        return (
+            pltpu.make_async_copy(wg_ref.at[pl.ds(first, tile)], gbuf.at[s], sem.at[0, s]),
+            pltpu.make_async_copy(wu_ref.at[pl.ds(first, tile)], ubuf.at[s], sem.at[1, s]),
+        )
+
+    hcopy = pltpu.make_async_copy(h_ref.at[0, micro], hbuf, hsem.at[0])
+    hcopy.start()
+    for i in range(min(depth, len(order))):
+        for c in fetch(i):
+            c.start()
+    hcopy.wait()
+    block = 512
+    for b in range(width // block):
+        at = slice(b * block, (b + 1) * block)
+        ga = ga_ref[:, at].astype(jnp.float32) + gb_ref[:, at].astype(jnp.float32)
+        hg = hbuf[0, :, at].astype(jnp.float32)
+        hu = hbuf[1, :, at].astype(jnp.float32)
+        sig = jax.nn.sigmoid(hg)
+        gate[:, at] = (ga * hu * sig * (1.0 + hg * (1.0 - sig))).astype(jnp.bfloat16)
+        upper[:, at] = (ga * hg * sig).astype(jnp.bfloat16)
+    for i, (j, p) in enumerate(order):
+        for c in fetch(i):
+            c.wait()
+        s = i % depth
+        acc = lax.dot_general(gate[...], gbuf[s], NT, preferred_element_type=jnp.float32)
+        acc += lax.dot_general(upper[...], ubuf[s], NT, preferred_element_type=jnp.float32)
+        outs[j][:, p * tile : (p + 1) * tile] = acc.astype(outs[j].dtype)
+        if i + depth < len(order):
+            for c in fetch(i + depth):
+                c.start()
+
+
+def up(step, ga, gb, hidden, wg, wu, cols):
+    rows = ga.shape[0]
+    feats, width = wg.shape
+    chunk = feats // cols
+    tile, depth = 256, 4
+    return pl.pallas_call(
+        functools.partial(up_kernel, step, cols, depth, tile),
+        in_specs=[VMEM, VMEM, ANY, ANY, ANY],
+        out_specs=[VMEM] * cols,
+        out_shape=[
+            jax.ShapeDtypeStruct((rows, chunk), jnp.float32 if j == 0 else jnp.bfloat16)
+            for j in range(cols)
+        ],
+        scratch_shapes=[
+            pltpu.VMEM((2, rows, width), hidden.dtype),
+            pltpu.VMEM((rows, width), jnp.bfloat16),
+            pltpu.VMEM((rows, width), jnp.bfloat16),
+            pltpu.VMEM((depth, tile, width), wg.dtype),
+            pltpu.VMEM((depth, tile, width), wu.dtype),
+            pltpu.SemaphoreType.DMA((1,)),
+            pltpu.SemaphoreType.DMA((2, depth)),
+        ],
+        compiler_params=pltpu.CompilerParams(vmem_limit_bytes=40 << 20),
+        cost_estimate=pl.CostEstimate(
+            flops=4 * rows * width * feats, bytes_accessed=4 * width * feats, transcendentals=0
+        ),
+    )(ga, gb, hidden, wg, wu)
+
+
 def shards(cotangent, incoming, upd_u, upd_v, saved_x, saved_h, norm_gain, w_gate, w_up, w_down):
+    sections, cols = lax.axis_size("section"), lax.axis_size("col")
+    section_idx = lax.axis_index("section")
+    inputs_all = saved_x[0].astype(jnp.float32)
+    gain = norm_gain[0]
+    wg, wu, wd = w_gate[0], w_up[0], w_down[0]
+    sumsq_all = group_sum(jnp.sum(inputs_all * inputs_all, axis=2))
+    rstd_all = lax.rsqrt(sumsq_all / D + eps)
+
+    carry = cotangent[0]
+    for step in range(2 * sections - 1):
+        gy = carry.astype(jnp.bfloat16)
+        pieces = [spread(gy, j) for j in range(cols)]
+        carry = rotate(carry)
+        micro = (section_idx + step + 1) % sections
+        ga = down(pieces, wd)
+        gb = shifted(ga, "row", 1)
+        outs = up(step, ga, gb, saved_h, wg, wu, cols)
+        normgrad = outs[0]
+        for j in range(1, cols):
+            normgrad = normgrad + shifted(outs[j], "col", j).astype(jnp.float32)
+        xf = lax.dynamic_index_in_dim(inputs_all, micro, 0, keepdims=False)
+        rstd = lax.dynamic_index_in_dim(rstd_all, micro, 0, keepdims=False)[:, None]
+        scaled = gain * normgrad
+        inner = group_sum(jnp.sum(scaled * xf, axis=1))[:, None] / D
+        updated = carry + rstd * scaled - xf * (rstd * rstd * rstd) * inner
+        active = jnp.logical_and(step >= micro, step - micro < sections)
+        carry = jnp.where(active, updated, carry)
+
+    pulled = rotate(carry)
+    resid = pulled + incoming[0] - cotangent[0]
+    local_dots = jnp.einsum("urd,rd->u", upd_v[0], resid, precision=lax.Precision.HIGHEST)
+    dots = group_sum(local_dots)
+    update = jnp.einsum("u,urd->rd", dots, upd_u[0], precision=lax.Precision.HIGHEST)
+    fresh = cotangent[0] + resid - update
+    return (fresh[None], resid[None])
+
+
+def plain_shards(cotangent, incoming, upd_u, upd_v, saved_x, saved_h, norm_gain, w_gate, w_up, w_down):
     sections = lax.axis_size("section")
     section_idx = lax.axis_index("section")
     inputs_all = saved_x[0].astype(jnp.float32)
@@ -36,9 +233,7 @@
         sumsq = lax.psum(jnp.sum(xf * xf, axis=1), ("row", "col"))
         gy = carry.astype(jnp.bfloat16)
         wide = lax.all_gather(gy, "col", axis=1, tiled=True)
-        ga_part = lax.dot_general(
-            wide, wd, (((1,), (1,)), ((), ())), preferred_element_type=jnp.float32
-        )
+        ga_part = lax.dot_general(wide, wd, NT, preferred_element_type=jnp.float32)
         ga = lax.psum_scatter(ga_part, "row", scatter_dimension=1, tiled=True)
         width = ga.shape[1]
         offset = lax.axis_index("row") * width
@@ -47,16 +242,10 @@
         sig = jax.nn.sigmoid(hg)
         part_gate = (ga * hu * sig * (1.0 + hg * (1.0 - sig))).astype(jnp.bfloat16)
         part_up = (ga * hg * sig).astype(jnp.bfloat16)
-        grad_gate, grad_up = (
-            lax.all_gather(part_gate, "row", axis=1, tiled=True),
-            lax.all_gather(part_up, "row", axis=1, tiled=True),
-        )
-        first = lax.dot_general(
-            wg, grad_gate, (((1,), (1,)), ((), ())), preferred_element_type=jnp.float32
-        )
-        second = lax.dot_general(
-            wu, grad_up, (((1,), (1,)), ((), ())), preferred_element_type=jnp.float32
-        )
+        grad_gate = lax.all_gather(part_gate, "row", axis=1, tiled=True)
+        grad_up = lax.all_gather(part_up, "row", axis=1, tiled=True)
+        first = lax.dot_general(wg, grad_gate, NT, preferred_element_type=jnp.float32)
+        second = lax.dot_general(wu, grad_up, NT, preferred_element_type=jnp.float32)
         normgrad = lax.psum_scatter(first + second, "col", scatter_dimension=0, tiled=True).T
         rstd = lax.rsqrt(sumsq / D + eps)[:, None]
         scaled = gain * normgrad
@@ -88,8 +277,15 @@
         P("section", "row", "col"),
         P("section", "col", "row"),
     )
+
+    def body(*args):
+        chunk, width = args[0].shape[2], args[7].shape[2]
+        if lax.axis_size("row") == 2 and chunk % 256 == 0 and width % 512 == 0:
+            return shards(*args)
+        return plain_shards(*args)
+
     return jax.shard_map(
-        shards,
+        body,
         mesh=mesh,
         in_specs=placed,
         out_specs=(P("section", None, ("row", "col")), P("section", None, ("row", "col"))),

time: 882 us -> 609 us (0.69)
  blocking collectives: 256 us -> 0 us
  matrix products: 228 us -> 2.84 us
  Pallas kernels: 0 us -> 182 us
  waiting for transfers between devices: 319 us -> 164 us
  starting transfers between devices: 21 us -> 167 us
  local copies, waits for them, and re-layouts: 1.88 us -> 53.2 us
  between operations: 13.7 us -> 1.44 us
  other arithmetic: 39.4 us -> 28 us
    reduce_scatter x14 -> x0, waiting for transfers between devices: 264 us -> none  [the longest x7 201 us: layer_step(): lax.psum_scatter(first + second, 'col', scatter_dimension=0, tiled=True)]
    dot_general x21 -> x0, matrix products: 225 us -> none  [the longest x7 79.4 us: layer_step(): lax.dot_general(wide, wd, (((1,), (1,)), ((), ())), preferred_element_typ...]
    pallas_call x0 -> x14, Pallas kernels: none -> 182 us  [the longest x7 134 us: up(): pl.pallas_call(functools.partial(up_kernel, step, cols, depth, tile), in_...]
    all_gather x21 -> x0, blocking collectives: 147 us -> none  [the longest x7 112 us: layer_step(): wide = lax.all_gather(gy, 'col', axis=1, tiled=True)]
    ppermute x0 -> x91, starting transfers between devices: none -> 119 us  [the longest x63 73.3 us: group_sum(): total = total + lax.ppermute(x, ('row', 'col'), pairs)]
    psum x8 -> x0, blocking collectives: 110 us -> none  [the longest x7 95.9 us: layer_step(): inner = lax.psum(jnp.sum(scaled * xf, axis=1), ('row', 'col'))[:, None] / D]
    ppermute x0 -> x91, waiting for transfers between devices: none -> 102 us  [the longest x28 57.4 us: spread(): return lax.ppermute(x, ('section', 'col'), pairs)]
    unnamed x5 -> x74, local copies, waits for them, and re-layouts: 1.84 us -> 53.2 us
  transfers between devices with their start and end apart: 22 -> 127, of which waited for: 22 -> 75; matrix products, arithmetic and copies ran while one was open for 0% -> 2% of each run, Pallas kernels for 0% -> 0%
where the time goes in v1:
time: 609 us; the launch traced here: 599 us
  Pallas kernels  182 us (30%)
  starting transfers between devices  167 us (27%)
  waiting for transfers between devices  164 us (27%)
  local copies, waits for them, and re-layouts  53.2 us (9%)
  other arithmetic  28 us (5%)
    pallas_call x7, Pallas kernels, up(): pl.pallas_call(functools.partial(up_kernel, step, cols, depth, tile), in_...  134 us
    ppermute x63, starting transfers between devices, group_sum(): total = total + lax.ppermute(x, ('row', 'col'), pairs)  73.3 us
    ppermute x36, waiting for transfers between devices, shifted(): lax.ppermute(x, axis, [(i, (i + by) % devices) for i in range(devices)])  62 us
    ppermute x28, waiting for transfers between devices, spread(): return lax.ppermute(x, ('section', 'col'), pairs)  57.4 us
    unnamed x74, local copies, waits for them, and re-layouts  53.2 us
    pallas_call x7, Pallas kernels, down(): pl.pallas_call(functools.partial(down_kernel, cols, depth, tile), in_spec...  48.2 us
    ppermute x36, starting transfers between devices, shifted(): lax.ppermute(x, axis, [(i, (i + by) % devices) for i in range(devices)])  47.9 us
    ppermute x28, starting transfers between devices, spread(): return lax.ppermute(x, ('section', 'col'), pairs)  45.8 us
  transfers between devices with their start and end apart: 127, of which 75 were waited for; matrix products, arithmetic and copies ran while one was open for 2% of the time, Pallas kernels for 0%

profile of v1, /device:TPU:0, one launch (start us, length us, event | category | flops | bytes accessed | tf_op | source)
XLA Modules:
  0.0 598.8 jit_solution(8824275541904491409)
XLA Ops:
  1.8 7.0 %collective-permute-start.11 = (bf16[128,512]{1,0:T(8,128)(2,1)S(1)}, bf16[128,512]{1,0:T(8,128)(2,1)S(1)}, u32[]{:S(2)}, u32[]{:S(2)}) collective-permute-start(bf16[128,512]{1,0:T(8,128)(2,1)S(1)} %bitcast_convert_fusion), channel_id=1, source_target_pairs={{0,27},{1,24},{2,25},{3,26},{8,3},{9,0},{10,1},{11,2},{16,11},{17,... | collective-permute-start | bytes 393224 | tf_op jit(solution)/shard_map/ppermute | solution.py:36
  12.7 7.3 %collective-permute-done.10.refs_2_ = bf16[128,512]{1,0:T(8,128)(2,1)S(1)} collective-permute-done((bf16[128,512]{1,0:T(8,128)(2,1)S(1)}, bf16[128,512]{1,0:T(8,128)(2,1)S(1)}, u32[]{:S(2)}, u32[]{:S(2)}) %collective-permute-start.10) | collective-permute-done | bytes 131104 | tf_op jit(solution)/shard_map/ppermute | solution.py:36
  20.9 5.2 copy-done.1
  26.1 6.9 %shard_map.113.ga_ref = bf16[128,3584]{1,0:T(8,128)(2,1)S(1)} custom-call(bf16[128,512]{1,0:T(8,128)(2,1)S(1)} %collective-permute-done.8.refs_0_, bf16[128,512]{1,0:T(8,128)(2,1)S(1)} %collective-permute-done.9.refs_1_, bf16[128,512]{1,0:T(8,128)(2,1)S(1)} %collective-permute-done.10.refs_2_, bf16[128,512]{1,0:T(8,128)(2,1)S(1)} %collective-permute-done.11.refs_3_, ...), custom_call_target="tpu_custom_call" | custom-call | flops 1879048192 | bytes 14680064 | tf_op jit(solution)/shard_map/pallas_call | solution.py:86
  35.5 19.1 %shard_map.114 = (f32[128,512]{1,0:T(8,128)S(1)}, bf16[128,512]{1,0:T(8,128)(2,1)S(1)}, bf16[128,512]{1,0:T(8,128)(2,1)S(1)}, bf16[128,512]{1,0:T(8,128)(2,1)S(1)}) custom-call(bf16[128,3584]{1,0:T(8,128)(2,1)S(1)} %shard_map.113.ga_ref, bf16[128,3584]{1,0:T(8,128)(2,1)S(1)} %collective-permute-done.12.gb_ref, bf16[1,4,2,128,3584]{4,3,2,1,0:T(8,128)(2,1)S(1)} %copy-done.8, ...), custom_call_target="tpu_custom_call" | custom-call | flops 3758096384 | bytes 29360128 | tf_op jit(solution)/shard_map/pallas_call | solution.py:156
  65.6 4.5 collective-permute-start.5
  98.1 6.2 %collective-permute-done.26.refs_2_ = bf16[128,512]{1,0:T(8,128)(2,1)S(1)} collective-permute-done((bf16[128,512]{1,0:T(8,128)(2,1)S(1)}, bf16[128,512]{1,0:T(8,128)(2,1)S(1)}, u32[]{:S(2)}, u32[]{:S(2)}) %collective-permute-start.26) | collective-permute-done | bytes 131104 | tf_op jit(solution)/shard_map/ppermute | solution.py:36
  105.0 5.2 copy-done.2
  110.2 6.9 %shard_map.115.ga_ref = bf16[128,3584]{1,0:T(8,128)(2,1)S(1)} custom-call(bf16[128,512]{1,0:T(8,128)(2,1)S(1)} %collective-permute-done.24.refs_0_, bf16[128,512]{1,0:T(8,128)(2,1)S(1)} %collective-permute-done.25.refs_1_, bf16[128,512]{1,0:T(8,128)(2,1)S(1)} %collective-permute-done.26.refs_2_, bf16[128,512]{1,0:T(8,128)(2,1)S(1)} %collective-permute-done.27.refs_3_, ...), custom_call_target="tpu_custom_call" | custom-call | flops 1879048192 | bytes 14680064 | tf_op jit(solution)/shard_map/pallas_call | solution.py:86
  119.6 19.1 %shard_map.116 = (f32[128,512]{1,0:T(8,128)S(1)}, bf16[128,512]{1,0:T(8,128)(2,1)S(1)}, bf16[128,512]{1,0:T(8,128)(2,1)S(1)}, bf16[128,512]{1,0:T(8,128)(2,1)S(1)}) custom-call(bf16[128,3584]{1,0:T(8,128)(2,1)S(1)} %shard_map.115.ga_ref, bf16[128,3584]{1,0:T(8,128)(2,1)S(1)} %collective-permute-done.28.gb_ref, bf16[1,4,2,128,3584]{4,3,2,1,0:T(8,128)(2,1)S(1)} %copy-done.9, ...), custom_call_target="tpu_custom_call" | custom-call | flops 3758096384 | bytes 29360128 | tf_op jit(solution)/shard_map/pallas_call | solution.py:156
  147.0 4.8 collective-permute-done.30
  156.7 4.3 collective-permute-start.34
  162.4 3.3 collective-permute-done.33
  177.2 6.0 collective-permute-done.42.refs_2_
  184.1 5.2 copy-done.3
  189.3 6.9 %shard_map.117.ga_ref = bf16[128,3584]{1,0:T(8,128)(2,1)S(1)} custom-call(bf16[128,512]{1,0:T(8,128)(2,1)S(1)} %collective-permute-done.40.refs_0_, bf16[128,512]{1,0:T(8,128)(2,1)S(1)} %collective-permute-done.41.refs_1_, bf16[128,512]{1,0:T(8,128)(2,1)S(1)} %collective-permute-done.42.refs_2_, bf16[128,512]{1,0:T(8,128)(2,1)S(1)} %collective-permute-done.43.refs_3_, ...), custom_call_target="tpu_custom_call" | custom-call | flops 1879048192 | bytes 14680064 | tf_op jit(solution)/shard_map/pallas_call | solution.py:86
  201.8 19.1 %shard_map.118 = (f32[128,512]{1,0:T(8,128)S(1)}, bf16[128,512]{1,0:T(8,128)(2,1)S(1)}, bf16[128,512]{1,0:T(8,128)(2,1)S(1)}, bf16[128,512]{1,0:T(8,128)(2,1)S(1)}) custom-call(bf16[128,3584]{1,0:T(8,128)(2,1)S(1)} %shard_map.117.ga_ref, bf16[128,3584]{1,0:T(8,128)(2,1)S(1)} %collective-permute-done.44.gb_ref, bf16[1,4,2,128,3584]{4,3,2,1,0:T(8,128)(2,1)S(1)} %copy-done.10, ...), custom_call_target="tpu_custom_call" | custom-call | flops 3758096384 | bytes 29360128 | tf_op jit(solution)/shard_map/pallas_call | solution.py:156
  229.3 4.8 collective-permute-done.46
  239.3 4.0 collective-permute-start.50
  244.7 3.3 collective-permute-done.49
  259.6 5.7 collective-permute-done.58.refs_2_
  266.5 5.2 copy-done.4
  271.7 6.9 %shard_map.119.ga_ref = bf16[128,3584]{1,0:T(8,128)(2,1)S(1)} custom-call(bf16[128,512]{1,0:T(8,128)(2,1)S(1)} %collective-permute-done.56.refs_0_, bf16[128,512]{1,0:T(8,128)(2,1)S(1)} %collective-permute-done.57.refs_1_, bf16[128,512]{1,0:T(8,128)(2,1)S(1)} %collective-permute-done.58.refs_2_, bf16[128,512]{1,0:T(8,128)(2,1)S(1)} %collective-permute-done.59.refs_3_, ...), custom_call_target="tpu_custom_call" | custom-call | flops 1879048192 | bytes 14680064 | tf_op jit(solution)/shard_map/pallas_call | solution.py:86
  284.2 19.1 %shard_map.120 = (f32[128,512]{1,0:T(8,128)S(1)}, bf16[128,512]{1,0:T(8,128)(2,1)S(1)}, bf16[128,512]{1,0:T(8,128)(2,1)S(1)}, bf16[128,512]{1,0:T(8,128)(2,1)S(1)}) custom-call(bf16[128,3584]{1,0:T(8,128)(2,1)S(1)} %shard_map.119.ga_ref, bf16[128,3584]{1,0:T(8,128)(2,1)S(1)} %collective-permute-done.60.gb_ref, bf16[1,4,2,128,3584]{4,3,2,1,0:T(8,128)(2,1)S(1)} %copy-done.11, ...), custom_call_target="tpu_custom_call" | custom-call | flops 3758096384 | bytes 29360128 | tf_op jit(solution)/shard_map/pallas_call | solution.py:156
  311.6 4.8 collective-permute-done.62
  321.4 4.7 collective-permute-start.66
  341.5 6.3 %collective-permute-done.74.refs_2_ = bf16[128,512]{1,0:T(8,128)(2,1)S(1)} collective-permute-done((bf16[128,512]{1,0:T(8,128)(2,1)S(1)}, bf16[128,512]{1,0:T(8,128)(2,1)S(1)}, u32[]{:S(2)}, u32[]{:S(2)}) %collective-permute-start.74) | collective-permute-done | bytes 131104 | tf_op jit(solution)/shard_map/ppermute | solution.py:36
  348.4 5.2 copy-done.5
  353.6 6.9 %shard_map.121.ga_ref = bf16[128,3584]{1,0:T(8,128)(2,1)S(1)} custom-call(bf16[128,512]{1,0:T(8,128)(2,1)S(1)} %collective-permute-done.72.refs_0_, bf16[128,512]{1,0:T(8,128)(2,1)S(1)} %collective-permute-done.73.refs_1_, bf16[128,512]{1,0:T(8,128)(2,1)S(1)} %collective-permute-done.74.refs_2_, bf16[128,512]{1,0:T(8,128)(2,1)S(1)} %collective-permute-done.75.refs_3_, ...), custom_call_target="tpu_custom_call" | custom-call | flops 1879048192 | bytes 14680064 | tf_op jit(solution)/shard_map/pallas_call | solution.py:86
  363.0 19.1 %shard_map.122 = (f32[128,512]{1,0:T(8,128)S(1)}, bf16[128,512]{1,0:T(8,128)(2,1)S(1)}, bf16[128,512]{1,0:T(8,128)(2,1)S(1)}, bf16[128,512]{1,0:T(8,128)(2,1)S(1)}) custom-call(bf16[128,3584]{1,0:T(8,128)(2,1)S(1)} %shard_map.121.ga_ref, bf16[128,3584]{1,0:T(8,128)(2,1)S(1)} %collective-permute-done.76.gb_ref, bf16[1,4,2,128,3584]{4,3,2,1,0:T(8,128)(2,1)S(1)} %copy-done.12, ...), custom_call_target="tpu_custom_call" | custom-call | flops 3758096384 | bytes 29360128 | tf_op jit(solution)/shard_map/pallas_call | solution.py:156
  390.5 4.7 collective-permute-done.78
  400.2 4.4 collective-permute-start.82
  415.9 3.3 collective-permute-start.89
  420.6 6.2 %collective-permute-done.90.refs_2_ = bf16[128,512]{1,0:T(8,128)(2,1)S(1)} collective-permute-done((bf16[128,512]{1,0:T(8,128)(2,1)S(1)}, bf16[128,512]{1,0:T(8,128)(2,1)S(1)}, u32[]{:S(2)}, u32[]{:S(2)}) %collective-permute-start.90) | collective-permute-done | bytes 131104 | tf_op jit(solution)/shard_map/ppermute | solution.py:36
  427.6 5.2 copy-done.6
  432.7 6.9 %shard_map.123.ga_ref = bf16[128,3584]{1,0:T(8,128)(2,1)S(1)} custom-call(bf16[128,512]{1,0:T(8,128)(2,1)S(1)} %collective-permute-done.88.refs_0_, bf16[128,512]{1,0:T(8,128)(2,1)S(1)} %collective-permute-done.89.refs_1_, bf16[128,512]{1,0:T(8,128)(2,1)S(1)} %collective-permute-done.90.refs_2_, bf16[128,512]{1,0:T(8,128)(2,1)S(1)} %collective-permute-done.91.refs_3_, ...), custom_call_target="tpu_custom_call" | custom-call | flops 1879048192 | bytes 14680064 | tf_op jit(solution)/shard_map/pallas_call | solution.py:86
  445.2 19.1 %shard_map.124 = (f32[128,512]{1,0:T(8,128)S(1)}, bf16[128,512]{1,0:T(8,128)(2,1)S(1)}, bf16[128,512]{1,0:T(8,128)(2,1)S(1)}, bf16[128,512]{1,0:T(8,128)(2,1)S(1)}) custom-call(bf16[128,3584]{1,0:T(8,128)(2,1)S(1)} %shard_map.123.ga_ref, bf16[128,3584]{1,0:T(8,128)(2,1)S(1)} %collective-permute-done.92.gb_ref, bf16[1,4,2,128,3584]{4,3,2,1,0:T(8,128)(2,1)S(1)} %copy-done.13, ...), custom_call_target="tpu_custom_call" | custom-call | flops 3758096384 | bytes 29360128 | tf_op jit(solution)/shard_map/pallas_call | solution.py:156
  472.7 4.8 collective-permute-done.94
  482.4 4.6 collective-permute-start.98
  497.7 3.3 collective-permute-start.105
  502.6 6.1 %collective-permute-done.106.refs_2_ = bf16[128,512]{1,0:T(8,128)(2,1)S(1)} collective-permute-done((bf16[128,512]{1,0:T(8,128)(2,1)S(1)}, bf16[128,512]{1,0:T(8,128)(2,1)S(1)}, u32[]{:S(2)}, u32[]{:S(2)}) %collective-permute-start.106) | collective-permute-done | bytes 131104 | tf_op jit(solution)/shard_map/ppermute | solution.py:36
  509.5 5.2 copy-done.7
  514.7 6.9 %shard_map.125.ga_ref = bf16[128,3584]{1,0:T(8,128)(2,1)S(1)} custom-call(bf16[128,512]{1,0:T(8,128)(2,1)S(1)} %collective-permute-done.104.refs_0_, bf16[128,512]{1,0:T(8,128)(2,1)S(1)} %collective-permute-done.105.refs_1_, bf16[128,512]{1,0:T(8,128)(2,1)S(1)} %collective-permute-done.106.refs_2_, bf16[128,512]{1,0:T(8,128)(2,1)S(1)} %collective-permute-done.107.refs_3_, ...), custom_call_target="tpu_custom_call" | custom-call | flops 1879048192 | bytes 14680064 | tf_op jit(solution)/shard_map/pallas_call | solution.py:86
  527.2 19.1 %shard_map.126 = (f32[128,512]{1,0:T(8,128)S(1)}, bf16[128,512]{1,0:T(8,128)(2,1)S(1)}, bf16[128,512]{1,0:T(8,128)(2,1)S(1)}, bf16[128,512]{1,0:T(8,128)(2,1)S(1)}) custom-call(bf16[128,3584]{1,0:T(8,128)(2,1)S(1)} %shard_map.125.ga_ref, bf16[128,3584]{1,0:T(8,128)(2,1)S(1)} %collective-permute-done.108.gb_ref, bf16[1,4,2,128,3584]{4,3,2,1,0:T(8,128)(2,1)S(1)} %copy-done.14, ...), custom_call_target="tpu_custom_call" | custom-call | flops 3758096384 | bytes 29360128 | tf_op jit(solution)/shard_map/pallas_call | solution.py:156
  554.6 4.8 collective-permute-done.110
  563.8 4.4 collective-permute-start.114
  569.5 3.3 collective-permute-done.113
  578.9 4.3 collective-permute-done.119
  (324 shorter events, 248.3 us)
Async XLA Ops:
  1.8 10.9 %collective-permute-start.11 = (bf16[128,512]{1,0:T(8,128)(2,1)S(1)}, bf16[128,512]{1,0:T(8,128)(2,1)S(1)}, u32[]{:S(2)}, u32[]{:S(2)}) collective-permute-start(bf16[128,512]{1,0:T(8,128)(2,1)S(1)} %bitcast_convert_fusion), channel_id=1, source_target_pairs={{0,27},{1,24},{2,25},{3,26},{8,3},{9,0},{10,1},{11,2},{16,11},{17,... | collective-permute-start | bytes 393224 | tf_op jit(solution)/shard_map/ppermute | solution.py:36
  8.8 11.2 %collective-permute-start.10 = (bf16[128,512]{1,0:T(8,128)(2,1)S(1)}, bf16[128,512]{1,0:T(8,128)(2,1)S(1)}, u32[]{:S(2)}, u32[]{:S(2)}) collective-permute-start(bf16[128,512]{1,0:T(8,128)(2,1)S(1)} %bitcast_convert_fusion), channel_id=1, source_target_pairs={{0,26},{1,27},{2,24},{3,25},{8,2},{9,3},{10,0},{11,1},{16,10},{17,... | collective-permute-start | bytes 393224 | tf_op jit(solution)/shard_map/ppermute | solution.py:36
  8.8 11.2 %collective-permute-start.9 = (bf16[128,512]{1,0:T(8,128)(2,1)S(1)}, bf16[128,512]{1,0:T(8,128)(2,1)S(1)}, u32[]{:S(2)}, u32[]{:S(2)}) collective-permute-start(bf16[128,512]{1,0:T(8,128)(2,1)S(1)} %bitcast_convert_fusion), channel_id=1, source_target_pairs={{0,25},{1,26},{2,27},{3,24},{8,1},{9,2},{10,3},{11,0},{16,9},{17,1... | collective-permute-start | bytes 393224 | tf_op jit(solution)/shard_map/ppermute | solution.py:36
  10.6 10.2 %collective-permute-start.8 = (bf16[128,512]{1,0:T(8,128)(2,1)S(1)}, bf16[128,512]{1,0:T(8,128)(2,1)S(1)}, u32[]{:S(2)}, u32[]{:S(2)}) collective-permute-start(bf16[128,512]{1,0:T(8,128)(2,1)S(1)} %bitcast_convert_fusion), channel_id=1, source_target_pairs={{0,24},{1,25},{2,26},{3,27},{8,0},{9,1},{10,2},{11,3},{16,8},{17,9... | collective-permute-start | bytes 393224 | tf_op jit(solution)/shard_map/ppermute | solution.py:36
  54.7 15.5 %collective-permute-start.13 = (bf16[128,512]{1,0:T(8,128)(2,1)S(1)}, bf16[128,512]{1,0:T(8,128)(2,1)S(1)}, u32[]{:S(2)}, u32[]{:S(2)}) collective-permute-start(bf16[128,512]{1,0:T(8,128)(2,1)S(1)} %get-tuple-element.31), channel_id=1, source_target_pairs={{0,1},{1,2},{2,3},{3,0},{4,5},{5,6},{6,7},{7,4},{8,9},{9,10},{10,1... | collective-permute-start | bytes 393224 | tf_op jit(solution)/shard_map/ppermute | solution.py:22
  54.7 16.6 %collective-permute-start.14 = (bf16[128,512]{1,0:T(8,128)(2,1)S(1)}, bf16[128,512]{1,0:T(8,128)(2,1)S(1)}, u32[]{:S(2)}, u32[]{:S(2)}) collective-permute-start(bf16[128,512]{1,0:T(8,128)(2,1)S(1)} %get-tuple-element.32), channel_id=1, source_target_pairs={{0,2},{1,3},{2,0},{3,1},{4,6},{5,7},{6,4},{7,5},{8,10},{9,11},{10,... | collective-permute-start | bytes 393224 | tf_op jit(solution)/shard_map/ppermute | solution.py:22
  57.8 14.2 %collective-permute-start.15 = (bf16[128,512]{1,0:T(8,128)(2,1)S(1)}, bf16[128,512]{1,0:T(8,128)(2,1)S(1)}, u32[]{:S(2)}, u32[]{:S(2)}) collective-permute-start(bf16[128,512]{1,0:T(8,128)(2,1)S(1)} %get-tuple-element.33), channel_id=1, source_target_pairs={{0,3},{1,0},{2,1},{3,2},{4,7},{5,4},{6,5},{7,6},{8,11},{9,8},{10,9... | collective-permute-start | bytes 393224 | tf_op jit(solution)/shard_map/ppermute | solution.py:22
  59.4 10.8 %collective-permute-start.6 = (f32[4,128]{1,0:T(4,128)S(1)}, f32[4,128]{1,0:T(4,128)S(1)}, u32[]{:S(2)}, u32[]{:S(2)}) collective-permute-start(f32[4,128]{1,0:T(4,128)S(1)} %multiply_reduce_fusion), channel_id=1, source_target_pairs={{0,6},{1,7},{2,4},{3,5},{4,2},{5,3},{6,0},{7,1},{8,14},{9,15},{10,... | collective-permute-start | bytes 6152 | tf_op jit(solution)/shard_map/ppermute | solution.py:51
  71.3 8.4 %collective-permute-start.2 = (f32[4,128]{1,0:T(4,128)S(1)}, f32[4,128]{1,0:T(4,128)S(1)}, u32[]{:S(2)}, u32[]{:S(2)}) collective-permute-start(f32[4,128]{1,0:T(4,128)S(1)} %multiply_reduce_fusion), channel_id=1, source_target_pairs={{0,2},{1,3},{2,0},{3,1},{4,6},{5,7},{6,4},{7,5},{8,10},{9,11},{10,... | collective-permute-start | bytes 6152 | tf_op jit(solution)/shard_map/ppermute | solution.py:51
  73.4 16.5 %collective-permute-start = (f32[128,512]{1,0:T(8,128)S(1)}, f32[128,512]{1,0:T(8,128)S(1)}, u32[]{:S(2)}, u32[]{:S(2)}) collective-permute-start(f32[128,512]{1,0:T(8,128)S(1)} %bitcast.158), channel_id=1, source_target_pairs={{0,24},{8,0},{16,8},{24,16},{1,25},{9,1},{17,9},{25,17},{2,26},{10... | collective-permute-start | bytes 786440 | tf_op jit(solution)/shard_map/ppermute | solution.py:22
  91.8 12.5 %collective-permute-start.26 = (bf16[128,512]{1,0:T(8,128)(2,1)S(1)}, bf16[128,512]{1,0:T(8,128)(2,1)S(1)}, u32[]{:S(2)}, u32[]{:S(2)}) collective-permute-start(bf16[128,512]{1,0:T(8,128)(2,1)S(1)} %get-tuple-element.80), channel_id=1, source_target_pairs={{0,26},{1,27},{2,24},{3,25},{8,2},{9,3},{10,0},{11,1},{16,10},{17,... | collective-permute-start | bytes 393224 | tf_op jit(solution)/shard_map/ppermute | solution.py:36
  93.3 11.1 %collective-permute-start.25 = (bf16[128,512]{1,0:T(8,128)(2,1)S(1)}, bf16[128,512]{1,0:T(8,128)(2,1)S(1)}, u32[]{:S(2)}, u32[]{:S(2)}) collective-permute-start(bf16[128,512]{1,0:T(8,128)(2,1)S(1)} %get-tuple-element.80), channel_id=1, source_target_pairs={{0,25},{1,26},{2,27},{3,24},{8,1},{9,2},{10,3},{11,0},{16,9},{17,1... | collective-permute-start | bytes 393224 | tf_op jit(solution)/shard_map/ppermute | solution.py:36
  95.5 9.5 %collective-permute-start.24 = (bf16[128,512]{1,0:T(8,128)(2,1)S(1)}, bf16[128,512]{1,0:T(8,128)(2,1)S(1)}, u32[]{:S(2)}, u32[]{:S(2)}) collective-permute-start(bf16[128,512]{1,0:T(8,128)(2,1)S(1)} %get-tuple-element.80), channel_id=1, source_target_pairs={{0,24},{1,25},{2,26},{3,27},{8,0},{9,1},{10,2},{11,3},{16,8},{17,9... | collective-permute-start | bytes 393224 | tf_op jit(solution)/shard_map/ppermute | solution.py:36
  138.7 8.3 %collective-permute-start.29 = (bf16[128,512]{1,0:T(8,128)(2,1)S(1)}, bf16[128,512]{1,0:T(8,128)(2,1)S(1)}, u32[]{:S(2)}, u32[]{:S(2)}) collective-permute-start(bf16[128,512]{1,0:T(8,128)(2,1)S(1)} %get-tuple-element.35), channel_id=1, source_target_pairs={{0,1},{1,2},{2,3},{3,0},{4,5},{5,6},{6,7},{7,4},{8,9},{9,10},{10,1... | collective-permute-start | bytes 393224 | tf_op jit(solution)/shard_map/ppermute | solution.py:22
  139.4 12.4 %collective-permute-start.30 = (bf16[128,512]{1,0:T(8,128)(2,1)S(1)}, bf16[128,512]{1,0:T(8,128)(2,1)S(1)}, u32[]{:S(2)}, u32[]{:S(2)}) collective-permute-start(bf16[128,512]{1,0:T(8,128)(2,1)S(1)} %get-tuple-element.36), channel_id=1, source_target_pairs={{0,2},{1,3},{2,0},{3,1},{4,6},{5,7},{6,4},{7,5},{8,10},{9,11},{10,... | collective-permute-start | bytes 393224 | tf_op jit(solution)/shard_map/ppermute | solution.py:22
  142.1 9.7 %collective-permute-start.31 = (bf16[128,512]{1,0:T(8,128)(2,1)S(1)}, bf16[128,512]{1,0:T(8,128)(2,1)S(1)}, u32[]{:S(2)}, u32[]{:S(2)}) collective-permute-start(bf16[128,512]{1,0:T(8,128)(2,1)S(1)} %get-tuple-element.37), channel_id=1, source_target_pairs={{0,3},{1,0},{2,1},{3,2},{4,7},{5,4},{6,5},{7,6},{8,11},{9,8},{10,9... | collective-permute-start | bytes 393224 | tf_op jit(solution)/shard_map/ppermute | solution.py:22
  142.7 25.2 %collective-permute-start.23 = (f32[128,512]{1,0:T(8,128)}, f32[128,512]{1,0:T(8,128)}, u32[]{:S(2)}, u32[]{:S(2)}) collective-permute-start(f32[128,512]{1,0:T(8,128)} %get-tuple-element.81), channel_id=1, source_target_pairs={{0,24},{8,0},{16,8},{24,16},{1,25},{9,1},{17,9},{25,17},{2,26},{10... | collective-permute-start | bytes 786440 | tf_op jit(solution)/shard_map/ppermute | solution.py:22
  171.8 11.3 %collective-permute-start.42 = (bf16[128,512]{1,0:T(8,128)(2,1)S(1)}, bf16[128,512]{1,0:T(8,128)(2,1)S(1)}, u32[]{:S(2)}, u32[]{:S(2)}) collective-permute-start(bf16[128,512]{1,0:T(8,128)(2,1)S(1)} %get-tuple-element.76), channel_id=1, source_target_pairs={{0,26},{1,27},{2,24},{3,25},{8,2},{9,3},{10,0},{11,1},{16,10},{17,... | collective-permute-start | bytes 393224 | tf_op jit(solution)/shard_map/ppermute | solution.py:36
  172.4 10.8 %collective-permute-start.41 = (bf16[128,512]{1,0:T(8,128)(2,1)S(1)}, bf16[128,512]{1,0:T(8,128)(2,1)S(1)}, u32[]{:S(2)}, u32[]{:S(2)}) collective-permute-start(bf16[128,512]{1,0:T(8,128)(2,1)S(1)} %get-tuple-element.76), channel_id=1, source_target_pairs={{0,25},{1,26},{2,27},{3,24},{8,1},{9,2},{10,3},{11,0},{16,9},{17,1... | collective-permute-start | bytes 393224 | tf_op jit(solution)/shard_map/ppermute | solution.py:36
  175.4 8.7 %collective-permute-start.40 = (bf16[128,512]{1,0:T(8,128)(2,1)S(1)}, bf16[128,512]{1,0:T(8,128)(2,1)S(1)}, u32[]{:S(2)}, u32[]{:S(2)}) collective-permute-start(bf16[128,512]{1,0:T(8,128)(2,1)S(1)} %get-tuple-element.76), channel_id=1, source_target_pairs={{0,24},{1,25},{2,26},{3,27},{8,0},{9,1},{10,2},{11,3},{16,8},{17,9... | collective-permute-start | bytes 393224 | tf_op jit(solution)/shard_map/ppermute | solution.py:36
  220.9 8.3 %collective-permute-start.45 = (bf16[128,512]{1,0:T(8,128)(2,1)S(1)}, bf16[128,512]{1,0:T(8,128)(2,1)S(1)}, u32[]{:S(2)}, u32[]{:S(2)}) collective-permute-start(bf16[128,512]{1,0:T(8,128)(2,1)S(1)} %get-tuple-element.39), channel_id=1, source_target_pairs={{0,1},{1,2},{2,3},{3,0},{4,5},{5,6},{6,7},{7,4},{8,9},{9,10},{10,1... | collective-permute-start | bytes 393224 | tf_op jit(solution)/shard_map/ppermute | solution.py:22
  221.7 12.4 %collective-permute-start.46 = (bf16[128,512]{1,0:T(8,128)(2,1)S(1)}, bf16[128,512]{1,0:T(8,128)(2,1)S(1)}, u32[]{:S(2)}, u32[]{:S(2)}) collective-permute-start(bf16[128,512]{1,0:T(8,128)(2,1)S(1)} %get-tuple-element.40), channel_id=1, source_target_pairs={{0,2},{1,3},{2,0},{3,1},{4,6},{5,7},{6,4},{7,5},{8,10},{9,11},{10,... | collective-permute-start | bytes 393224 | tf_op jit(solution)/shard_map/ppermute | solution.py:22
  223.7 10.4 %collective-permute-start.47 = (bf16[128,512]{1,0:T(8,128)(2,1)S(1)}, bf16[128,512]{1,0:T(8,128)(2,1)S(1)}, u32[]{:S(2)}, u32[]{:S(2)}) collective-permute-start(bf16[128,512]{1,0:T(8,128)(2,1)S(1)} %get-tuple-element.41), channel_id=1, source_target_pairs={{0,3},{1,0},{2,1},{3,2},{4,7},{5,4},{6,5},{7,6},{8,11},{9,8},{10,9... | collective-permute-start | bytes 393224 | tf_op jit(solution)/shard_map/ppermute | solution.py:22
  224.9 25.7 %collective-permute-start.39 = (f32[128,512]{1,0:T(8,128)}, f32[128,512]{1,0:T(8,128)}, u32[]{:S(2)}, u32[]{:S(2)}) collective-permute-start(f32[128,512]{1,0:T(8,128)} %get-tuple-element.77), channel_id=1, source_target_pairs={{0,24},{8,0},{16,8},{24,16},{1,25},{9,1},{17,9},{25,17},{2,26},{10... | collective-permute-start | bytes 786440 | tf_op jit(solution)/shard_map/ppermute | solution.py:22
  253.9 11.4 %collective-permute-start.58 = (bf16[128,512]{1,0:T(8,128)(2,1)S(1)}, bf16[128,512]{1,0:T(8,128)(2,1)S(1)}, u32[]{:S(2)}, u32[]{:S(2)}) collective-permute-start(bf16[128,512]{1,0:T(8,128)(2,1)S(1)} %get-tuple-element.72), channel_id=1, source_target_pairs={{0,26},{1,27},{2,24},{3,25},{8,2},{9,3},{10,0},{11,1},{16,10},{17,... | collective-permute-start | bytes 393224 | tf_op jit(solution)/shard_map/ppermute | solution.py:36
  254.5 10.8 %collective-permute-start.57 = (bf16[128,512]{1,0:T(8,128)(2,1)S(1)}, bf16[128,512]{1,0:T(8,128)(2,1)S(1)}, u32[]{:S(2)}, u32[]{:S(2)}) collective-permute-start(bf16[128,512]{1,0:T(8,128)(2,1)S(1)} %get-tuple-element.72), channel_id=1, source_target_pairs={{0,25},{1,26},{2,27},{3,24},{8,1},{9,2},{10,3},{11,0},{16,9},{17,1... | collective-permute-start | bytes 393224 | tf_op jit(solution)/shard_map/ppermute | solution.py:36
  257.5 9.0 %collective-permute-start.56 = (bf16[128,512]{1,0:T(8,128)(2,1)S(1)}, bf16[128,512]{1,0:T(8,128)(2,1)S(1)}, u32[]{:S(2)}, u32[]{:S(2)}) collective-permute-start(bf16[128,512]{1,0:T(8,128)(2,1)S(1)} %get-tuple-element.72), channel_id=1, source_target_pairs={{0,24},{1,25},{2,26},{3,27},{8,0},{9,1},{10,2},{11,3},{16,8},{17,9... | collective-permute-start | bytes 393224 | tf_op jit(solution)/shard_map/ppermute | solution.py:36
  303.5 12.9 %collective-permute-start.62 = (bf16[128,512]{1,0:T(8,128)(2,1)S(1)}, bf16[128,512]{1,0:T(8,128)(2,1)S(1)}, u32[]{:S(2)}, u32[]{:S(2)}) collective-permute-start(bf16[128,512]{1,0:T(8,128)(2,1)S(1)} %get-tuple-element.44), channel_id=1, source_target_pairs={{0,2},{1,3},{2,0},{3,1},{4,6},{5,7},{6,4},{7,5},{8,10},{9,11},{10,... | collective-permute-start | bytes 393224 | tf_op jit(solution)/shard_map/ppermute | solution.py:22
  306.4 9.9 %collective-permute-start.63 = (bf16[128,512]{1,0:T(8,128)(2,1)S(1)}, bf16[128,512]{1,0:T(8,128)(2,1)S(1)}, u32[]{:S(2)}, u32[]{:S(2)}) collective-permute-start(bf16[128,512]{1,0:T(8,128)(2,1)S(1)} %get-tuple-element.45), channel_id=1, source_target_pairs={{0,3},{1,0},{2,1},{3,2},{4,7},{5,4},{6,5},{7,6},{8,11},{9,8},{10,9... | collective-permute-start | bytes 393224 | tf_op jit(solution)/shard_map/ppermute | solution.py:22
  307.6 24.7 %collective-permute-start.55 = (f32[128,512]{1,0:T(8,128)}, f32[128,512]{1,0:T(8,128)}, u32[]{:S(2)}, u32[]{:S(2)}) collective-permute-start(f32[128,512]{1,0:T(8,128)} %get-tuple-element.73), channel_id=1, source_target_pairs={{0,24},{8,0},{16,8},{24,16},{1,25},{9,1},{17,9},{25,17},{2,26},{10... | collective-permute-start | bytes 786440 | tf_op jit(solution)/shard_map/ppermute | solution.py:22
  336.2 11.6 %collective-permute-start.74 = (bf16[128,512]{1,0:T(8,128)(2,1)S(1)}, bf16[128,512]{1,0:T(8,128)(2,1)S(1)}, u32[]{:S(2)}, u32[]{:S(2)}) collective-permute-start(bf16[128,512]{1,0:T(8,128)(2,1)S(1)} %get-tuple-element.68), channel_id=1, source_target_pairs={{0,26},{1,27},{2,24},{3,25},{8,2},{9,3},{10,0},{11,1},{16,10},{17,... | collective-permute-start | bytes 393224 | tf_op jit(solution)/shard_map/ppermute | solution.py:36
  336.7 11.1 %collective-permute-start.73 = (bf16[128,512]{1,0:T(8,128)(2,1)S(1)}, bf16[128,512]{1,0:T(8,128)(2,1)S(1)}, u32[]{:S(2)}, u32[]{:S(2)}) collective-permute-start(bf16[128,512]{1,0:T(8,128)(2,1)S(1)} %get-tuple-element.68), channel_id=1, source_target_pairs={{0,25},{1,26},{2,27},{3,24},{8,1},{9,2},{10,3},{11,0},{16,9},{17,1... | collective-permute-start | bytes 393224 | tf_op jit(solution)/shard_map/ppermute | solution.py:36
  339.9 8.6 %collective-permute-start.72 = (bf16[128,512]{1,0:T(8,128)(2,1)S(1)}, bf16[128,512]{1,0:T(8,128)(2,1)S(1)}, u32[]{:S(2)}, u32[]{:S(2)}) collective-permute-start(bf16[128,512]{1,0:T(8,128)(2,1)S(1)} %get-tuple-element.68), channel_id=1, source_target_pairs={{0,24},{1,25},{2,26},{3,27},{8,0},{9,1},{10,2},{11,3},{16,8},{17,9... | collective-permute-start | bytes 393224 | tf_op jit(solution)/shard_map/ppermute | solution.py:36
  382.2 13.0 %collective-permute-start.78 = (bf16[128,512]{1,0:T(8,128)(2,1)S(1)}, bf16[128,512]{1,0:T(8,128)(2,1)S(1)}, u32[]{:S(2)}, u32[]{:S(2)}) collective-permute-start(bf16[128,512]{1,0:T(8,128)(2,1)S(1)} %get-tuple-element.48), channel_id=1, source_target_pairs={{0,2},{1,3},{2,0},{3,1},{4,6},{5,7},{6,4},{7,5},{8,10},{9,11},{10,... | collective-permute-start | bytes 393224 | tf_op jit(solution)/shard_map/ppermute | solution.py:22
  385.2 10.0 %collective-permute-start.79 = (bf16[128,512]{1,0:T(8,128)(2,1)S(1)}, bf16[128,512]{1,0:T(8,128)(2,1)S(1)}, u32[]{:S(2)}, u32[]{:S(2)}) collective-permute-start(bf16[128,512]{1,0:T(8,128)(2,1)S(1)} %get-tuple-element.49), channel_id=1, source_target_pairs={{0,3},{1,0},{2,1},{3,2},{4,7},{5,4},{6,5},{7,6},{8,11},{9,8},{10,9... | collective-permute-start | bytes 393224 | tf_op jit(solution)/shard_map/ppermute | solution.py:22
  386.2 25.2 %collective-permute-start.71 = (f32[128,512]{1,0:T(8,128)}, f32[128,512]{1,0:T(8,128)}, u32[]{:S(2)}, u32[]{:S(2)}) collective-permute-start(f32[128,512]{1,0:T(8,128)} %get-tuple-element.69), channel_id=1, source_target_pairs={{0,24},{8,0},{16,8},{24,16},{1,25},{9,1},{17,9},{25,17},{2,26},{10... | collective-permute-start | bytes 786440 | tf_op jit(solution)/shard_map/ppermute | solution.py:22
  415.3 11.5 %collective-permute-start.90 = (bf16[128,512]{1,0:T(8,128)(2,1)S(1)}, bf16[128,512]{1,0:T(8,128)(2,1)S(1)}, u32[]{:S(2)}, u32[]{:S(2)}) collective-permute-start(bf16[128,512]{1,0:T(8,128)(2,1)S(1)} %get-tuple-element.64), channel_id=1, source_target_pairs={{0,26},{1,27},{2,24},{3,25},{8,2},{9,3},{10,0},{11,1},{16,10},{17,... | collective-permute-start | bytes 393224 | tf_op jit(solution)/shard_map/ppermute | solution.py:36
  415.9 10.9 %collective-permute-start.89 = (bf16[128,512]{1,0:T(8,128)(2,1)S(1)}, bf16[128,512]{1,0:T(8,128)(2,1)S(1)}, u32[]{:S(2)}, u32[]{:S(2)}) collective-permute-start(bf16[128,512]{1,0:T(8,128)(2,1)S(1)} %get-tuple-element.64), channel_id=1, source_target_pairs={{0,25},{1,26},{2,27},{3,24},{8,1},{9,2},{10,3},{11,0},{16,9},{17,1... | collective-permute-start | bytes 393224 | tf_op jit(solution)/shard_map/ppermute | solution.py:36
  419.2 8.3 %collective-permute-start.88 = (bf16[128,512]{1,0:T(8,128)(2,1)S(1)}, bf16[128,512]{1,0:T(8,128)(2,1)S(1)}, u32[]{:S(2)}, u32[]{:S(2)}) collective-permute-start(bf16[128,512]{1,0:T(8,128)(2,1)S(1)} %get-tuple-element.64), channel_id=1, source_target_pairs={{0,24},{1,25},{2,26},{3,27},{8,0},{9,1},{10,2},{11,3},{16,8},{17,9... | collective-permute-start | bytes 393224 | tf_op jit(solution)/shard_map/ppermute | solution.py:36
  464.6 12.9 %collective-permute-start.94 = (bf16[128,512]{1,0:T(8,128)(2,1)S(1)}, bf16[128,512]{1,0:T(8,128)(2,1)S(1)}, u32[]{:S(2)}, u32[]{:S(2)}) collective-permute-start(bf16[128,512]{1,0:T(8,128)(2,1)S(1)} %get-tuple-element.52), channel_id=1, source_target_pairs={{0,2},{1,3},{2,0},{3,1},{4,6},{5,7},{6,4},{7,5},{8,10},{9,11},{10,... | collective-permute-start | bytes 393224 | tf_op jit(solution)/shard_map/ppermute | solution.py:22
  467.4 10.0 %collective-permute-start.95 = (bf16[128,512]{1,0:T(8,128)(2,1)S(1)}, bf16[128,512]{1,0:T(8,128)(2,1)S(1)}, u32[]{:S(2)}, u32[]{:S(2)}) collective-permute-start(bf16[128,512]{1,0:T(8,128)(2,1)S(1)} %get-tuple-element.53), channel_id=1, source_target_pairs={{0,3},{1,0},{2,1},{3,2},{4,7},{5,4},{6,5},{7,6},{8,11},{9,8},{10,9... | collective-permute-start | bytes 393224 | tf_op jit(solution)/shard_map/ppermute | solution.py:22
  468.6 24.7 %collective-permute-start.87 = (f32[128,512]{1,0:T(8,128)}, f32[128,512]{1,0:T(8,128)}, u32[]{:S(2)}, u32[]{:S(2)}) collective-permute-start(f32[128,512]{1,0:T(8,128)} %get-tuple-element.65), channel_id=1, source_target_pairs={{0,24},{8,0},{16,8},{24,16},{1,25},{9,1},{17,9},{25,17},{2,26},{10... | collective-permute-start | bytes 786440 | tf_op jit(solution)/shard_map/ppermute | solution.py:22
  497.2 11.5 %collective-permute-start.106 = (bf16[128,512]{1,0:T(8,128)(2,1)S(1)}, bf16[128,512]{1,0:T(8,128)(2,1)S(1)}, u32[]{:S(2)}, u32[]{:S(2)}) collective-permute-start(bf16[128,512]{1,0:T(8,128)(2,1)S(1)} %get-tuple-element.60), channel_id=1, source_target_pairs={{0,26},{1,27},{2,24},{3,25},{8,2},{9,3},{10,0},{11,1},{16,10},{17,... | collective-permute-start | bytes 393224 | tf_op jit(solution)/shard_map/ppermute | solution.py:36
  497.7 11.0 %collective-permute-start.105 = (bf16[128,512]{1,0:T(8,128)(2,1)S(1)}, bf16[128,512]{1,0:T(8,128)(2,1)S(1)}, u32[]{:S(2)}, u32[]{:S(2)}) collective-permute-start(bf16[128,512]{1,0:T(8,128)(2,1)S(1)} %get-tuple-element.60), channel_id=1, source_target_pairs={{0,25},{1,26},{2,27},{3,24},{8,1},{9,2},{10,3},{11,0},{16,9},{17,1... | collective-permute-start | bytes 393224 | tf_op jit(solution)/shard_map/ppermute | solution.py:36
  501.0 8.5 %collective-permute-start.104 = (bf16[128,512]{1,0:T(8,128)(2,1)S(1)}, bf16[128,512]{1,0:T(8,128)(2,1)S(1)}, u32[]{:S(2)}, u32[]{:S(2)}) collective-permute-start(bf16[128,512]{1,0:T(8,128)(2,1)S(1)} %get-tuple-element.60), channel_id=1, source_target_pairs={{0,24},{1,25},{2,26},{3,27},{8,0},{9,1},{10,2},{11,3},{16,8},{17,9... | collective-permute-start | bytes 393224 | tf_op jit(solution)/shard_map/ppermute | solution.py:36
  546.4 12.9 %collective-permute-start.110 = (bf16[128,512]{1,0:T(8,128)(2,1)S(1)}, bf16[128,512]{1,0:T(8,128)(2,1)S(1)}, u32[]{:S(2)}, u32[]{:S(2)}) collective-permute-start(bf16[128,512]{1,0:T(8,128)(2,1)S(1)} %get-tuple-element.56), channel_id=1, source_target_pairs={{0,2},{1,3},{2,0},{3,1},{4,6},{5,7},{6,4},{7,5},{8,10},{9,11},{10,... | collective-permute-start | bytes 393224 | tf_op jit(solution)/shard_map/ppermute | solution.py:22
  549.4 10.0 %collective-permute-start.111 = (bf16[128,512]{1,0:T(8,128)(2,1)S(1)}, bf16[128,512]{1,0:T(8,128)(2,1)S(1)}, u32[]{:S(2)}, u32[]{:S(2)}) collective-permute-start(bf16[128,512]{1,0:T(8,128)(2,1)S(1)} %get-tuple-element.57), channel_id=1, source_target_pairs={{0,3},{1,0},{2,1},{3,2},{4,7},{5,4},{6,5},{7,6},{8,11},{9,8},{10,9... | collective-permute-start | bytes 393224 | tf_op jit(solution)/shard_map/ppermute | solution.py:22
  550.6 24.8 %collective-permute-start.103 = (f32[128,512]{1,0:T(8,128)}, f32[128,512]{1,0:T(8,128)}, u32[]{:S(2)}, u32[]{:S(2)}) collective-permute-start(f32[128,512]{1,0:T(8,128)} %get-tuple-element.61), channel_id=1, source_target_pairs={{0,24},{8,0},{16,8},{24,16},{1,25},{9,1},{17,9},{25,17},{2,26},{10... | collective-permute-start | bytes 786440 | tf_op jit(solution)/shard_map/ppermute | solution.py:22
  (116 other events, 1248.2 us)

commit v2 on v0

--- a/solution.py
+++ b/solution.py
@@ -1,12 +1,25 @@
+import functools
+
 import jax
 import jax.numpy as jnp
 from jax import lax
+from jax.experimental import pallas as pl
+from jax.experimental.pallas import tpu as pltpu
 from jax.sharding import PartitionSpec as P
 
+
 D = 4096
 
 
 eps = 1e-05
+
+NT = (((1,), (1,)), ((), ()))
+VMEM = pl.BlockSpec(memory_space=pltpu.VMEM)
+HBM = pl.BlockSpec(memory_space=pltpu.HBM)
+
+
+def in_hbm(x):
+    return pltpu.with_memory_space_constraint(x, pltpu.HBM)
 
 
 def shifted(x, axis, by):
@@ -18,7 +31,271 @@
     return shifted(carry, "section", -1)
 
 
+def swapped(x, axis, by):
+    return lax.ppermute(x, axis, [(i, i ^ by) for i in range(lax.axis_size(axis))])
+
+
+def spread(x, by):
+    sections, cols = lax.axis_size("section"), lax.axis_size("col")
+    pairs = [
+        (s * cols + c, ((s - 1) % sections) * cols + (c ^ by))
+        for s in range(sections)
+        for c in range(cols)
+    ]
+    return lax.ppermute(x, ("section", "col"), pairs)
+
+
+def group_sum(x):
+    for axis in ("row", "col"):
+        by = 1
+        while by < lax.axis_size(axis):
+            x = x + swapped(x, axis, by)
+            by *= 2
+    return x
+
+
+def micro_of(step, sections):
+    return lax.rem(lax.axis_index("section") + step + 1, sections)
+
+
+def down_kernel(step, side, tile, half, *refs):
+    pieces, rest = refs[:half], refs[half:]
+    before, rest = (rest[0], rest[1:]) if side else (None, rest)
+    w_ref, h_ref, o_ref = rest[:3]
+    hout, rest = (None, rest[3:]) if side else (rest[3], rest[4:])
+    buf, gy, hsem, sem = rest
+    tiles = w_ref.shape[0] // tile
+    depth, _, span = buf.shape
+    chunk = span // half
+    col = lax.axis_index("col")
+    group = lax.bitwise_xor(lax.div(col, half), side)
+    columns = pl.ds(pl.multiple_of(group * span, span), span)
+
+    def fetch(i):
+        s = lax.rem(i, depth)
+        first = pl.multiple_of(i * tile, tile)
+        return pltpu.make_async_copy(w_ref.at[pl.ds(first, tile), columns], buf.at[s], sem.at[s])
+
+    for i in range(depth - 1):
+        fetch(i).start()
+    for j in range(half):
+        source = lax.bitwise_xor(lax.rem(col, half), j)
+        gy[:, pl.ds(pl.multiple_of(source * chunk, chunk), chunk)] = pieces[j][...]
+    if not side:
+        hcopy = pltpu.make_async_copy(h_ref.at[0, micro_of(step, h_ref.shape[1])], hout, hsem.at[0])
+
+    @pl.loop(0, tiles)
+    def _(i):
+        fetch(i).wait()
+
+        @pl.when(i + depth - 1 < tiles)
+        def _():
+            fetch(i + depth - 1).start()
+
+        if not side:
+
+            @pl.when(i == tiles - depth)
+            def _():
+                hcopy.start()
+
+        at = pl.ds(pl.multiple_of(i * tile, tile), tile)
+        part = lax.dot_general(
+            gy[...], buf[lax.rem(i, depth)], NT, preferred_element_type=jnp.float32
+        )
+        if side:
+            part += before[:, at]
+        o_ref[:, at] = part.astype(o_ref.dtype)
+
+    if not side:
+        hcopy.wait()
+
+
+def down(step, side, pieces, before, wd, hidden):
+    half = len(pieces)
+    rows, chunk = pieces[0].shape
+    width = wd.shape[0]
+    span = half * chunk
+    tile, depth = 512, 3
+    out = [jax.ShapeDtypeStruct((rows, width), jnp.bfloat16 if side else jnp.float32)]
+    if not side:
+        out.append(jax.ShapeDtypeStruct((2, rows, width), hidden.dtype))
+    return pl.pallas_call(
+        functools.partial(down_kernel, step, side, tile, half),
+        in_specs=[VMEM] * (half + len(before)) + [HBM, HBM],
+        out_specs=[VMEM] * len(out),
+        out_shape=out,
+        scratch_shapes=[
+            pltpu.VMEM((depth, tile, span), wd.dtype),
+            pltpu.VMEM((rows, span), jnp.bfloat16),
+            pltpu.SemaphoreType.DMA((1,)),
+            pltpu.SemaphoreType.DMA((depth,)),
+        ],
+        compiler_params=pltpu.CompilerParams(vmem_limit_bytes=16 << 20),
+        cost_estimate=pl.CostEstimate(
+            flops=8 * rows * width * span, bytes_accessed=2 * width * span, transcendentals=0
+        ),
+    )(*pieces, *before, in_hbm(wd), in_hbm(hidden))
+
+
+def up_tiles(step, dests, tile, gate, upper, wg_ref, wu_ref, x_ref, o_ref, i_ref, bufs, between):
+    gbuf, ubuf, xbuf, sem = bufs
+    depth = gbuf.shape[0]
+    chunk = o_ref.shape[2]
+    parts = chunk // tile
+    tiles = len(dests) * parts
+    col = lax.axis_index("col")
+    micro = micro_of(step, x_ref.shape[0])
+
+    def fetch(i):
+        k = lax.div(i, parts)
+        j = dests[0]
+        for at, other in enumerate(dests[1:]):
+            j = jnp.where(k == at + 1, other, j)
+        dest = lax.bitwise_xor(col, j)
+        first = pl.multiple_of(dest * chunk + lax.rem(i, parts) * tile, tile)
+        s = lax.rem(i, depth)
+        return (
+            pltpu.make_async_copy(wg_ref.at[pl.ds(first, tile)], gbuf.at[s], sem.at[0, s]),
+            pltpu.make_async_copy(wu_ref.at[pl.ds(first, tile)], ubuf.at[s], sem.at[1, s]),
+            pltpu.make_async_copy(x_ref.at[micro, :, pl.ds(first, tile)], xbuf.at[s], sem.at[2, s]),
+        )
+
+    def start(i):
+        for c in fetch(jnp.int32(i)):
+            c.start()
+
+    for i in range(min(depth - 1, tiles)):
+        start(i)
+    between()
+    i_ref[...] = jnp.zeros_like(i_ref)
+
+    @pl.loop(0, tiles)
+    def _(i):
+        for c in fetch(i):
+            c.wait()
+
+        @pl.when(i + depth - 1 < tiles)
+        def _():
+            start(i + depth - 1)
+
+        s = lax.rem(i, depth)
+        acc = lax.dot_general(gate[...], gbuf[s], NT, preferred_element_type=jnp.float32)
+        acc += lax.dot_general(upper[...], ubuf[s], NT, preferred_element_type=jnp.float32)
+        at = pl.ds(pl.multiple_of(lax.rem(i, parts) * tile, tile), tile)
+        o_ref[lax.div(i, parts), :, at] = acc.astype(o_ref.dtype)
+        prod = acc * xbuf[s].astype(jnp.float32)
+        lanes = i_ref.shape[1]
+        total = i_ref[...]
+        for b in range(tile // lanes):
+            total += prod[:, b * lanes : (b + 1) * lanes]
+        i_ref[...] = total
+
+
+def far_kernel(step, dests, tile, ga, gb, h_ref, wg_ref, wu_ref, x_ref, o_ref, i_ref, gate, upper, *bufs):
+    def gradients():
+        block = 512
+
+        @pl.loop(0, gate.shape[1] // block)
+        def _(b):
+            at = pl.ds(pl.multiple_of(b * block, block), block)
+            g = ga[:, at].astype(jnp.float32) + gb[:, at].astype(jnp.float32)
+            hg = h_ref[0, :, at].astype(jnp.float32)
+            hu = h_ref[1, :, at].astype(jnp.float32)
+            sig = jax.nn.sigmoid(hg)
+            gate[:, at] = (g * hu * sig * (1.0 + hg * (1.0 - sig))).astype(jnp.bfloat16)
+            upper[:, at] = (g * hg * sig).astype(jnp.bfloat16)
+
+    up_tiles(step, dests, tile, gate, upper, wg_ref, wu_ref, x_ref, o_ref, i_ref, bufs, gradients)
+
+
+def near_kernel(step, dests, tile, gate, upper, wg_ref, wu_ref, x_ref, o_ref, i_ref, *bufs):
+    up_tiles(step, dests, tile, gate, upper, wg_ref, wu_ref, x_ref, o_ref, i_ref, bufs, lambda: None)
+
+
+def up_call(kernel, step, dests, operands, wg, wu, inputs, extra):
+    feats, width = wg.shape
+    rows, chunk = inputs.shape[1], feats // lax.axis_size("col")
+    tile, depth = 256, 3
+    return pl.pallas_call(
+        functools.partial(kernel, step, dests, tile),
+        in_specs=[VMEM] * len(operands) + [HBM, HBM, HBM],
+        out_specs=[VMEM] * (2 + extra),
+        out_shape=[
+            jax.ShapeDtypeStruct((len(dests), rows, chunk), jnp.bfloat16),
+            jax.ShapeDtypeStruct((rows, 128), jnp.float32),
+        ]
+        + [jax.ShapeDtypeStruct((rows, width), jnp.bfloat16)] * extra,
+        scratch_shapes=[
+            pltpu.VMEM((depth, tile, width), wg.dtype),
+            pltpu.VMEM((depth, tile, width), wu.dtype),
+            pltpu.VMEM((depth, rows, tile), inputs.dtype),
+            pltpu.SemaphoreType.DMA((3, depth)),
+        ],
+        compiler_params=pltpu.CompilerParams(vmem_limit_bytes=24 << 20),
+        cost_estimate=pl.CostEstimate(
+            flops=16 * rows * width * chunk * len(dests),
+            bytes_accessed=4 * width * chunk * len(dests),
+            transcendentals=0,
+        ),
+    )(*operands, in_hbm(wg), in_hbm(wu), in_hbm(inputs))
+
+
 def shards(cotangent, incoming, upd_u, upd_v, saved_x, saved_h, norm_gain, w_gate, w_up, w_down):
+    sections, cols = lax.axis_size("section"), lax.axis_size("col")
+    section_idx = lax.axis_index("section")
+    inputs_all = saved_x[0].astype(jnp.float32)
+    gain = norm_gain[0]
+    wg, wu, wd = w_gate[0], w_up[0], w_down[0]
+    weighted = (gain * inputs_all).astype(jnp.bfloat16)
+    weighted = lax.all_gather(weighted, "col", axis=2, tiled=True)
+    sumsq_all = jnp.sum(inputs_all * inputs_all, axis=2)
+    rstd_all = None
+    half = cols // 2
+    far = tuple(range(cols - 1, half - 1, -1))
+    near = tuple(range(half - 1, -1, -1))
+
+    carry = cotangent[0]
+    for step in range(2 * sections - 1):
+        gy = carry.astype(jnp.bfloat16)
+        far_pieces = [spread(gy, j) for j in range(half, cols)]
+        near_pieces = [spread(gy, j) for j in range(half)]
+        carry = rotate(carry)
+        micro = (section_idx + step + 1) % sections
+        ga, hpair = down(step, 0, near_pieces, [], wd, saved_h)
+        (ga,) = down(step, 1, far_pieces, [ga], wd, saved_h)
+        gb = swapped(ga, "row", 1)
+        outs_far, inner_far, gate, upper = up_call(
+            far_kernel, step, far, (ga, gb, hpair), wg, wu, weighted, 2
+        )
+        normgrad = [swapped(outs_far[k], "col", j) for k, j in enumerate(far)]
+        outs_near, inner_near = up_call(near_kernel, step, near, (gate, upper), wg, wu, weighted, 0)
+        normgrad += [
+            swapped(outs_near[k], "col", j) if j else outs_near[k] for k, j in enumerate(near)
+        ]
+        inner = jnp.sum(inner_far + inner_near, axis=1)[None]
+        if step == 0:
+            sums = group_sum(jnp.concatenate([inner, sumsq_all], axis=0))
+            inner, rstd_all = sums[:1], lax.rsqrt(sums[1:] / D + eps)
+        else:
+            inner = group_sum(inner)
+        inner = inner[0][:, None] / D
+        normgrad = sum(p.astype(jnp.float32) for p in normgrad)
+        xf = lax.dynamic_index_in_dim(saved_x[0], micro, 0, keepdims=False).astype(jnp.float32)
+        rstd = lax.dynamic_index_in_dim(rstd_all, micro, 0, keepdims=False)[:, None]
+        updated = carry + rstd * (gain * normgrad) - xf * (rstd * rstd * rstd) * inner
+        active = jnp.logical_and(step >= micro, step - micro < sections)
+        carry = jnp.where(active, updated, carry)
+
+    pulled = rotate(carry)
+    resid = pulled + incoming[0] - cotangent[0]
+    local_dots = jnp.einsum("urd,rd->u", upd_v[0], resid, precision=lax.Precision.HIGHEST)
+    dots = group_sum(local_dots)
+    update = jnp.einsum("u,urd->rd", dots, upd_u[0], precision=lax.Precision.HIGHEST)
+    fresh = cotangent[0] + resid - update
+    return (fresh[None], resid[None])
+
+
+def plain_shards(cotangent, incoming, upd_u, upd_v, saved_x, saved_h, norm_gain, w_gate, w_up, w_down):
     sections = lax.axis_size("section")
     section_idx = lax.axis_index("section")
     inputs_all = saved_x[0].astype(jnp.float32)
@@ -36,9 +313,7 @@
         sumsq = lax.psum(jnp.sum(xf * xf, axis=1), ("row", "col"))
         gy = carry.astype(jnp.bfloat16)
         wide = lax.all_gather(gy, "col", axis=1, tiled=True)
-        ga_part = lax.dot_general(
-            wide, wd, (((1,), (1,)), ((), ())), preferred_element_type=jnp.float32
-        )
+        ga_part = lax.dot_general(wide, wd, NT, preferred_element_type=jnp.float32)
         ga = lax.psum_scatter(ga_part, "row", scatter_dimension=1, tiled=True)
         width = ga.shape[1]
         offset = lax.axis_index("row") * width
@@ -47,16 +322,10 @@
         sig = jax.nn.sigmoid(hg)
         part_gate = (ga * hu * sig * (1.0 + hg * (1.0 - sig))).astype(jnp.bfloat16)
         part_up = (ga * hg * sig).astype(jnp.bfloat16)
-        grad_gate, grad_up = (
-            lax.all_gather(part_gate, "row", axis=1, tiled=True),
-            lax.all_gather(part_up, "row", axis=1, tiled=True),
-        )
-        first = lax.dot_general(
-            wg, grad_gate, (((1,), (1,)), ((), ())), preferred_element_type=jnp.float32
-        )
-        second = lax.dot_general(
-            wu, grad_up, (((1,), (1,)), ((), ())), preferred_element_type=jnp.float32
-        )
+        grad_gate = lax.all_gather(part_gate, "row", axis=1, tiled=True)
+        grad_up = lax.all_gather(part_up, "row", axis=1, tiled=True)
+        first = lax.dot_general(wg, grad_gate, NT, preferred_element_type=jnp.float32)
+        second = lax.dot_general(wu, grad_up, NT, preferred_element_type=jnp.float32)
         normgrad = lax.psum_scatter(first + second, "col", scatter_dimension=0, tiled=True).T
         rstd = lax.rsqrt(sumsq / D + eps)[:, None]
         scaled = gain * normgrad
@@ -88,10 +357,21 @@
         P("section", "row", "col"),
         P("section", "col", "row"),
     )
-    return jax.shard_map(
-        shards,
-        mesh=mesh,
-        in_specs=placed,
-        out_specs=(P("section", None, ("row", "col")), P("section", None, ("row", "col"))),
-        check_vma=False,
-    )
+
+    sizes = dict(mesh.shape)
+    rows, cols = sizes["row"], sizes["col"]
+
+    def run(*args):
+        chunk, width = args[0].shape[2] // (rows * cols), args[7].shape[2] // cols
+        paired = rows == 2 and cols > 1 and cols & (cols - 1) == 0
+        tuned = paired and chunk % 256 == 0 and width % 512 == 0
+        step = jax.shard_map(
+            shards if tuned else plain_shards,
+            mesh=mesh,
+            in_specs=placed,
+            out_specs=(P("section", None, ("row", "col")), P("section", None, ("row", "col"))),
+            check_vma=False,
+        )
+        return step(*args)
+
+    return run

time: 882 us -> 489 us (0.55)
  blocking collectives: 256 us -> 0 us
  matrix products: 228 us -> 2.84 us
  Pallas kernels: 0 us -> 188 us
  waiting for transfers between devices: 319 us -> 157 us
  starting transfers between devices: 21 us -> 109 us
  other arithmetic: 39.4 us -> 11.6 us
    reduce_scatter x14 -> x0, waiting for transfers between devices: 264 us -> none  [the longest x7 201 us: layer_step(): lax.psum_scatter(first + second, 'col', scatter_dimension=0, tiled=True)]
    dot_general x21 -> x0, matrix products: 225 us -> none  [the longest x7 79.4 us: layer_step(): lax.dot_general(wide, wd, (((1,), (1,)), ((), ())), preferred_element_typ...]
    pallas_call x0 -> x28, Pallas kernels: none -> 188 us  [the longest x14 105 us: up_call(): pl.pallas_call(functools.partial(kernel, step, dests, tile), in_specs=[VM...]
    all_gather x21 -> x0, blocking collectives: 147 us -> none  [the longest x7 112 us: layer_step(): wide = lax.all_gather(gy, 'col', axis=1, tiled=True)]
    ppermute x0 -> x80, waiting for transfers between devices: none -> 141 us  [the longest x52 94.1 us: swapped(): lax.ppermute(x, axis, [(i, i ^ by) for i in range(lax.axis_size(axis))])]
    psum x8 -> x0, blocking collectives: 110 us -> none  [the longest x7 95.9 us: layer_step(): inner = lax.psum(jnp.sum(scaled * xf, axis=1), ('row', 'col'))[:, None] / D]
    ppermute x0 -> x80, starting transfers between devices: none -> 96.4 us  [the longest x28 49.8 us: spread(): return lax.ppermute(x, ('section', 'col'), pairs)]
    ppermute x8, waiting for transfers between devices: 54.8 us -> 6.3 us  [shifted(): lax.ppermute(x, axis, [(i, (i + by) % devices) for i in range(devices)])]
  transfers between devices with their start and end apart: 22 -> 89, of which waited for: 22 -> 38; matrix products, arithmetic and copies ran while one was open for 0% -> 0% of each run, Pallas kernels for 0% -> 13%
where the time goes in v2:
time: 489 us; the launch traced here: 487 us
  Pallas kernels  188 us (38%)
  waiting for transfers between devices  157 us (32%)
  starting transfers between devices  109 us (22%)
  between operations  15 us (3%)
  other arithmetic  11.6 us (2%)
    pallas_call x14, Pallas kernels, up_call(): pl.pallas_call(functools.partial(kernel, step, dests, tile), in_specs=[VM...  105 us
    ppermute x52, waiting for transfers between devices, swapped(): lax.ppermute(x, axis, [(i, i ^ by) for i in range(lax.axis_size(axis))])  94.1 us
    pallas_call x14, Pallas kernels, down(): pl.pallas_call(functools.partial(down_kernel, step, side, tile, half), in...  83.4 us
    ppermute x28, starting transfers between devices, spread(): return lax.ppermute(x, ('section', 'col'), pairs)  49.8 us
    ppermute x28, waiting for transfers between devices, spread(): return lax.ppermute(x, ('section', 'col'), pairs)  46.9 us
    ppermute x52, starting transfers between devices, swapped(): lax.ppermute(x, axis, [(i, i ^ by) for i in range(lax.axis_size(axis))])  46.6 us
    ppermute x8, starting transfers between devices, shifted(): lax.ppermute(x, axis, [(i, (i + by) % devices) for i in range(devices)])  12.8 us
    all_gather x1, waiting for transfers between devices, shards(): weighted = lax.all_gather(weighted, 'col', axis=2, tiled=True)  9.95 us
  transfers between devices with their start and end apart: 89, of which 38 were waited for; matrix products, arithmetic and copies ran while one was open for 0% of the time, Pallas kernels for 13%

profile of v2, /device:TPU:0, one launch (start us, length us, event | category | flops | bytes accessed | tf_op | source)
XLA Modules:
  0.0 486.9 jit_solution(1397136986459685325)
XLA Ops:
  10.4 5.0 %collective-permute-start.4 = (bf16[128,512]{1,0:T(8,128)(2,1)S(1)}, bf16[128,512]{1,0:T(8,128)(2,1)S(1)}, u32[]{:S(2)}, u32[]{:S(2)}) collective-permute-start(bf16[128,512]{1,0:T(8,128)(2,1)S(1)} %bitcast_convert_fusion), channel_id=1, source_target_pairs={{0,25},{1,24},{2,27},{3,26},{8,1},{9,0},{10,3},{11,2},{16,9},{17,8... | collective-permute-start | bytes 393224 | tf_op jit(solution)/shard_map/ppermute | solution.py:45
  15.9 3.3 collective-permute-start.2
  19.3 3.8 collective-permute-done.3.refs_0_
  23.2 6.2 %shard_map.113 = (f32[128,3584]{1,0:T(8,128)S(1)}, bf16[2,128,3584]{2,1,0:T(8,128)(2,1)S(1)}) custom-call(bf16[128,512]{1,0:T(8,128)(2,1)S(1)} %collective-permute-done.3.refs_0_, bf16[128,512]{1,0:T(8,128)(2,1)S(1)} %collective-permute-done.4.refs_1_, bf16[3584,2048]{1,0:T(8,128)(2,1)} %bitcast.179, bf16[1,4,2,128,3584]{4,3,2,1,0:T(8,128)(2,1)} %refs_4_.13), custom_call_target="tpu_custom_call" | custom-call | flops 3758096384 | bytes 7340032 | tf_op jit(solution)/shard_map/pallas_call | solution.py:122
  30.7 15.5 %collective-permute-done.1.refs_0_ = bf16[128,512]{1,0:T(8,128)(2,1)S(1)} collective-permute-done((bf16[128,512]{1,0:T(8,128)(2,1)S(1)}, bf16[128,512]{1,0:T(8,128)(2,1)S(1)}, u32[]{:S(2)}, u32[]{:S(2)}) %collective-permute-start.1) | collective-permute-done | bytes 131104 | tf_op jit(solution)/shard_map/ppermute | solution.py:45
  46.2 5.7 %shard_map.114.ga = bf16[128,3584]{1,0:T(8,128)(2,1)S(1)} custom-call(bf16[128,512]{1,0:T(8,128)(2,1)S(1)} %collective-permute-done.1.refs_0_, bf16[128,512]{1,0:T(8,128)(2,1)S(1)} %collective-permute-done.2.refs_1_, f32[128,3584]{1,0:T(8,128)S(1)} %get-tuple-element.58.refs_2_, bf16[3584,2048]{1,0:T(8,128)(2,1)} %bitcast.180, ...), custom_call_target="tpu_custom_call" | custom-call | flops 3758096384 | bytes 7340032 | tf_op jit(solution)/shard_map/pallas_call | solution.py:122
  54.6 9.9 %all-gather.2.cloned.1.call-done.x_ref = bf16[4,128,2048]{2,1,0:T(8,128)(2,1)} async-done(((bf16[4,128,512]{2,1,0:T(8,128)(2,1)}), bf16[4,128,2048]{2,1,0:T(8,128)(2,1)}) %all-gather.2.cloned.1.call-update) | async-done | bytes 2097168 | tf_op jit(solution)/shard_map/all_gather | solution.py:250
  66.1 8.6 %shard_map.115 = (bf16[2,128,512]{2,1,0:T(8,128)(2,1)S(1)}, f32[128,128]{1,0:T(8,128)S(1)}, bf16[128,3584]{1,0:T(8,128)(2,1)S(1)}, bf16[128,3584]{1,0:T(8,128)(2,1)S(1)}) custom-call(bf16[128,3584]{1,0:T(8,128)(2,1)S(1)} %shard_map.114.ga, bf16[128,3584]{1,0:T(8,128)(2,1)} %collective-permute-done.5.gb, bf16[2,128,3584]{2,1,0:T(8,128)(2,1)S(1)} %copy-done.2, ...), custom_call_target="tpu_custom_call" | custom-call | flops 7516192768 | bytes 14680064 | tf_op jit(solution)/shard_map/pallas_call | solution.py:219
  74.6 7.4 %shard_map.116 = (bf16[2,128,512]{2,1,0:T(8,128)(2,1)S(1)}, f32[128,128]{1,0:T(8,128)S(1)}) custom-call(bf16[128,3584]{1,0:T(8,128)(2,1)S(1)} %get-tuple-element.61.gate, bf16[128,3584]{1,0:T(8,128)(2,1)S(1)} %get-tuple-element.62.upper, bf16[2048,3584]{1,0:T(8,128)(2,1)} %bitcast.194, bf16[2048,3584]{1,0:T(8,128)(2,1)} %bitcast.208, ...), custom_call_target="tpu_custom_call" | custom-call | flops 7516192768 | bytes 14680064 | tf_op jit(solution)/shard_map/pallas_call | solution.py:219
  83.5 3.0 collective-permute-start.9
  90.7 8.5 %collective-permute-done.8 = f32[5,128]{1,0:T(8,128)S(1)} collective-permute-done((f32[5,128]{1,0:T(8,128)S(1)}, f32[5,128]{1,0:T(8,128)S(1)}, u32[]{:S(2)}, u32[]{:S(2)}) %collective-permute-start.8) | collective-permute-done | bytes 2592 | tf_op jit(solution)/shard_map/ppermute | solution.py:35
  107.8 3.4 collective-permute-done.15.refs_0_
  111.3 6.2 %shard_map.117 = (f32[128,3584]{1,0:T(8,128)S(1)}, bf16[2,128,3584]{2,1,0:T(8,128)(2,1)S(1)}) custom-call(bf16[128,512]{1,0:T(8,128)(2,1)S(1)} %collective-permute-done.15.refs_0_, bf16[128,512]{1,0:T(8,128)(2,1)S(1)} %collective-permute-done.16.refs_1_, bf16[3584,2048]{1,0:T(8,128)(2,1)} %bitcast.181, bf16[1,4,2,128,3584]{4,3,2,1,0:T(8,128)(2,1)} %refs_4_.13), custom_call_target="tpu_custom_call" | custom-call | flops 3758096384 | bytes 7340032 | tf_op jit(solution)/shard_map/pallas_call | solution.py:122
  118.7 5.7 %shard_map.118.ga = bf16[128,3584]{1,0:T(8,128)(2,1)S(1)} custom-call(bf16[128,512]{1,0:T(8,128)(2,1)S(1)} %collective-permute-done.13.refs_0_, bf16[128,512]{1,0:T(8,128)(2,1)S(1)} %collective-permute-done.14.refs_1_, f32[128,3584]{1,0:T(8,128)S(1)} %get-tuple-element.66.refs_2_, bf16[3584,2048]{1,0:T(8,128)(2,1)} %bitcast.182, ...), custom_call_target="tpu_custom_call" | custom-call | flops 3758096384 | bytes 7340032 | tf_op jit(solution)/shard_map/pallas_call | solution.py:122
  126.9 7.4 %shard_map.119 = (bf16[2,128,512]{2,1,0:T(8,128)(2,1)S(1)}, f32[128,128]{1,0:T(8,128)S(1)}, bf16[128,3584]{1,0:T(8,128)(2,1)S(1)}, bf16[128,3584]{1,0:T(8,128)(2,1)S(1)}) custom-call(bf16[128,3584]{1,0:T(8,128)(2,1)S(1)} %shard_map.118.ga, bf16[128,3584]{1,0:T(8,128)(2,1)S(1)} %collective-permute-done.17.gb, ...), custom_call_target="tpu_custom_call" | custom-call | flops 7516192768 | bytes 14680064 | tf_op jit(solution)/shard_map/pallas_call | solution.py:219
  134.3 7.4 %shard_map.120 = (bf16[2,128,512]{2,1,0:T(8,128)(2,1)S(1)}, f32[128,128]{1,0:T(8,128)S(1)}) custom-call(bf16[128,3584]{1,0:T(8,128)(2,1)S(1)} %get-tuple-element.69.gate, bf16[128,3584]{1,0:T(8,128)(2,1)S(1)} %get-tuple-element.70.upper, bf16[2048,3584]{1,0:T(8,128)(2,1)} %bitcast.196, bf16[2048,3584]{1,0:T(8,128)(2,1)} %bitcast.210, ...), custom_call_target="tpu_custom_call" | custom-call | flops 7516192768 | bytes 14680064 | tf_op jit(solution)/shard_map/pallas_call | solution.py:219
  150.2 8.7 %collective-permute-done.23 = f32[1,128]{1,0:T(1,128)S(1)} collective-permute-done((f32[1,128]{1,0:T(1,128)S(1)}, f32[1,128]{1,0:T(1,128)S(1)}, u32[]{:S(2)}, u32[]{:S(2)}) %collective-permute-start.23) | collective-permute-done | bytes 544 | tf_op jit(solution)/shard_map/ppermute | solution.py:35
  159.9 3.1 collective-permute-start.27
  169.3 6.2 %shard_map.121 = (f32[128,3584]{1,0:T(8,128)S(1)}, bf16[2,128,3584]{2,1,0:T(8,128)(2,1)S(1)}) custom-call(bf16[128,512]{1,0:T(8,128)(2,1)S(1)} %collective-permute-done.27.refs_0_, bf16[128,512]{1,0:T(8,128)(2,1)S(1)} %collective-permute-done.28.refs_1_, bf16[3584,2048]{1,0:T(8,128)(2,1)} %bitcast.183, bf16[1,4,2,128,3584]{4,3,2,1,0:T(8,128)(2,1)} %refs_4_.13), custom_call_target="tpu_custom_call" | custom-call | flops 3758096384 | bytes 7340032 | tf_op jit(solution)/shard_map/pallas_call | solution.py:122
  178.2 5.7 %shard_map.122.ga = bf16[128,3584]{1,0:T(8,128)(2,1)S(1)} custom-call(bf16[128,512]{1,0:T(8,128)(2,1)S(1)} %collective-permute-done.25.refs_0_, bf16[128,512]{1,0:T(8,128)(2,1)S(1)} %collective-permute-done.26.refs_1_, f32[128,3584]{1,0:T(8,128)S(1)} %get-tuple-element.74.refs_2_, bf16[3584,2048]{1,0:T(8,128)(2,1)} %bitcast.184, ...), custom_call_target="tpu_custom_call" | custom-call | flops 3758096384 | bytes 7340032 | tf_op jit(solution)/shard_map/pallas_call | solution.py:122
  186.4 7.4 %shard_map.123 = (bf16[2,128,512]{2,1,0:T(8,128)(2,1)S(1)}, f32[128,128]{1,0:T(8,128)S(1)}, bf16[128,3584]{1,0:T(8,128)(2,1)S(1)}, bf16[128,3584]{1,0:T(8,128)(2,1)S(1)}) custom-call(bf16[128,3584]{1,0:T(8,128)(2,1)S(1)} %shard_map.122.ga, bf16[128,3584]{1,0:T(8,128)(2,1)S(1)} %collective-permute-done.29.gb, ...), custom_call_target="tpu_custom_call" | custom-call | flops 7516192768 | bytes 14680064 | tf_op jit(solution)/shard_map/pallas_call | solution.py:219
  193.8 7.4 %shard_map.124 = (bf16[2,128,512]{2,1,0:T(8,128)(2,1)S(1)}, f32[128,128]{1,0:T(8,128)S(1)}) custom-call(bf16[128,3584]{1,0:T(8,128)(2,1)S(1)} %get-tuple-element.77.gate, bf16[128,3584]{1,0:T(8,128)(2,1)S(1)} %get-tuple-element.78.upper, bf16[2048,3584]{1,0:T(8,128)(2,1)} %bitcast.198, bf16[2048,3584]{1,0:T(8,128)(2,1)} %bitcast.212, ...), custom_call_target="tpu_custom_call" | custom-call | flops 7516192768 | bytes 14680064 | tf_op jit(solution)/shard_map/pallas_call | solution.py:219
  210.2 8.7 %collective-permute-done.35 = f32[1,128]{1,0:T(1,128)S(1)} collective-permute-done((f32[1,128]{1,0:T(1,128)S(1)}, f32[1,128]{1,0:T(1,128)S(1)}, u32[]{:S(2)}, u32[]{:S(2)}) %collective-permute-start.35) | collective-permute-done | bytes 544 | tf_op jit(solution)/shard_map/ppermute | solution.py:35
  229.3 6.2 %shard_map.125 = (f32[128,3584]{1,0:T(8,128)S(1)}, bf16[2,128,3584]{2,1,0:T(8,128)(2,1)S(1)}) custom-call(bf16[128,512]{1,0:T(8,128)(2,1)S(1)} %collective-permute-done.39.refs_0_, bf16[128,512]{1,0:T(8,128)(2,1)S(1)} %collective-permute-done.40.refs_1_, bf16[3584,2048]{1,0:T(8,128)(2,1)} %bitcast.185, bf16[1,4,2,128,3584]{4,3,2,1,0:T(8,128)(2,1)} %refs_4_.13), custom_call_target="tpu_custom_call" | custom-call | flops 3758096384 | bytes 7340032 | tf_op jit(solution)/shard_map/pallas_call | solution.py:122
  237.6 5.7 %shard_map.126.ga = bf16[128,3584]{1,0:T(8,128)(2,1)S(1)} custom-call(bf16[128,512]{1,0:T(8,128)(2,1)S(1)} %collective-permute-done.37.refs_0_, bf16[128,512]{1,0:T(8,128)(2,1)S(1)} %collective-permute-done.38.refs_1_, f32[128,3584]{1,0:T(8,128)S(1)} %get-tuple-element.82.refs_2_, bf16[3584,2048]{1,0:T(8,128)(2,1)} %bitcast.186, ...), custom_call_target="tpu_custom_call" | custom-call | flops 3758096384 | bytes 7340032 | tf_op jit(solution)/shard_map/pallas_call | solution.py:122
  245.8 7.4 %shard_map.127 = (bf16[2,128,512]{2,1,0:T(8,128)(2,1)S(1)}, f32[128,128]{1,0:T(8,128)S(1)}, bf16[128,3584]{1,0:T(8,128)(2,1)S(1)}, bf16[128,3584]{1,0:T(8,128)(2,1)S(1)}) custom-call(bf16[128,3584]{1,0:T(8,128)(2,1)S(1)} %shard_map.126.ga, bf16[128,3584]{1,0:T(8,128)(2,1)S(1)} %collective-permute-done.41.gb, ...), custom_call_target="tpu_custom_call" | custom-call | flops 7516192768 | bytes 14680064 | tf_op jit(solution)/shard_map/pallas_call | solution.py:219
  253.2 7.4 %shard_map.128 = (bf16[2,128,512]{2,1,0:T(8,128)(2,1)S(1)}, f32[128,128]{1,0:T(8,128)S(1)}) custom-call(bf16[128,3584]{1,0:T(8,128)(2,1)S(1)} %get-tuple-element.85.gate, bf16[128,3584]{1,0:T(8,128)(2,1)S(1)} %get-tuple-element.86.upper, bf16[2048,3584]{1,0:T(8,128)(2,1)} %bitcast.200, bf16[2048,3584]{1,0:T(8,128)(2,1)} %bitcast.214, ...), custom_call_target="tpu_custom_call" | custom-call | flops 7516192768 | bytes 14680064 | tf_op jit(solution)/shard_map/pallas_call | solution.py:219
  269.7 8.5 %collective-permute-done.47 = f32[1,128]{1,0:T(1,128)S(1)} collective-permute-done((f32[1,128]{1,0:T(1,128)S(1)}, f32[1,128]{1,0:T(1,128)S(1)}, u32[]{:S(2)}, u32[]{:S(2)}) %collective-permute-start.47) | collective-permute-done | bytes 544 | tf_op jit(solution)/shard_map/ppermute | solution.py:35
  288.7 6.2 %shard_map.129 = (f32[128,3584]{1,0:T(8,128)S(1)}, bf16[2,128,3584]{2,1,0:T(8,128)(2,1)S(1)}) custom-call(bf16[128,512]{1,0:T(8,128)(2,1)S(1)} %collective-permute-done.51.refs_0_, bf16[128,512]{1,0:T(8,128)(2,1)S(1)} %collective-permute-done.52.refs_1_, bf16[3584,2048]{1,0:T(8,128)(2,1)} %bitcast.187, bf16[1,4,2,128,3584]{4,3,2,1,0:T(8,128)(2,1)} %refs_4_.13), custom_call_target="tpu_custom_call" | custom-call | flops 3758096384 | bytes 7340032 | tf_op jit(solution)/shard_map/pallas_call | solution.py:122
  297.0 5.7 %shard_map.130.ga = bf16[128,3584]{1,0:T(8,128)(2,1)S(1)} custom-call(bf16[128,512]{1,0:T(8,128)(2,1)S(1)} %collective-permute-done.49.refs_0_, bf16[128,512]{1,0:T(8,128)(2,1)S(1)} %collective-permute-done.50.refs_1_, f32[128,3584]{1,0:T(8,128)S(1)} %get-tuple-element.90.refs_2_, bf16[3584,2048]{1,0:T(8,128)(2,1)} %bitcast.188, ...), custom_call_target="tpu_custom_call" | custom-call | flops 3758096384 | bytes 7340032 | tf_op jit(solution)/shard_map/pallas_call | solution.py:122
  305.2 7.4 %shard_map.131 = (bf16[2,128,512]{2,1,0:T(8,128)(2,1)S(1)}, f32[128,128]{1,0:T(8,128)S(1)}, bf16[128,3584]{1,0:T(8,128)(2,1)S(1)}, bf16[128,3584]{1,0:T(8,128)(2,1)S(1)}) custom-call(bf16[128,3584]{1,0:T(8,128)(2,1)S(1)} %shard_map.130.ga, bf16[128,3584]{1,0:T(8,128)(2,1)S(1)} %collective-permute-done.53.gb, ...), custom_call_target="tpu_custom_call" | custom-call | flops 7516192768 | bytes 14680064 | tf_op jit(solution)/shard_map/pallas_call | solution.py:219
  312.6 7.4 %shard_map.132 = (bf16[2,128,512]{2,1,0:T(8,128)(2,1)S(1)}, f32[128,128]{1,0:T(8,128)S(1)}) custom-call(bf16[128,3584]{1,0:T(8,128)(2,1)S(1)} %get-tuple-element.93.gate, bf16[128,3584]{1,0:T(8,128)(2,1)S(1)} %get-tuple-element.94.upper, bf16[2048,3584]{1,0:T(8,128)(2,1)} %bitcast.202, bf16[2048,3584]{1,0:T(8,128)(2,1)} %bitcast.216, ...), custom_call_target="tpu_custom_call" | custom-call | flops 7516192768 | bytes 14680064 | tf_op jit(solution)/shard_map/pallas_call | solution.py:219
  329.0 8.7 %collective-permute-done.59 = f32[1,128]{1,0:T(1,128)S(1)} collective-permute-done((f32[1,128]{1,0:T(1,128)S(1)}, f32[1,128]{1,0:T(1,128)S(1)}, u32[]{:S(2)}, u32[]{:S(2)}) %collective-permute-start.59) | collective-permute-done | bytes 544 | tf_op jit(solution)/shard_map/ppermute | solution.py:35
  346.9 6.2 %shard_map.133 = (f32[128,3584]{1,0:T(8,128)S(1)}, bf16[2,128,3584]{2,1,0:T(8,128)(2,1)S(1)}) custom-call(bf16[128,512]{1,0:T(8,128)(2,1)S(1)} %collective-permute-done.63.refs_0_, bf16[128,512]{1,0:T(8,128)(2,1)S(1)} %collective-permute-done.64.refs_1_, bf16[3584,2048]{1,0:T(8,128)(2,1)} %bitcast.189, bf16[1,4,2,128,3584]{4,3,2,1,0:T(8,128)(2,1)} %refs_4_.13), custom_call_target="tpu_custom_call" | custom-call | flops 3758096384 | bytes 7340032 | tf_op jit(solution)/shard_map/pallas_call | solution.py:122
  355.4 5.7 %shard_map.134.ga = bf16[128,3584]{1,0:T(8,128)(2,1)S(1)} custom-call(bf16[128,512]{1,0:T(8,128)(2,1)S(1)} %collective-permute-done.61.refs_0_, bf16[128,512]{1,0:T(8,128)(2,1)S(1)} %collective-permute-done.62.refs_1_, f32[128,3584]{1,0:T(8,128)S(1)} %get-tuple-element.98.refs_2_, bf16[3584,2048]{1,0:T(8,128)(2,1)} %bitcast.190, ...), custom_call_target="tpu_custom_call" | custom-call | flops 3758096384 | bytes 7340032 | tf_op jit(solution)/shard_map/pallas_call | solution.py:122
  363.6 7.4 %shard_map.135 = (bf16[2,128,512]{2,1,0:T(8,128)(2,1)S(1)}, f32[128,128]{1,0:T(8,128)S(1)}, bf16[128,3584]{1,0:T(8,128)(2,1)S(1)}, bf16[128,3584]{1,0:T(8,128)(2,1)S(1)}) custom-call(bf16[128,3584]{1,0:T(8,128)(2,1)S(1)} %shard_map.134.ga, bf16[128,3584]{1,0:T(8,128)(2,1)S(1)} %collective-permute-done.65.gb, ...), custom_call_target="tpu_custom_call" | custom-call | flops 7516192768 | bytes 14680064 | tf_op jit(solution)/shard_map/pallas_call | solution.py:219
  371.0 7.4 %shard_map.136 = (bf16[2,128,512]{2,1,0:T(8,128)(2,1)S(1)}, f32[128,128]{1,0:T(8,128)S(1)}) custom-call(bf16[128,3584]{1,0:T(8,128)(2,1)S(1)} %get-tuple-element.101.gate, bf16[128,3584]{1,0:T(8,128)(2,1)S(1)} %get-tuple-element.102.upper, bf16[2048,3584]{1,0:T(8,128)(2,1)} %bitcast.204, bf16[2048,3584]{1,0:T(8,128)(2,1)} %bitcast.218, ...), custom_call_target="tpu_custom_call" | custom-call | flops 7516192768 | bytes 14680064 | tf_op jit(solution)/shard_map/pallas_call | solution.py:219
  387.4 8.7 %collective-permute-done.71 = f32[1,128]{1,0:T(1,128)S(1)} collective-permute-done((f32[1,128]{1,0:T(1,128)S(1)}, f32[1,128]{1,0:T(1,128)S(1)}, u32[]{:S(2)}, u32[]{:S(2)}) %collective-permute-start.71) | collective-permute-done | bytes 544 | tf_op jit(solution)/shard_map/ppermute | solution.py:35
  407.2 6.2 %shard_map.137 = (f32[128,3584]{1,0:T(8,128)S(1)}, bf16[2,128,3584]{2,1,0:T(8,128)(2,1)S(1)}) custom-call(bf16[128,512]{1,0:T(8,128)(2,1)S(1)} %collective-permute-done.75.refs_0_, bf16[128,512]{1,0:T(8,128)(2,1)S(1)} %collective-permute-done.76.refs_1_, bf16[3584,2048]{1,0:T(8,128)(2,1)} %bitcast.191, bf16[1,4,2,128,3584]{4,3,2,1,0:T(8,128)(2,1)} %refs_4_.13), custom_call_target="tpu_custom_call" | custom-call | flops 3758096384 | bytes 7340032 | tf_op jit(solution)/shard_map/pallas_call | solution.py:122
  413.7 5.7 %shard_map.138.ga = bf16[128,3584]{1,0:T(8,128)(2,1)S(1)} custom-call(bf16[128,512]{1,0:T(8,128)(2,1)S(1)} %collective-permute-done.73.refs_0_, bf16[128,512]{1,0:T(8,128)(2,1)S(1)} %collective-permute-done.74.refs_1_, f32[128,3584]{1,0:T(8,128)S(1)} %get-tuple-element.106.refs_2_, bf16[3584,2048]{1,0:T(8,128)(2,1)} %bitcast.192, ...), custom_call_target="tpu_custom_call" | custom-call | flops 3758096384 | bytes 7340032 | tf_op jit(solution)/shard_map/pallas_call | solution.py:122
  421.9 7.4 %shard_map.139 = (bf16[2,128,512]{2,1,0:T(8,128)(2,1)S(1)}, f32[128,128]{1,0:T(8,128)S(1)}, bf16[128,3584]{1,0:T(8,128)(2,1)S(1)}, bf16[128,3584]{1,0:T(8,128)(2,1)S(1)}) custom-call(bf16[128,3584]{1,0:T(8,128)(2,1)S(1)} %shard_map.138.ga, bf16[128,3584]{1,0:T(8,128)(2,1)S(1)} %collective-permute-done.77.gb, ...), custom_call_target="tpu_custom_call" | custom-call | flops 7516192768 | bytes 14680064 | tf_op jit(solution)/shard_map/pallas_call | solution.py:219
  429.3 7.4 %shard_map.140 = (bf16[2,128,512]{2,1,0:T(8,128)(2,1)S(1)}, f32[128,128]{1,0:T(8,128)S(1)}) custom-call(bf16[128,3584]{1,0:T(8,128)(2,1)S(1)} %get-tuple-element.109.gate, bf16[128,3584]{1,0:T(8,128)(2,1)S(1)} %get-tuple-element.110.upper, bf16[2048,3584]{1,0:T(8,128)(2,1)} %bitcast.206, bf16[2048,3584]{1,0:T(8,128)(2,1)} %bitcast.220, ...), custom_call_target="tpu_custom_call" | custom-call | flops 7516192768 | bytes 14680064 | tf_op jit(solution)/shard_map/pallas_call | solution.py:219
  439.2 3.5 collective-permute-done.82
  449.5 4.9 %collective-permute-done.78 = bf16[128,512]{1,0:T(8,128)(2,1)S(1)} collective-permute-done((bf16[128,512]{1,0:T(8,128)(2,1)S(1)}, bf16[128,512]{1,0:T(8,128)(2,1)S(1)}, u32[]{:S(2)}, u32[]{:S(2)}) %collective-permute-start.78) | collective-permute-done | bytes 131104 | tf_op jit(solution)/shard_map/ppermute | solution.py:35
  454.4 4.1 collective-permute-done.79
  459.6 6.3 %collective-permute-done.84 = f32[128,512]{1,0:T(8,128)S(1)} collective-permute-done((f32[128,512]{1,0:T(8,128)S(1)}, f32[128,512]{1,0:T(8,128)S(1)}, u32[]{:S(2)}, u32[]{:S(2)}) %collective-permute-start.84) | collective-permute-done | bytes 262176 | tf_op jit(solution)/shard_map/ppermute | solution.py:27
  468.4 3.6 collective-permute-done.86
  472.2 4.2 collective-permute-done.87
  (246 shorter events, 158.4 us)
Async XLA Ops:
  7.2 57.4 %all-gather.2.cloned.1.call-start = ((), (), s32[]{:S(2)}) async-start(), calls=%async_computation | async-start | bytes 2621440 | tf_op jit(solution)/shard_map/all_gather | solution.py:250
  15.9 14.8 %collective-permute-start.2 = (bf16[128,512]{1,0:T(8,128)(2,1)S(1)}, bf16[128,512]{1,0:T(8,128)(2,1)S(1)}, u32[]{:S(2)}, u32[]{:S(2)}) collective-permute-start(bf16[128,512]{1,0:T(8,128)(2,1)S(1)} %bitcast_convert_fusion), channel_id=1, source_target_pairs={{0,27},{1,26},{2,25},{3,24},{8,3},{9,2},{10,1},{11,0},{16,11},{17,... | collective-permute-start | bytes 393224 | tf_op jit(solution)/shard_map/ppermute | solution.py:45
  19.2 27.0 %collective-permute-start.1 = (bf16[128,512]{1,0:T(8,128)(2,1)S(1)}, bf16[128,512]{1,0:T(8,128)(2,1)S(1)}, u32[]{:S(2)}, u32[]{:S(2)}) collective-permute-start(bf16[128,512]{1,0:T(8,128)(2,1)S(1)} %bitcast_convert_fusion), channel_id=1, source_target_pairs={{0,26},{1,27},{2,24},{3,25},{8,2},{9,3},{10,0},{11,1},{16,10},{17,... | collective-permute-start | bytes 393224 | tf_op jit(solution)/shard_map/ppermute | solution.py:45
  52.0 47.8 %collective-permute-start = (f32[128,512]{1,0:T(8,128)S(1)}, f32[128,512]{1,0:T(8,128)}, u32[]{:S(2)}, u32[]{:S(2)}) collective-permute-start(f32[128,512]{1,0:T(8,128)S(1)} %bitcast.223), channel_id=1, source_target_pairs={{0,24},{8,0},{16,8},{24,16},{1,25},{9,1},{17,9},{25,17},{2,26},{10... | collective-permute-start | bytes 786440 | tf_op jit(solution)/shard_map/ppermute | solution.py:27
  83.5 16.3 %collective-permute-start.9 = (bf16[128,512]{1,0:T(8,128)(2,1)S(1)}, bf16[128,512]{1,0:T(8,128)(2,1)S(1)}, u32[]{:S(2)}, u32[]{:S(2)}) collective-permute-start(bf16[128,512]{1,0:T(8,128)(2,1)S(1)} %get-tuple-element.154), channel_id=1, source_target_pairs={{0,3},{1,2},{2,1},{3,0},{4,7},{5,6},{6,5},{7,4},{8,11},{9,10},{10,... | collective-permute-start | bytes 393224 | tf_op jit(solution)/shard_map/ppermute | solution.py:35
  86.5 13.3 %collective-permute-start.10 = (bf16[128,512]{1,0:T(8,128)(2,1)S(1)}, bf16[128,512]{1,0:T(8,128)(2,1)S(1)}, u32[]{:S(2)}, u32[]{:S(2)}) collective-permute-start(bf16[128,512]{1,0:T(8,128)(2,1)S(1)} %get-tuple-element.155), channel_id=1, source_target_pairs={{0,2},{1,3},{2,0},{3,1},{4,6},{5,7},{6,4},{7,5},{8,10},{9,11},{10,... | collective-permute-start | bytes 393224 | tf_op jit(solution)/shard_map/ppermute | solution.py:35
  87.2 12.0 %collective-permute-start.8 = (f32[5,128]{1,0:T(8,128)S(1)}, f32[5,128]{1,0:T(8,128)S(1)}, u32[]{:S(2)}, u32[]{:S(2)}) collective-permute-start(f32[5,128]{1,0:T(8,128)S(1)} %add.296), channel_id=1, source_target_pairs={{0,2},{1,3},{2,0},{3,1},{4,6},{5,7},{6,4},{7,5},{8,10},{9,11},{10,... | collective-permute-start | bytes 7688 | tf_op jit(solution)/shard_map/ppermute | solution.py:35
  89.5 10.4 %collective-permute-start.11 = (bf16[128,512]{1,0:T(8,128)(2,1)S(1)}, bf16[128,512]{1,0:T(8,128)(2,1)S(1)}, u32[]{:S(2)}, u32[]{:S(2)}) collective-permute-start(bf16[128,512]{1,0:T(8,128)(2,1)S(1)} %slice_bitcast_fusion.18), channel_id=1, source_target_pairs={{0,1},{1,0},{2,3},{3,2},{4,5},{5,4},{6,7},{7,6},{8,9},{9,8},{10,11... | collective-permute-start | bytes 393224 | tf_op jit(solution)/shard_map/ppermute | solution.py:35
  101.1 10.1 %collective-permute-start.15 = (bf16[128,512]{1,0:T(8,128)(2,1)S(1)}, bf16[128,512]{1,0:T(8,128)(2,1)S(1)}, u32[]{:S(2)}, u32[]{:S(2)}) collective-permute-start(bf16[128,512]{1,0:T(8,128)(2,1)S(1)} %get-tuple-element.136), channel_id=1, source_target_pairs={{0,24},{1,25},{2,26},{3,27},{8,0},{9,1},{10,2},{11,3},{16,8},{17,9... | collective-permute-start | bytes 393224 | tf_op jit(solution)/shard_map/ppermute | solution.py:45
  103.4 14.1 %collective-permute-start.14 = (bf16[128,512]{1,0:T(8,128)(2,1)S(1)}, bf16[128,512]{1,0:T(8,128)(2,1)S(1)}, u32[]{:S(2)}, u32[]{:S(2)}) collective-permute-start(bf16[128,512]{1,0:T(8,128)(2,1)S(1)} %get-tuple-element.136), channel_id=1, source_target_pairs={{0,27},{1,26},{2,25},{3,24},{8,3},{9,2},{10,1},{11,0},{16,11},{17,... | collective-permute-start | bytes 393224 | tf_op jit(solution)/shard_map/ppermute | solution.py:45
  106.3 12.5 %collective-permute-start.13 = (bf16[128,512]{1,0:T(8,128)(2,1)S(1)}, bf16[128,512]{1,0:T(8,128)(2,1)S(1)}, u32[]{:S(2)}, u32[]{:S(2)}) collective-permute-start(bf16[128,512]{1,0:T(8,128)(2,1)S(1)} %get-tuple-element.136), channel_id=1, source_target_pairs={{0,26},{1,27},{2,24},{3,25},{8,2},{9,3},{10,0},{11,1},{16,10},{17,... | collective-permute-start | bytes 393224 | tf_op jit(solution)/shard_map/ppermute | solution.py:45
  142.1 16.8 %collective-permute-start.12 = (f32[128,512]{1,0:T(8,128)S(1)}, f32[128,512]{1,0:T(8,128)S(1)}, u32[]{:S(2)}, u32[]{:S(2)}) collective-permute-start(f32[128,512]{1,0:T(8,128)S(1)} %get-tuple-element.137), channel_id=1, source_target_pairs={{0,24},{8,0},{16,8},{24,16},{1,25},{9,1},{17,9},{25,17},{2,26},{10... | collective-permute-start | bytes 786440 | tf_op jit(solution)/shard_map/ppermute | solution.py:27
  143.6 15.3 %collective-permute-start.18 = (bf16[128,512]{1,0:T(8,128)(2,1)S(1)}, bf16[128,512]{1,0:T(8,128)(2,1)S(1)}, u32[]{:S(2)}, u32[]{:S(2)}) collective-permute-start(bf16[128,512]{1,0:T(8,128)(2,1)S(1)} %get-tuple-element.152), channel_id=1, source_target_pairs={{0,3},{1,2},{2,1},{3,0},{4,7},{5,6},{6,5},{7,4},{8,11},{9,10},{10,... | collective-permute-start | bytes 393224 | tf_op jit(solution)/shard_map/ppermute | solution.py:35
  146.1 12.8 %collective-permute-start.19 = (bf16[128,512]{1,0:T(8,128)(2,1)S(1)}, bf16[128,512]{1,0:T(8,128)(2,1)S(1)}, u32[]{:S(2)}, u32[]{:S(2)}) collective-permute-start(bf16[128,512]{1,0:T(8,128)(2,1)S(1)} %get-tuple-element.153), channel_id=1, source_target_pairs={{0,2},{1,3},{2,0},{3,1},{4,6},{5,7},{6,4},{7,5},{8,10},{9,11},{10,... | collective-permute-start | bytes 393224 | tf_op jit(solution)/shard_map/ppermute | solution.py:35
  147.2 11.7 %collective-permute-start.23 = (f32[1,128]{1,0:T(1,128)S(1)}, f32[1,128]{1,0:T(1,128)S(1)}, u32[]{:S(2)}, u32[]{:S(2)}) collective-permute-start(f32[1,128]{1,0:T(1,128)S(1)} %add.312), channel_id=1, source_target_pairs={{0,2},{1,3},{2,0},{3,1},{4,6},{5,7},{6,4},{7,5},{8,10},{9,11},{10,... | collective-permute-start | bytes 1544 | tf_op jit(solution)/shard_map/ppermute | solution.py:35
  149.0 9.9 %collective-permute-start.20 = (bf16[128,512]{1,0:T(8,128)(2,1)S(1)}, bf16[128,512]{1,0:T(8,128)(2,1)S(1)}, u32[]{:S(2)}, u32[]{:S(2)}) collective-permute-start(bf16[128,512]{1,0:T(8,128)(2,1)S(1)} %slice_bitcast_fusion.15), channel_id=1, source_target_pairs={{0,1},{1,0},{2,3},{3,2},{4,5},{5,4},{6,7},{7,6},{8,9},{9,8},{10,11... | collective-permute-start | bytes 393224 | tf_op jit(solution)/shard_map/ppermute | solution.py:35
  163.0 12.6 %collective-permute-start.26 = (bf16[128,512]{1,0:T(8,128)(2,1)S(1)}, bf16[128,512]{1,0:T(8,128)(2,1)S(1)}, u32[]{:S(2)}, u32[]{:S(2)}) collective-permute-start(bf16[128,512]{1,0:T(8,128)(2,1)S(1)} %get-tuple-element.132), channel_id=1, source_target_pairs={{0,27},{1,26},{2,25},{3,24},{8,3},{9,2},{10,1},{11,0},{16,11},{17,... | collective-permute-start | bytes 393224 | tf_op jit(solution)/shard_map/ppermute | solution.py:45
  165.7 12.5 %collective-permute-start.25 = (bf16[128,512]{1,0:T(8,128)(2,1)S(1)}, bf16[128,512]{1,0:T(8,128)(2,1)S(1)}, u32[]{:S(2)}, u32[]{:S(2)}) collective-permute-start(bf16[128,512]{1,0:T(8,128)(2,1)S(1)} %get-tuple-element.132), channel_id=1, source_target_pairs={{0,26},{1,27},{2,24},{3,25},{8,2},{9,3},{10,0},{11,1},{16,10},{17,... | collective-permute-start | bytes 393224 | tf_op jit(solution)/shard_map/ppermute | solution.py:45
  201.5 17.4 %collective-permute-start.24 = (f32[128,512]{1,0:T(8,128)S(1)}, f32[128,512]{1,0:T(8,128)S(1)}, u32[]{:S(2)}, u32[]{:S(2)}) collective-permute-start(f32[128,512]{1,0:T(8,128)S(1)} %get-tuple-element.133), channel_id=1, source_target_pairs={{0,24},{8,0},{16,8},{24,16},{1,25},{9,1},{17,9},{25,17},{2,26},{10... | collective-permute-start | bytes 786440 | tf_op jit(solution)/shard_map/ppermute | solution.py:27
  204.2 14.7 %collective-permute-start.30 = (bf16[128,512]{1,0:T(8,128)(2,1)S(1)}, bf16[128,512]{1,0:T(8,128)(2,1)S(1)}, u32[]{:S(2)}, u32[]{:S(2)}) collective-permute-start(bf16[128,512]{1,0:T(8,128)(2,1)S(1)} %get-tuple-element.150), channel_id=1, source_target_pairs={{0,3},{1,2},{2,1},{3,0},{4,7},{5,6},{6,5},{7,4},{8,11},{9,10},{10,... | collective-permute-start | bytes 393224 | tf_op jit(solution)/shard_map/ppermute | solution.py:35
  206.0 12.9 %collective-permute-start.31 = (bf16[128,512]{1,0:T(8,128)(2,1)S(1)}, bf16[128,512]{1,0:T(8,128)(2,1)S(1)}, u32[]{:S(2)}, u32[]{:S(2)}) collective-permute-start(bf16[128,512]{1,0:T(8,128)(2,1)S(1)} %get-tuple-element.151), channel_id=1, source_target_pairs={{0,2},{1,3},{2,0},{3,1},{4,6},{5,7},{6,4},{7,5},{8,10},{9,11},{10,... | collective-permute-start | bytes 393224 | tf_op jit(solution)/shard_map/ppermute | solution.py:35
  207.1 11.7 %collective-permute-start.35 = (f32[1,128]{1,0:T(1,128)S(1)}, f32[1,128]{1,0:T(1,128)S(1)}, u32[]{:S(2)}, u32[]{:S(2)}) collective-permute-start(f32[1,128]{1,0:T(1,128)S(1)} %add.321), channel_id=1, source_target_pairs={{0,2},{1,3},{2,0},{3,1},{4,6},{5,7},{6,4},{7,5},{8,10},{9,11},{10,... | collective-permute-start | bytes 1544 | tf_op jit(solution)/shard_map/ppermute | solution.py:35
  209.0 9.9 %collective-permute-start.32 = (bf16[128,512]{1,0:T(8,128)(2,1)S(1)}, bf16[128,512]{1,0:T(8,128)(2,1)S(1)}, u32[]{:S(2)}, u32[]{:S(2)}) collective-permute-start(bf16[128,512]{1,0:T(8,128)(2,1)S(1)} %slice_bitcast_fusion.12), channel_id=1, source_target_pairs={{0,1},{1,0},{2,3},{3,2},{4,5},{5,4},{6,7},{7,6},{8,9},{9,8},{10,11... | collective-permute-start | bytes 393224 | tf_op jit(solution)/shard_map/ppermute | solution.py:35
  222.7 12.9 %collective-permute-start.38 = (bf16[128,512]{1,0:T(8,128)(2,1)S(1)}, bf16[128,512]{1,0:T(8,128)(2,1)S(1)}, u32[]{:S(2)}, u32[]{:S(2)}) collective-permute-start(bf16[128,512]{1,0:T(8,128)(2,1)S(1)} %get-tuple-element.128), channel_id=1, source_target_pairs={{0,27},{1,26},{2,25},{3,24},{8,3},{9,2},{10,1},{11,0},{16,11},{17,... | collective-permute-start | bytes 393224 | tf_op jit(solution)/shard_map/ppermute | solution.py:45
  225.4 12.3 %collective-permute-start.37 = (bf16[128,512]{1,0:T(8,128)(2,1)S(1)}, bf16[128,512]{1,0:T(8,128)(2,1)S(1)}, u32[]{:S(2)}, u32[]{:S(2)}) collective-permute-start(bf16[128,512]{1,0:T(8,128)(2,1)S(1)} %get-tuple-element.128), channel_id=1, source_target_pairs={{0,26},{1,27},{2,24},{3,25},{8,2},{9,3},{10,0},{11,1},{16,10},{17,... | collective-permute-start | bytes 393224 | tf_op jit(solution)/shard_map/ppermute | solution.py:45
  260.9 17.3 %collective-permute-start.36 = (f32[128,512]{1,0:T(8,128)S(1)}, f32[128,512]{1,0:T(8,128)S(1)}, u32[]{:S(2)}, u32[]{:S(2)}) collective-permute-start(f32[128,512]{1,0:T(8,128)S(1)} %get-tuple-element.129), channel_id=1, source_target_pairs={{0,24},{8,0},{16,8},{24,16},{1,25},{9,1},{17,9},{25,17},{2,26},{10... | collective-permute-start | bytes 786440 | tf_op jit(solution)/shard_map/ppermute | solution.py:27
  263.6 14.6 %collective-permute-start.42 = (bf16[128,512]{1,0:T(8,128)(2,1)S(1)}, bf16[128,512]{1,0:T(8,128)(2,1)S(1)}, u32[]{:S(2)}, u32[]{:S(2)}) collective-permute-start(bf16[128,512]{1,0:T(8,128)(2,1)S(1)} %get-tuple-element.148), channel_id=1, source_target_pairs={{0,3},{1,2},{2,1},{3,0},{4,7},{5,6},{6,5},{7,4},{8,11},{9,10},{10,... | collective-permute-start | bytes 393224 | tf_op jit(solution)/shard_map/ppermute | solution.py:35
  266.6 11.7 %collective-permute-start.43 = (bf16[128,512]{1,0:T(8,128)(2,1)S(1)}, bf16[128,512]{1,0:T(8,128)(2,1)S(1)}, u32[]{:S(2)}, u32[]{:S(2)}) collective-permute-start(bf16[128,512]{1,0:T(8,128)(2,1)S(1)} %get-tuple-element.149), channel_id=1, source_target_pairs={{0,2},{1,3},{2,0},{3,1},{4,6},{5,7},{6,4},{7,5},{8,10},{9,11},{10,... | collective-permute-start | bytes 393224 | tf_op jit(solution)/shard_map/ppermute | solution.py:35
  266.6 11.6 %collective-permute-start.47 = (f32[1,128]{1,0:T(1,128)S(1)}, f32[1,128]{1,0:T(1,128)S(1)}, u32[]{:S(2)}, u32[]{:S(2)}) collective-permute-start(f32[1,128]{1,0:T(1,128)S(1)} %add.330), channel_id=1, source_target_pairs={{0,2},{1,3},{2,0},{3,1},{4,6},{5,7},{6,4},{7,5},{8,10},{9,11},{10,... | collective-permute-start | bytes 1544 | tf_op jit(solution)/shard_map/ppermute | solution.py:35
  282.0 12.9 %collective-permute-start.50 = (bf16[128,512]{1,0:T(8,128)(2,1)S(1)}, bf16[128,512]{1,0:T(8,128)(2,1)S(1)}, u32[]{:S(2)}, u32[]{:S(2)}) collective-permute-start(bf16[128,512]{1,0:T(8,128)(2,1)S(1)} %get-tuple-element.124), channel_id=1, source_target_pairs={{0,27},{1,26},{2,25},{3,24},{8,3},{9,2},{10,1},{11,0},{16,11},{17,... | collective-permute-start | bytes 393224 | tf_op jit(solution)/shard_map/ppermute | solution.py:45
  284.7 12.3 %collective-permute-start.49 = (bf16[128,512]{1,0:T(8,128)(2,1)S(1)}, bf16[128,512]{1,0:T(8,128)(2,1)S(1)}, u32[]{:S(2)}, u32[]{:S(2)}) collective-permute-start(bf16[128,512]{1,0:T(8,128)(2,1)S(1)} %get-tuple-element.124), channel_id=1, source_target_pairs={{0,26},{1,27},{2,24},{3,25},{8,2},{9,3},{10,0},{11,1},{16,10},{17,... | collective-permute-start | bytes 393224 | tf_op jit(solution)/shard_map/ppermute | solution.py:45
  320.3 17.4 %collective-permute-start.48 = (f32[128,512]{1,0:T(8,128)S(1)}, f32[128,512]{1,0:T(8,128)S(1)}, u32[]{:S(2)}, u32[]{:S(2)}) collective-permute-start(f32[128,512]{1,0:T(8,128)S(1)} %get-tuple-element.125), channel_id=1, source_target_pairs={{0,24},{8,0},{16,8},{24,16},{1,25},{9,1},{17,9},{25,17},{2,26},{10... | collective-permute-start | bytes 786440 | tf_op jit(solution)/shard_map/ppermute | solution.py:27
  323.1 14.6 %collective-permute-start.54 = (bf16[128,512]{1,0:T(8,128)(2,1)S(1)}, bf16[128,512]{1,0:T(8,128)(2,1)S(1)}, u32[]{:S(2)}, u32[]{:S(2)}) collective-permute-start(bf16[128,512]{1,0:T(8,128)(2,1)S(1)} %get-tuple-element.146), channel_id=1, source_target_pairs={{0,3},{1,2},{2,1},{3,0},{4,7},{5,6},{6,5},{7,4},{8,11},{9,10},{10,... | collective-permute-start | bytes 393224 | tf_op jit(solution)/shard_map/ppermute | solution.py:35
  324.8 12.9 %collective-permute-start.55 = (bf16[128,512]{1,0:T(8,128)(2,1)S(1)}, bf16[128,512]{1,0:T(8,128)(2,1)S(1)}, u32[]{:S(2)}, u32[]{:S(2)}) collective-permute-start(bf16[128,512]{1,0:T(8,128)(2,1)S(1)} %get-tuple-element.147), channel_id=1, source_target_pairs={{0,2},{1,3},{2,0},{3,1},{4,6},{5,7},{6,4},{7,5},{8,10},{9,11},{10,... | collective-permute-start | bytes 393224 | tf_op jit(solution)/shard_map/ppermute | solution.py:35
  326.0 11.7 %collective-permute-start.59 = (f32[1,128]{1,0:T(1,128)S(1)}, f32[1,128]{1,0:T(1,128)S(1)}, u32[]{:S(2)}, u32[]{:S(2)}) collective-permute-start(f32[1,128]{1,0:T(1,128)S(1)} %add.339), channel_id=1, source_target_pairs={{0,2},{1,3},{2,0},{3,1},{4,6},{5,7},{6,4},{7,5},{8,10},{9,11},{10,... | collective-permute-start | bytes 1544 | tf_op jit(solution)/shard_map/ppermute | solution.py:35
  327.8 9.9 %collective-permute-start.56 = (bf16[128,512]{1,0:T(8,128)(2,1)S(1)}, bf16[128,512]{1,0:T(8,128)(2,1)S(1)}, u32[]{:S(2)}, u32[]{:S(2)}) collective-permute-start(bf16[128,512]{1,0:T(8,128)(2,1)S(1)} %slice_bitcast_fusion.6), channel_id=1, source_target_pairs={{0,1},{1,0},{2,3},{3,2},{4,5},{5,4},{6,7},{7,6},{8,9},{9,8},{10,11... | collective-permute-start | bytes 393224 | tf_op jit(solution)/shard_map/ppermute | solution.py:35
  340.4 12.8 %collective-permute-start.62 = (bf16[128,512]{1,0:T(8,128)(2,1)S(1)}, bf16[128,512]{1,0:T(8,128)(2,1)S(1)}, u32[]{:S(2)}, u32[]{:S(2)}) collective-permute-start(bf16[128,512]{1,0:T(8,128)(2,1)S(1)} %get-tuple-element.120), channel_id=1, source_target_pairs={{0,27},{1,26},{2,25},{3,24},{8,3},{9,2},{10,1},{11,0},{16,11},{17,... | collective-permute-start | bytes 393224 | tf_op jit(solution)/shard_map/ppermute | solution.py:45
  343.0 12.3 %collective-permute-start.61 = (bf16[128,512]{1,0:T(8,128)(2,1)S(1)}, bf16[128,512]{1,0:T(8,128)(2,1)S(1)}, u32[]{:S(2)}, u32[]{:S(2)}) collective-permute-start(bf16[128,512]{1,0:T(8,128)(2,1)S(1)} %get-tuple-element.120), channel_id=1, source_target_pairs={{0,26},{1,27},{2,24},{3,25},{8,2},{9,3},{10,0},{11,1},{16,10},{17,... | collective-permute-start | bytes 393224 | tf_op jit(solution)/shard_map/ppermute | solution.py:45
  378.7 17.4 %collective-permute-start.60 = (f32[128,512]{1,0:T(8,128)S(1)}, f32[128,512]{1,0:T(8,128)S(1)}, u32[]{:S(2)}, u32[]{:S(2)}) collective-permute-start(f32[128,512]{1,0:T(8,128)S(1)} %get-tuple-element.121), channel_id=1, source_target_pairs={{0,24},{8,0},{16,8},{24,16},{1,25},{9,1},{17,9},{25,17},{2,26},{10... | collective-permute-start | bytes 786440 | tf_op jit(solution)/shard_map/ppermute | solution.py:27
  381.3 14.8 %collective-permute-start.66 = (bf16[128,512]{1,0:T(8,128)(2,1)S(1)}, bf16[128,512]{1,0:T(8,128)(2,1)S(1)}, u32[]{:S(2)}, u32[]{:S(2)}) collective-permute-start(bf16[128,512]{1,0:T(8,128)(2,1)S(1)} %get-tuple-element.144), channel_id=1, source_target_pairs={{0,3},{1,2},{2,1},{3,0},{4,7},{5,6},{6,5},{7,4},{8,11},{9,10},{10,... | collective-permute-start | bytes 393224 | tf_op jit(solution)/shard_map/ppermute | solution.py:35
  383.3 12.9 %collective-permute-start.67 = (bf16[128,512]{1,0:T(8,128)(2,1)S(1)}, bf16[128,512]{1,0:T(8,128)(2,1)S(1)}, u32[]{:S(2)}, u32[]{:S(2)}) collective-permute-start(bf16[128,512]{1,0:T(8,128)(2,1)S(1)} %get-tuple-element.145), channel_id=1, source_target_pairs={{0,2},{1,3},{2,0},{3,1},{4,6},{5,7},{6,4},{7,5},{8,10},{9,11},{10,... | collective-permute-start | bytes 393224 | tf_op jit(solution)/shard_map/ppermute | solution.py:35
  384.4 11.7 %collective-permute-start.71 = (f32[1,128]{1,0:T(1,128)S(1)}, f32[1,128]{1,0:T(1,128)S(1)}, u32[]{:S(2)}, u32[]{:S(2)}) collective-permute-start(f32[1,128]{1,0:T(1,128)S(1)} %add.348), channel_id=1, source_target_pairs={{0,2},{1,3},{2,0},{3,1},{4,6},{5,7},{6,4},{7,5},{8,10},{9,11},{10,... | collective-permute-start | bytes 1544 | tf_op jit(solution)/shard_map/ppermute | solution.py:35
  386.2 9.9 %collective-permute-start.68 = (bf16[128,512]{1,0:T(8,128)(2,1)S(1)}, bf16[128,512]{1,0:T(8,128)(2,1)S(1)}, u32[]{:S(2)}, u32[]{:S(2)}) collective-permute-start(bf16[128,512]{1,0:T(8,128)(2,1)S(1)} %slice_bitcast_fusion.3), channel_id=1, source_target_pairs={{0,1},{1,0},{2,3},{3,2},{4,5},{5,4},{6,7},{7,6},{8,9},{9,8},{10,11... | collective-permute-start | bytes 393224 | tf_op jit(solution)/shard_map/ppermute | solution.py:35
  397.1 10.1 %collective-permute-start.75 = (bf16[128,512]{1,0:T(8,128)(2,1)S(1)}, bf16[128,512]{1,0:T(8,128)(2,1)S(1)}, u32[]{:S(2)}, u32[]{:S(2)}) collective-permute-start(bf16[128,512]{1,0:T(8,128)(2,1)S(1)} %get-tuple-element.116), channel_id=1, source_target_pairs={{0,24},{1,25},{2,26},{3,27},{8,0},{9,1},{10,2},{11,3},{16,8},{17,9... | collective-permute-start | bytes 393224 | tf_op jit(solution)/shard_map/ppermute | solution.py:45
  398.5 15.0 %collective-permute-start.74 = (bf16[128,512]{1,0:T(8,128)(2,1)S(1)}, bf16[128,512]{1,0:T(8,128)(2,1)S(1)}, u32[]{:S(2)}, u32[]{:S(2)}) collective-permute-start(bf16[128,512]{1,0:T(8,128)(2,1)S(1)} %get-tuple-element.116), channel_id=1, source_target_pairs={{0,27},{1,26},{2,25},{3,24},{8,3},{9,2},{10,1},{11,0},{16,11},{17,... | collective-permute-start | bytes 393224 | tf_op jit(solution)/shard_map/ppermute | solution.py:45
  401.1 12.5 %collective-permute-start.73 = (bf16[128,512]{1,0:T(8,128)(2,1)S(1)}, bf16[128,512]{1,0:T(8,128)(2,1)S(1)}, u32[]{:S(2)}, u32[]{:S(2)}) collective-permute-start(bf16[128,512]{1,0:T(8,128)(2,1)S(1)} %get-tuple-element.116), channel_id=1, source_target_pairs={{0,26},{1,27},{2,24},{3,25},{8,2},{9,3},{10,0},{11,1},{16,10},{17,... | collective-permute-start | bytes 393224 | tf_op jit(solution)/shard_map/ppermute | solution.py:45
  437.0 10.2 %collective-permute-start.72 = (f32[128,512]{1,0:T(8,128)}, f32[128,512]{1,0:T(8,128)S(1)}, u32[]{:S(2)}, u32[]{:S(2)}) collective-permute-start(f32[128,512]{1,0:T(8,128)} %get-tuple-element.117), channel_id=1, source_target_pairs={{0,24},{8,0},{16,8},{24,16},{1,25},{9,1},{17,9},{25,17},{2,26},{10... | collective-permute-start | bytes 786440 | tf_op jit(solution)/shard_map/ppermute | solution.py:27
  447.2 11.4 %collective-permute-start.79 = (bf16[128,512]{1,0:T(8,128)(2,1)S(1)}, bf16[128,512]{1,0:T(8,128)(2,1)S(1)}, u32[]{:S(2)}, u32[]{:S(2)}) collective-permute-start(bf16[128,512]{1,0:T(8,128)(2,1)S(1)} %get-tuple-element.143), channel_id=1, source_target_pairs={{0,2},{1,3},{2,0},{3,1},{4,6},{5,7},{6,4},{7,5},{8,10},{9,11},{10,... | collective-permute-start | bytes 393224 | tf_op jit(solution)/shard_map/ppermute | solution.py:35
  (54 other events, 905.1 us)
Sparse Core Ops, SparseCore 0:
  9.6 54.9 all-gather.1

commit v3 on v2

--- a/solution.py
+++ b/solution.py
@@ -58,17 +58,49 @@
     return lax.rem(lax.axis_index("section") + step + 1, sections)
 
 
-def down_kernel(step, side, tile, half, *refs):
-    pieces, rest = refs[:half], refs[half:]
-    before, rest = (rest[0], rest[1:]) if side else (None, rest)
-    w_ref, h_ref, o_ref = rest[:3]
-    hout, rest = (None, rest[3:]) if side else (rest[3], rest[4:])
-    buf, gy, hsem, sem = rest
+def bring_kernel(step, cols, ahead, *refs):
+    w_ref, sources = refs[0], refs[1 : 1 + ahead]
+    other, outs, sem = refs[1 + ahead], refs[2 + ahead : 2 + 2 * ahead], refs[2 + 2 * ahead]
+    width, span = other.shape
+    group = lax.div(lax.axis_index("col"), cols // 2)
+    columns = pl.ds(pl.multiple_of((1 - group) * span, span), span)
+    parts = sem.shape[0] - ahead
+    copies = []
+    for k in range(ahead):
+        micro = micro_of(step, sources[k].shape[0])
+        copies.append(pltpu.make_async_copy(sources[k].at[micro], outs[k], sem.at[parts + k]))
+    for p in range(parts):
+        at = pl.ds(p * (width // parts), width // parts)
+        copies.append(pltpu.make_async_copy(w_ref.at[at, columns], other.at[at], sem.at[p]))
+    for c in copies:
+        c.start()
+    for c in copies:
+        c.wait()
+
+
+def bring(step, wd, ahead):
+    width, span = wd.shape[0], wd.shape[1] // 2
+    parts = 4
+    size = 2 * width * span
+    return pl.pallas_call(
+        functools.partial(bring_kernel, step, lax.axis_size("col"), len(ahead)),
+        in_specs=[HBM] * (1 + len(ahead)),
+        out_specs=[VMEM] * (1 + len(ahead)),
+        out_shape=[jax.ShapeDtypeStruct((width, span), wd.dtype)]
+        + [jax.ShapeDtypeStruct(x.shape[1:], x.dtype) for x in ahead],
+        scratch_shapes=[pltpu.SemaphoreType.DMA((parts + len(ahead),))],
+        compiler_params=pltpu.CompilerParams(vmem_limit_bytes=16 << 20),
+        cost_estimate=pl.CostEstimate(flops=0, bytes_accessed=size, transcendentals=0),
+    )(in_hbm(wd), *[in_hbm(x) for x in ahead])
+
+
+def near_down_kernel(tile, half, *refs):
+    pieces, (w_ref, o_ref, buf, gy, sem) = refs[:half], refs[half:]
+    depth, _, span = buf.shape
     tiles = w_ref.shape[0] // tile
-    depth, _, span = buf.shape
     chunk = span // half
     col = lax.axis_index("col")
-    group = lax.bitwise_xor(lax.div(col, half), side)
+    group = lax.div(col, half)
     columns = pl.ds(pl.multiple_of(group * span, span), span)
 
     def fetch(i):
@@ -81,8 +113,6 @@
     for j in range(half):
         source = lax.bitwise_xor(lax.rem(col, half), j)
         gy[:, pl.ds(pl.multiple_of(source * chunk, chunk), chunk)] = pieces[j][...]
-    if not side:
-        hcopy = pltpu.make_async_copy(h_ref.at[0, micro_of(step, h_ref.shape[1])], hout, hsem.at[0])
 
     @pl.loop(0, tiles)
     def _(i):
@@ -92,106 +122,173 @@
         def _():
             fetch(i + depth - 1).start()
 
-        if not side:
-
-            @pl.when(i == tiles - depth)
-            def _():
-                hcopy.start()
-
         at = pl.ds(pl.multiple_of(i * tile, tile), tile)
-        part = lax.dot_general(
+        o_ref[:, at] = lax.dot_general(
             gy[...], buf[lax.rem(i, depth)], NT, preferred_element_type=jnp.float32
         )
-        if side:
-            part += before[:, at]
-        o_ref[:, at] = part.astype(o_ref.dtype)
-
-    if not side:
-        hcopy.wait()
-
-
-def down(step, side, pieces, before, wd, hidden):
+
+
+def near_down(pieces, wd):
     half = len(pieces)
     rows, chunk = pieces[0].shape
     width = wd.shape[0]
     span = half * chunk
     tile, depth = 512, 3
-    out = [jax.ShapeDtypeStruct((rows, width), jnp.bfloat16 if side else jnp.float32)]
-    if not side:
-        out.append(jax.ShapeDtypeStruct((2, rows, width), hidden.dtype))
     return pl.pallas_call(
-        functools.partial(down_kernel, step, side, tile, half),
-        in_specs=[VMEM] * (half + len(before)) + [HBM, HBM],
-        out_specs=[VMEM] * len(out),
-        out_shape=out,
+        functools.partial(near_down_kernel, tile, half),
+        in_specs=[VMEM] * half + [HBM],
+        out_specs=VMEM,
+        out_shape=jax.ShapeDtypeStruct((rows, width), jnp.float32),
         scratch_shapes=[
             pltpu.VMEM((depth, tile, span), wd.dtype),
             pltpu.VMEM((rows, span), jnp.bfloat16),
-            pltpu.SemaphoreType.DMA((1,)),
             pltpu.SemaphoreType.DMA((depth,)),
         ],
         compiler_params=pltpu.CompilerParams(vmem_limit_bytes=16 << 20),
         cost_estimate=pl.CostEstimate(
             flops=8 * rows * width * span, bytes_accessed=2 * width * span, transcendentals=0
         ),
-    )(*pieces, *before, in_hbm(wd), in_hbm(hidden))
-
-
-def up_tiles(step, dests, tile, gate, upper, wg_ref, wu_ref, x_ref, o_ref, i_ref, bufs, between):
-    gbuf, ubuf, xbuf, sem = bufs
+    )(*pieces, in_hbm(wd))
+
+
+def first_tile(far, wg_ref, wu_ref, g_ref, u_ref, sem):
+    tile = g_ref.shape[0]
+    chunk = wg_ref.shape[0] // lax.axis_size("col")
+    dest = lax.bitwise_xor(lax.axis_index("col"), far)
+    at = pl.ds(pl.multiple_of(dest * chunk, tile), tile)
+    return (
+        pltpu.make_async_copy(wg_ref.at[at], g_ref, sem.at[0]),
+        pltpu.make_async_copy(wu_ref.at[at], u_ref, sem.at[1]),
+    )
+
+
+def far_down_kernel(tile, half, far, *refs):
+    pieces, (before, w_ref, wg_ref, wu_ref, o_ref, g_ref, u_ref, gy, sem) = refs[:half], refs[half:]
+    width, span = w_ref.shape
+    chunk = span // half
+    copies = first_tile(far, wg_ref, wu_ref, g_ref, u_ref, sem)
+    for c in copies:
+        c.start()
+    col = lax.axis_index("col")
+    for j in range(half):
+        source = lax.bitwise_xor(lax.rem(col, half), j)
+        gy[:, pl.ds(pl.multiple_of(source * chunk, chunk), chunk)] = pieces[j][...]
+
+    @pl.loop(0, width // tile)
+    def _(i):
+        at = pl.ds(pl.multiple_of(i * tile, tile), tile)
+        part = before[:, at] + lax.dot_general(
+            gy[...], w_ref[at, :], NT, preferred_element_type=jnp.float32
+        )
+        o_ref[:, at] = part.astype(o_ref.dtype)
+
+    for c in copies:
+        c.wait()
+
+
+TILE = 256
+
+
+def far_down(pieces, before, weights, wg, wu, far):
+    half = len(pieces)
+    rows = pieces[0].shape[0]
+    width, span = weights.shape
+    return pl.pallas_call(
+        functools.partial(far_down_kernel, 512, half, far),
+        in_specs=[VMEM] * (half + 2) + [HBM, HBM],
+        out_specs=[VMEM] * 3,
+        out_shape=[jax.ShapeDtypeStruct((rows, width), jnp.bfloat16)]
+        + [jax.ShapeDtypeStruct((TILE, width), wg.dtype)] * 2,
+        scratch_shapes=[pltpu.VMEM((rows, span), jnp.bfloat16), pltpu.SemaphoreType.DMA((2,))],
+        compiler_params=pltpu.CompilerParams(vmem_limit_bytes=16 << 20),
+        cost_estimate=pl.CostEstimate(
+            flops=8 * rows * width * span, bytes_accessed=2 * width * span, transcendentals=0
+        ),
+    )(*pieces, before, weights, in_hbm(wg), in_hbm(wu))
+
+
+def up_tiles(dests, gate, upper, g_ref, u_ref, x_ref, wg_ref, wu_ref, outs, i_ref, after, bufs, between):
+    gbuf, ubuf, sem, nsem = bufs
+    tile = gbuf.shape[1]
     depth = gbuf.shape[0]
-    chunk = o_ref.shape[2]
+    chunk = outs[0].shape[1]
     parts = chunk // tile
     tiles = len(dests) * parts
     col = lax.axis_index("col")
-    micro = micro_of(step, x_ref.shape[0])
-
-    def fetch(i):
+
+    def row(i):
         k = lax.div(i, parts)
         j = dests[0]
         for at, other in enumerate(dests[1:]):
             j = jnp.where(k == at + 1, other, j)
         dest = lax.bitwise_xor(col, j)
-        first = pl.multiple_of(dest * chunk + lax.rem(i, parts) * tile, tile)
+        return pl.multiple_of(dest * chunk + lax.rem(i, parts) * tile, tile)
+
+    def fetch(i):
+        at = pl.ds(row(i), tile)
         s = lax.rem(i, depth)
         return (
-            pltpu.make_async_copy(wg_ref.at[pl.ds(first, tile)], gbuf.at[s], sem.at[0, s]),
-            pltpu.make_async_copy(wu_ref.at[pl.ds(first, tile)], ubuf.at[s], sem.at[1, s]),
-            pltpu.make_async_copy(x_ref.at[micro, :, pl.ds(first, tile)], xbuf.at[s], sem.at[2, s]),
+            pltpu.make_async_copy(wg_ref.at[at], gbuf.at[s], sem.at[0, s]),
+            pltpu.make_async_copy(wu_ref.at[at], ubuf.at[s], sem.at[1, s]),
         )
 
-    def start(i):
+    def product(i, g, u):
+        acc = lax.dot_general(gate[...], g, NT, preferred_element_type=jnp.float32)
+        acc += lax.dot_general(upper[...], u, NT, preferred_element_type=jnp.float32)
+        if x_ref is not None:
+            prod = acc * x_ref[:, pl.ds(row(i), tile)].astype(jnp.float32)
+            lanes = i_ref.shape[1]
+            total = i_ref[...]
+            for b in range(tile // lanes):
+                total += prod[:, b * lanes : (b + 1) * lanes]
+            i_ref[...] = total
+        return acc
+
+    for i in range(1, min(depth, tiles)):
         for c in fetch(jnp.int32(i)):
             c.start()
-
-    for i in range(min(depth - 1, tiles)):
-        start(i)
     between()
-    i_ref[...] = jnp.zeros_like(i_ref)
-
-    @pl.loop(0, tiles)
+    if x_ref is not None:
+        i_ref[...] = jnp.zeros_like(i_ref)
+    outs[0][:, :tile] = product(jnp.int32(0), g_ref[...], u_ref[...]).astype(outs[0].dtype)
+
+    @pl.loop(1, tiles)
     def _(i):
         for c in fetch(i):
             c.wait()
 
         @pl.when(i + depth - 1 < tiles)
         def _():
-            start(i + depth - 1)
+            for c in fetch(i + depth - 1):
+                c.start()
+
+        if after is not None:
+
+            @pl.when(i == tiles - 2)
+            def _():
+                for c in first_tile(*after, nsem):
+                    c.start()
 
         s = lax.rem(i, depth)
-        acc = lax.dot_general(gate[...], gbuf[s], NT, preferred_element_type=jnp.float32)
-        acc += lax.dot_general(upper[...], ubuf[s], NT, preferred_element_type=jnp.float32)
+        acc = product(i, gbuf[s], ubuf[s])
         at = pl.ds(pl.multiple_of(lax.rem(i, parts) * tile, tile), tile)
-        o_ref[lax.div(i, parts), :, at] = acc.astype(o_ref.dtype)
-        prod = acc * xbuf[s].astype(jnp.float32)
-        lanes = i_ref.shape[1]
-        total = i_ref[...]
-        for b in range(tile // lanes):
-            total += prod[:, b * lanes : (b + 1) * lanes]
-        i_ref[...] = total
-
-
-def far_kernel(step, dests, tile, ga, gb, h_ref, wg_ref, wu_ref, x_ref, o_ref, i_ref, gate, upper, *bufs):
+        for k in range(len(dests)):
+
+            @pl.when(lax.div(i, parts) == k)
+            def _():
+                outs[k][:, at] = acc.astype(outs[k].dtype)
+
+    if after is not None:
+        for c in first_tile(*after, nsem):
+            c.wait()
+
+
+def far_up_kernel(summed, dests, near, ga, gb, h_ref, g_ref, u_ref, *refs):
+    x_ref, refs = (refs[0], refs[1:]) if summed else (None, refs)
+    wg_ref, wu_ref, gate, upper, ng_ref, nu_ref, *refs = refs
+    i_ref, refs = (refs[0], refs[1:]) if summed else (None, refs)
+    outs, bufs = refs[: len(dests)], refs[len(dests) :]
+
     def gradients():
         block = 512
 
@@ -205,39 +302,44 @@
             gate[:, at] = (g * hu * sig * (1.0 + hg * (1.0 - sig))).astype(jnp.bfloat16)
             upper[:, at] = (g * hg * sig).astype(jnp.bfloat16)
 
-    up_tiles(step, dests, tile, gate, upper, wg_ref, wu_ref, x_ref, o_ref, i_ref, bufs, gradients)
-
-
-def near_kernel(step, dests, tile, gate, upper, wg_ref, wu_ref, x_ref, o_ref, i_ref, *bufs):
-    up_tiles(step, dests, tile, gate, upper, wg_ref, wu_ref, x_ref, o_ref, i_ref, bufs, lambda: None)
-
-
-def up_call(kernel, step, dests, operands, wg, wu, inputs, extra):
+    after = (near, wg_ref, wu_ref, ng_ref, nu_ref)
+    up_tiles(dests, gate, upper, g_ref, u_ref, x_ref, wg_ref, wu_ref, outs, i_ref, after, bufs, gradients)
+
+
+def near_up_kernel(summed, dests, near, gate, upper, g_ref, u_ref, *refs):
+    x_ref, refs = (refs[0], refs[1:]) if summed else (None, refs)
+    wg_ref, wu_ref, *refs = refs
+    i_ref, refs = (refs[0], refs[1:]) if summed else (None, refs)
+    outs, bufs = refs[: len(dests)], refs[len(dests) :]
+    up_tiles(dests, gate, upper, g_ref, u_ref, x_ref, wg_ref, wu_ref, outs, i_ref, None, bufs, lambda: None)
+
+
+def up_call(kernel, summed, dests, near, operands, wg, wu, extra):
     feats, width = wg.shape
-    rows, chunk = inputs.shape[1], feats // lax.axis_size("col")
-    tile, depth = 256, 3
+    rows, chunk = operands[0].shape[0], feats // lax.axis_size("col")
+    depth = 3
+    shapes = [jax.ShapeDtypeStruct(x.shape, x.dtype) for x in extra]
+    if summed:
+        shapes.append(jax.ShapeDtypeStruct((rows, 128), jnp.float32))
+    shapes += [jax.ShapeDtypeStruct((rows, chunk), jnp.bfloat16)] * len(dests)
     return pl.pallas_call(
-        functools.partial(kernel, step, dests, tile),
-        in_specs=[VMEM] * len(operands) + [HBM, HBM, HBM],
-        out_specs=[VMEM] * (2 + extra),
-        out_shape=[
-            jax.ShapeDtypeStruct((len(dests), rows, chunk), jnp.bfloat16),
-            jax.ShapeDtypeStruct((rows, 128), jnp.float32),
-        ]
-        + [jax.ShapeDtypeStruct((rows, width), jnp.bfloat16)] * extra,
+        functools.partial(kernel, summed, dests, near),
+        in_specs=[VMEM] * len(operands) + [HBM, HBM],
+        out_specs=[VMEM] * len(shapes),
+        out_shape=shapes,
         scratch_shapes=[
-            pltpu.VMEM((depth, tile, width), wg.dtype),
-            pltpu.VMEM((depth, tile, width), wu.dtype),
-            pltpu.VMEM((depth, rows, tile), inputs.dtype),
-            pltpu.SemaphoreType.DMA((3, depth)),
+            pltpu.VMEM((depth, TILE, width), wg.dtype),
+            pltpu.VMEM((depth, TILE, width), wu.dtype),
+            pltpu.SemaphoreType.DMA((2, depth)),
+            pltpu.SemaphoreType.DMA((2,)),
         ],
-        compiler_params=pltpu.CompilerParams(vmem_limit_bytes=24 << 20),
+        compiler_params=pltpu.CompilerParams(vmem_limit_bytes=28 << 20),
         cost_estimate=pl.CostEstimate(
             flops=16 * rows * width * chunk * len(dests),
             bytes_accessed=4 * width * chunk * len(dests),
             transcendentals=0,
         ),
-    )(*operands, in_hbm(wg), in_hbm(wu), in_hbm(inputs))
+    )(*operands, in_hbm(wg), in_hbm(wu))
 
 
 def shards(cotangent, incoming, upd_u, upd_v, saved_x, saved_h, norm_gain, w_gate, w_up, w_down):
@@ -257,30 +359,37 @@
     carry = cotangent[0]
     for step in range(2 * sections - 1):
         gy = carry.astype(jnp.bfloat16)
+        near_pieces = [spread(gy, j) for j in range(half)]
         far_pieces = [spread(gy, j) for j in range(half, cols)]
-        near_pieces = [spread(gy, j) for j in range(half)]
         carry = rotate(carry)
         micro = (section_idx + step + 1) % sections
-        ga, hpair = down(step, 0, near_pieces, [], wd, saved_h)
-        (ga,) = down(step, 1, far_pieces, [ga], wd, saved_h)
+        summed = step > 0
+        ahead = [saved_h[0], weighted] if summed else [saved_h[0]]
+        other, hpair, *xs = bring(step, wd, ahead)
+        part = near_down(near_pieces, wd)
+        ga, *firsts = far_down(far_pieces, part, other, wg, wu, far[0])
         gb = swapped(ga, "row", 1)
-        outs_far, inner_far, gate, upper = up_call(
-            far_kernel, step, far, (ga, gb, hpair), wg, wu, weighted, 2
+        gate, upper, ng, nu, *outs = up_call(
+            far_up_kernel, summed, far, near[0], (ga, gb, hpair, *firsts, *xs), wg, wu, [ga, ga, *firsts]
         )
+        inner_far, outs_far = outs[: -len(far)], outs[-len(far) :]
         normgrad = [swapped(outs_far[k], "col", j) for k, j in enumerate(far)]
-        outs_near, inner_near = up_call(near_kernel, step, near, (gate, upper), wg, wu, weighted, 0)
+        outs = up_call(near_up_kernel, summed, near, None, (gate, upper, ng, nu, *xs), wg, wu, [])
+        inner_near, outs_near = outs[: -len(near)], outs[-len(near) :]
         normgrad += [
             swapped(outs_near[k], "col", j) if j else outs_near[k] for k, j in enumerate(near)
         ]
-        inner = jnp.sum(inner_far + inner_near, axis=1)[None]
-        if step == 0:
+        xf = lax.dynamic_index_in_dim(saved_x[0], micro, 0, keepdims=False).astype(jnp.float32)
+        if summed:
+            inner = jnp.sum(inner_far[0] + inner_near[0], axis=1)[None]
+            inner = group_sum(inner)
+            normgrad = sum(p.astype(jnp.float32) for p in normgrad)
+        else:
+            normgrad = sum(p.astype(jnp.float32) for p in normgrad)
+            inner = jnp.sum(gain * normgrad * xf, axis=1)[None]
             sums = group_sum(jnp.concatenate([inner, sumsq_all], axis=0))
             inner, rstd_all = sums[:1], lax.rsqrt(sums[1:] / D + eps)
-        else:
-            inner = group_sum(inner)
         inner = inner[0][:, None] / D
-        normgrad = sum(p.astype(jnp.float32) for p in normgrad)
-        xf = lax.dynamic_index_in_dim(saved_x[0], micro, 0, keepdims=False).astype(jnp.float32)
         rstd = lax.dynamic_index_in_dim(rstd_all, micro, 0, keepdims=False)[:, None]
         updated = carry + rstd * (gain * normgrad) - xf * (rstd * rstd * rstd) * inner
         active = jnp.logical_and(step >= micro, step - micro < sections)
@@ -288,9 +397,9 @@
 
     pulled = rotate(carry)
     resid = pulled + incoming[0] - cotangent[0]
-    local_dots = jnp.einsum("urd,rd->u", upd_v[0], resid, precision=lax.Precision.HIGHEST)
+    local_dots = jnp.sum(upd_v[0] * resid[None], axis=(1, 2))
     dots = group_sum(local_dots)
-    update = jnp.einsum("u,urd->rd", dots, upd_u[0], precision=lax.Precision.HIGHEST)
+    update = jnp.sum(dots[:, None, None] * upd_u[0], axis=0)
     fresh = cotangent[0] + resid - update
     return (fresh[None], resid[None])
 

time: 489 us -> 481 us (0.984)
  starting transfers between devices: 109 us -> 150 us
  waiting for transfers between devices: 157 us -> 120 us
  Pallas kernels: 188 us -> 180 us
    ppermute x28, waiting for transfers between devices: 46.9 us -> 10.6 us  [spread(): return lax.ppermute(x, ('section', 'col'), pairs)]
    ppermute x52, starting transfers between devices: 46.6 us -> 76.8 us  [swapped(): lax.ppermute(x, axis, [(i, i ^ by) for i in range(lax.axis_size(axis))])]
    ppermute x28, starting transfers between devices: 49.8 us -> 60.2 us  [spread(): return lax.ppermute(x, ('section', 'col'), pairs)]
    all_gather x1, waiting for transfers between devices: 9.95 us -> 0.02 us  [shards(): weighted = lax.all_gather(weighted, 'col', axis=2, tiled=True)]
    ppermute x52, waiting for transfers between devices: 94.1 us -> 103 us  [swapped(): lax.ppermute(x, axis, [(i, i ^ by) for i in range(lax.axis_size(axis))])]
    pallas_call x28 -> x35, Pallas kernels: 188 us -> 180 us  [the longest x14 89.1 us: up_call(): pl.pallas_call(functools.partial(kernel, summed, dests, near), in_specs=[...]
  transfers between devices with their start and end apart: 89 -> 89, of which waited for: 38 -> 44; matrix products, arithmetic and copies ran while one was open for 0% -> 1% of each run, Pallas kernels for 13% -> 17%
where the time goes in v3:
time: 481 us; the launch traced here: 480 us
  Pallas kernels  180 us (37%)
  starting transfers between devices  150 us (31%)
  waiting for transfers between devices  120 us (25%)
  between operations  14.8 us (3%)
  other arithmetic  9.47 us (2%)
  local copies, waits for them, and re-layouts  5.6 us (1%)
    ppermute x52, waiting for transfers between devices, swapped(): lax.ppermute(x, axis, [(i, i ^ by) for i in range(lax.axis_size(axis))])  103 us
    pallas_call x14, Pallas kernels, up_call(): pl.pallas_call(functools.partial(kernel, summed, dests, near), in_specs=[...  89.1 us
    ppermute x52, starting transfers between devices, swapped(): lax.ppermute(x, axis, [(i, i ^ by) for i in range(lax.axis_size(axis))])  76.8 us
    ppermute x28, starting transfers between devices, spread(): return lax.ppermute(x, ('section', 'col'), pairs)  60.2 us
    pallas_call x7, Pallas kernels, near_down(): pl.pallas_call(functools.partial(near_down_kernel, tile, half), in_specs=...  39.6 us
    pallas_call x7, Pallas kernels, bring(): pl.pallas_call(functools.partial(bring_kernel, step, lax.axis_size('col')...  27 us
    pallas_call x7, Pallas kernels, far_down(): pl.pallas_call(functools.partial(far_down_kernel, 512, half, far), in_spe...  23.9 us
    ppermute x8, starting transfers between devices, shifted(): lax.ppermute(x, axis, [(i, (i + by) % devices) for i in range(devices)])  13.3 us
  transfers between devices with their start and end apart: 89, of which 44 were waited for; matrix products, arithmetic and copies ran while one was open for 1% of the time, Pallas kernels for 17%

profile of v3, /device:TPU:0, one launch (start us, length us, event | category | flops | bytes accessed | tf_op | source)
XLA Modules:
  0.0 479.8 jit_solution(16814426797874704558)
XLA Ops:
  8.2 4.0 collective-permute-start.3
  13.7 3.5 collective-permute-start.1
  17.2 3.7 shard_map.114
  20.9 5.7 %shard_map.113.refs_2_ = f32[128,3584]{1,0:T(8,128)S(1)} custom-call(bf16[128,512]{1,0:T(8,128)(2,1)S(1)} %collective-permute-done.3.refs_0_, bf16[128,512]{1,0:T(8,128)(2,1)S(1)} %collective-permute-done.4.refs_1_, bf16[3584,2048]{1,0:T(8,128)(2,1)} %bitcast.147), custom_call_target="tpu_custom_call" | custom-call | flops 3758096384 | bytes 7340032 | tf_op jit(solution)/shard_map/pallas_call | solution.py:137
  38.6 7.5 %shard_map.116 = (bf16[128,3584]{1,0:T(8,128)(2,1)S(1)}, bf16[128,3584]{1,0:T(8,128)(2,1)S(1)}, bf16[256,3584]{1,0:T(8,128)(2,1)S(1)}, bf16[256,3584]{1,0:T(8,12...) custom-call(bf16[128,3584]{1,0:T(8,128)(2,1)S(1)} %get-tuple-element.112.ga, ...), custom_call_target="tpu_custom_call" | custom-call | flops 7516192768 | bytes 14680064 | tf_op jit(solution)/shard_map/pallas_call | solution.py:325
  46.2 6.7 %shard_map.117 = (bf16[128,512]{1,0:T(8,128)(2,1)S(1)}, bf16[128,512]{1,0:T(8,128)(2,1)S(1)}) custom-call(bf16[128,3584]{1,0:T(8,128)(2,1)S(1)} %get-tuple-element.118.gate, bf16[128,3584]{1,0:T(8,128)(2,1)S(1)} %get-tuple-element.119.upper, bf16[256,3584]{1,0:T(8,128)(2,1)S(1)} %get-tuple-element.120.g_ref, bf16[256,3584]{1,0:T(8,128)(2,1)S(1)} %get-tuple-element.121.u_ref, ...), custom_call_target="tpu_custom_call" | custom-call | flops 7516192768 | bytes 14680064 | tf_op jit(solution)/shard_map/pallas_call | solution.py:325
  57.6 10.4 %collective-permute-done.8 = bf16[128,512]{1,0:T(8,128)(2,1)S(1)} collective-permute-done((bf16[128,512]{1,0:T(8,128)(2,1)S(1)}, bf16[128,512]{1,0:T(8,128)(2,1)S(1)}, u32[]{:S(2)}, u32[]{:S(2)}) %collective-permute-start.8) | collective-permute-done | bytes 131104 | tf_op jit(solution)/shard_map/ppermute | solution.py:35
  68.0 5.9 %collective-permute-done.7 = bf16[128,512]{1,0:T(8,128)(2,1)S(1)} collective-permute-done((bf16[128,512]{1,0:T(8,128)(2,1)S(1)}, bf16[128,512]{1,0:T(8,128)(2,1)S(1)}, u32[]{:S(2)}, u32[]{:S(2)}) %collective-permute-start.7) | collective-permute-done | bytes 131104 | tf_op jit(solution)/shard_map/ppermute | solution.py:35
  77.2 10.4 %collective-permute-start.10 = (f32[5,128]{1,0:T(8,128)S(1)}, f32[5,128]{1,0:T(8,128)S(1)}, u32[]{:S(2)}, u32[]{:S(2)}) collective-permute-start(f32[5,128]{1,0:T(8,128)S(1)} %fusion.34), channel_id=1, source_target_pairs={{0,1},{1,0},{2,3},{3,2},{4,5},{5,4},{6,7},{7,6},{8,9},{9,8},{10,11... | collective-permute-start | bytes 7688 | tf_op jit(solution)/shard_map/ppermute | solution.py:35
  98.3 6.1 %collective-permute-start.13 = (bf16[128,512]{1,0:T(8,128)(2,1)S(1)}, bf16[128,512]{1,0:T(8,128)(2,1)S(1)}, u32[]{:S(2)}, u32[]{:S(2)}) collective-permute-start(bf16[128,512]{1,0:T(8,128)(2,1)S(1)} %get-tuple-element.242), channel_id=1, source_target_pairs={{0,26},{1,27},{2,24},{3,25},{8,2},{9,3},{10,0},{11,1},{16,10},{17,... | collective-permute-start | bytes 393224 | tf_op jit(solution)/shard_map/ppermute | solution.py:45
  107.2 5.7 %shard_map.118.refs_2_ = f32[128,3584]{1,0:T(8,128)S(1)} custom-call(bf16[128,512]{1,0:T(8,128)(2,1)S(1)} %collective-permute-done.15.refs_0_, bf16[128,512]{1,0:T(8,128)(2,1)S(1)} %collective-permute-done.16.refs_1_, bf16[3584,2048]{1,0:T(8,128)(2,1)} %bitcast.148), custom_call_target="tpu_custom_call" | custom-call | flops 3758096384 | bytes 7340032 | tf_op jit(solution)/shard_map/pallas_call | solution.py:137
  112.9 3.9 shard_map.119
  122.8 6.4 %shard_map.121 = (bf16[128,3584]{1,0:T(8,128)(2,1)S(1)}, bf16[128,3584]{1,0:T(8,128)(2,1)S(1)}, bf16[256,3584]{1,0:T(8,128)(2,1)S(1)}, bf16[256,3584]{1,0:T(8,12...) custom-call(bf16[128,3584]{1,0:T(8,128)(2,1)S(1)} %get-tuple-element.125.ga, ...), custom_call_target="tpu_custom_call" | custom-call | flops 7516192768 | bytes 14680064 | tf_op jit(solution)/shard_map/pallas_call | solution.py:325
  129.2 6.1 %shard_map.122 = (f32[128,128]{1,0:T(8,128)S(1)}, bf16[128,512]{1,0:T(8,128)(2,1)S(1)}, bf16[128,512]{1,0:T(8,128)(2,1)S(1)}) custom-call(bf16[128,3584]{1,0:T(8,128)(2,1)S(1)} %get-tuple-element.132.gate, bf16[128,3584]{1,0:T(8,128)(2,1)S(1)} %get-tuple-element.133.upper, bf16[256,3584]{1,0:T(8,128)(2,1)S(1)} %get-tuple-element.134.g_ref, ...), custom_call_target="tpu_custom_call" | custom-call | flops 7516192768 | bytes 14680064 | tf_op jit(solution)/shard_map/pallas_call | solution.py:325
  136.7 3.6 collective-permute-done.22
  143.2 3.9 collective-permute-start.18
  148.6 6.3 %collective-permute-done.19 = bf16[128,512]{1,0:T(8,128)(2,1)S(1)} collective-permute-done((bf16[128,512]{1,0:T(8,128)(2,1)S(1)}, bf16[128,512]{1,0:T(8,128)(2,1)S(1)}, u32[]{:S(2)}, u32[]{:S(2)}) %collective-permute-start.19) | collective-permute-done | bytes 131104 | tf_op jit(solution)/shard_map/ppermute | solution.py:35
  158.2 5.9 %collective-permute-start.28 = (bf16[128,512]{1,0:T(8,128)(2,1)S(1)}, bf16[128,512]{1,0:T(8,128)(2,1)S(1)}, u32[]{:S(2)}, u32[]{:S(2)}) collective-permute-start(bf16[128,512]{1,0:T(8,128)(2,1)S(1)} %get-tuple-element.238), channel_id=1, source_target_pairs={{0,25},{1,24},{2,27},{3,26},{8,1},{9,0},{10,3},{11,2},{16,9},{17,8... | collective-permute-start | bytes 393224 | tf_op jit(solution)/shard_map/ppermute | solution.py:45
  164.1 3.9 shard_map.124
  170.8 5.7 %shard_map.123.refs_2_ = f32[128,3584]{1,0:T(8,128)S(1)} custom-call(bf16[128,512]{1,0:T(8,128)(2,1)S(1)} %collective-permute-done.27.refs_0_, bf16[128,512]{1,0:T(8,128)(2,1)S(1)} %collective-permute-done.28.refs_1_, bf16[3584,2048]{1,0:T(8,128)(2,1)} %bitcast.151), custom_call_target="tpu_custom_call" | custom-call | flops 3758096384 | bytes 7340032 | tf_op jit(solution)/shard_map/pallas_call | solution.py:137
  185.0 6.4 %shard_map.126 = (bf16[128,3584]{1,0:T(8,128)(2,1)S(1)}, bf16[128,3584]{1,0:T(8,128)(2,1)S(1)}, bf16[256,3584]{1,0:T(8,128)(2,1)S(1)}, bf16[256,3584]{1,0:T(8,12...) custom-call(bf16[128,3584]{1,0:T(8,128)(2,1)S(1)} %get-tuple-element.141.ga, ...), custom_call_target="tpu_custom_call" | custom-call | flops 7516192768 | bytes 14680064 | tf_op jit(solution)/shard_map/pallas_call | solution.py:325
  191.4 6.1 %shard_map.127 = (f32[128,128]{1,0:T(8,128)S(1)}, bf16[128,512]{1,0:T(8,128)(2,1)S(1)}, bf16[128,512]{1,0:T(8,128)(2,1)S(1)}) custom-call(bf16[128,3584]{1,0:T(8,128)(2,1)S(1)} %get-tuple-element.148.gate, bf16[128,3584]{1,0:T(8,128)(2,1)S(1)} %get-tuple-element.149.upper, bf16[256,3584]{1,0:T(8,128)(2,1)S(1)} %get-tuple-element.150.g_ref, ...), custom_call_target="tpu_custom_call" | custom-call | flops 7516192768 | bytes 14680064 | tf_op jit(solution)/shard_map/pallas_call | solution.py:325
  212.4 6.7 %collective-permute-done.31 = bf16[128,512]{1,0:T(8,128)(2,1)S(1)} collective-permute-done((bf16[128,512]{1,0:T(8,128)(2,1)S(1)}, bf16[128,512]{1,0:T(8,128)(2,1)S(1)}, u32[]{:S(2)}, u32[]{:S(2)}) %collective-permute-start.31) | collective-permute-done | bytes 131104 | tf_op jit(solution)/shard_map/ppermute | solution.py:35
  221.9 3.9 shard_map.129
  227.5 3.5 collective-permute-start.38
  230.9 5.7 %shard_map.128.refs_2_ = f32[128,3584]{1,0:T(8,128)S(1)} custom-call(bf16[128,512]{1,0:T(8,128)(2,1)S(1)} %collective-permute-done.39.refs_0_, bf16[128,512]{1,0:T(8,128)(2,1)S(1)} %collective-permute-done.40.refs_1_, bf16[3584,2048]{1,0:T(8,128)(2,1)} %bitcast.153), custom_call_target="tpu_custom_call" | custom-call | flops 3758096384 | bytes 7340032 | tf_op jit(solution)/shard_map/pallas_call | solution.py:137
  243.2 6.4 %shard_map.131 = (bf16[128,3584]{1,0:T(8,128)(2,1)S(1)}, bf16[128,3584]{1,0:T(8,128)(2,1)S(1)}, bf16[256,3584]{1,0:T(8,128)(2,1)S(1)}, bf16[256,3584]{1,0:T(8,12...) custom-call(bf16[128,3584]{1,0:T(8,128)(2,1)S(1)} %get-tuple-element.157.ga, ...), custom_call_target="tpu_custom_call" | custom-call | flops 7516192768 | bytes 14680064 | tf_op jit(solution)/shard_map/pallas_call | solution.py:325
  249.6 6.1 %shard_map.132 = (f32[128,128]{1,0:T(8,128)S(1)}, bf16[128,512]{1,0:T(8,128)(2,1)S(1)}, bf16[128,512]{1,0:T(8,128)(2,1)S(1)}) custom-call(bf16[128,3584]{1,0:T(8,128)(2,1)S(1)} %get-tuple-element.164.gate, bf16[128,3584]{1,0:T(8,128)(2,1)S(1)} %get-tuple-element.165.upper, bf16[256,3584]{1,0:T(8,128)(2,1)S(1)} %get-tuple-element.166.g_ref, ...), custom_call_target="tpu_custom_call" | custom-call | flops 7516192768 | bytes 14680064 | tf_op jit(solution)/shard_map/pallas_call | solution.py:325
  270.6 6.3 %collective-permute-done.43 = bf16[128,512]{1,0:T(8,128)(2,1)S(1)} collective-permute-done((bf16[128,512]{1,0:T(8,128)(2,1)S(1)}, bf16[128,512]{1,0:T(8,128)(2,1)S(1)}, u32[]{:S(2)}, u32[]{:S(2)}) %collective-permute-start.43) | collective-permute-done | bytes 131104 | tf_op jit(solution)/shard_map/ppermute | solution.py:35
  278.3 3.7 collective-permute-start.52
  282.0 3.9 shard_map.134
  288.8 5.7 %shard_map.133.refs_2_ = f32[128,3584]{1,0:T(8,128)S(1)} custom-call(bf16[128,512]{1,0:T(8,128)(2,1)S(1)} %collective-permute-done.51.refs_0_, bf16[128,512]{1,0:T(8,128)(2,1)S(1)} %collective-permute-done.52.refs_1_, bf16[3584,2048]{1,0:T(8,128)(2,1)} %bitcast.155), custom_call_target="tpu_custom_call" | custom-call | flops 3758096384 | bytes 7340032 | tf_op jit(solution)/shard_map/pallas_call | solution.py:137
  302.4 6.4 %shard_map.136 = (bf16[128,3584]{1,0:T(8,128)(2,1)S(1)}, bf16[128,3584]{1,0:T(8,128)(2,1)S(1)}, bf16[256,3584]{1,0:T(8,128)(2,1)S(1)}, bf16[256,3584]{1,0:T(8,12...) custom-call(bf16[128,3584]{1,0:T(8,128)(2,1)S(1)} %get-tuple-element.173.ga, ...), custom_call_target="tpu_custom_call" | custom-call | flops 7516192768 | bytes 14680064 | tf_op jit(solution)/shard_map/pallas_call | solution.py:325
  308.8 6.1 %shard_map.137 = (f32[128,128]{1,0:T(8,128)S(1)}, bf16[128,512]{1,0:T(8,128)(2,1)S(1)}, bf16[128,512]{1,0:T(8,128)(2,1)S(1)}) custom-call(bf16[128,3584]{1,0:T(8,128)(2,1)S(1)} %get-tuple-element.180.gate, bf16[128,3584]{1,0:T(8,128)(2,1)S(1)} %get-tuple-element.181.upper, bf16[256,3584]{1,0:T(8,128)(2,1)S(1)} %get-tuple-element.182.g_ref, ...), custom_call_target="tpu_custom_call" | custom-call | flops 7516192768 | bytes 14680064 | tf_op jit(solution)/shard_map/pallas_call | solution.py:325
  330.0 6.2 %collective-permute-done.55 = bf16[128,512]{1,0:T(8,128)(2,1)S(1)} collective-permute-done((bf16[128,512]{1,0:T(8,128)(2,1)S(1)}, bf16[128,512]{1,0:T(8,128)(2,1)S(1)}, u32[]{:S(2)}, u32[]{:S(2)}) %collective-permute-start.55) | collective-permute-done | bytes 131104 | tf_op jit(solution)/shard_map/ppermute | solution.py:35
  339.2 3.9 shard_map.139
  344.3 3.7 collective-permute-start.62
  348.0 5.7 %shard_map.138.refs_2_ = f32[128,3584]{1,0:T(8,128)S(1)} custom-call(bf16[128,512]{1,0:T(8,128)(2,1)S(1)} %collective-permute-done.63.refs_0_, bf16[128,512]{1,0:T(8,128)(2,1)S(1)} %collective-permute-done.64.refs_1_, bf16[3584,2048]{1,0:T(8,128)(2,1)} %bitcast.157), custom_call_target="tpu_custom_call" | custom-call | flops 3758096384 | bytes 7340032 | tf_op jit(solution)/shard_map/pallas_call | solution.py:137
  354.1 3.4 shard_map.140
  360.0 6.4 %shard_map.141 = (bf16[128,3584]{1,0:T(8,128)(2,1)S(1)}, bf16[128,3584]{1,0:T(8,128)(2,1)S(1)}, bf16[256,3584]{1,0:T(8,128)(2,1)S(1)}, bf16[256,3584]{1,0:T(8,12...) custom-call(bf16[128,3584]{1,0:T(8,128)(2,1)S(1)} %get-tuple-element.189.ga, ...), custom_call_target="tpu_custom_call" | custom-call | flops 7516192768 | bytes 14680064 | tf_op jit(solution)/shard_map/pallas_call | solution.py:325
  366.4 6.1 %shard_map.142 = (f32[128,128]{1,0:T(8,128)S(1)}, bf16[128,512]{1,0:T(8,128)(2,1)S(1)}, bf16[128,512]{1,0:T(8,128)(2,1)S(1)}) custom-call(bf16[128,3584]{1,0:T(8,128)(2,1)S(1)} %get-tuple-element.196.gate, bf16[128,3584]{1,0:T(8,128)(2,1)S(1)} %get-tuple-element.197.upper, bf16[256,3584]{1,0:T(8,128)(2,1)S(1)} %get-tuple-element.198.g_ref, ...), custom_call_target="tpu_custom_call" | custom-call | flops 7516192768 | bytes 14680064 | tf_op jit(solution)/shard_map/pallas_call | solution.py:325
  387.6 6.2 %collective-permute-done.67 = bf16[128,512]{1,0:T(8,128)(2,1)S(1)} collective-permute-done((bf16[128,512]{1,0:T(8,128)(2,1)S(1)}, bf16[128,512]{1,0:T(8,128)(2,1)S(1)}, u32[]{:S(2)}, u32[]{:S(2)}) %collective-permute-start.67) | collective-permute-done | bytes 131104 | tf_op jit(solution)/shard_map/ppermute | solution.py:35
  399.2 3.9 shard_map.144
  406.3 5.7 %shard_map.143.refs_2_ = f32[128,3584]{1,0:T(8,128)S(1)} custom-call(bf16[128,512]{1,0:T(8,128)(2,1)S(1)} %collective-permute-done.75.refs_0_, bf16[128,512]{1,0:T(8,128)(2,1)S(1)} %collective-permute-done.76.refs_1_, bf16[3584,2048]{1,0:T(8,128)(2,1)} %bitcast.159), custom_call_target="tpu_custom_call" | custom-call | flops 3758096384 | bytes 7340032 | tf_op jit(solution)/shard_map/pallas_call | solution.py:137
  419.6 6.4 %shard_map.146 = (bf16[128,3584]{1,0:T(8,128)(2,1)S(1)}, bf16[128,3584]{1,0:T(8,128)(2,1)S(1)}, bf16[256,3584]{1,0:T(8,128)(2,1)S(1)}, bf16[256,3584]{1,0:T(8,12...) custom-call(bf16[128,3584]{1,0:T(8,128)(2,1)S(1)} %get-tuple-element.205.ga, ...), custom_call_target="tpu_custom_call" | custom-call | flops 7516192768 | bytes 14680064 | tf_op jit(solution)/shard_map/pallas_call | solution.py:325
  426.0 6.1 %shard_map.147 = (f32[128,128]{1,0:T(8,128)S(1)}, bf16[128,512]{1,0:T(8,128)(2,1)S(1)}, bf16[128,512]{1,0:T(8,128)(2,1)S(1)}) custom-call(bf16[128,3584]{1,0:T(8,128)(2,1)S(1)} %get-tuple-element.212.gate, bf16[128,3584]{1,0:T(8,128)(2,1)S(1)} %get-tuple-element.213.upper, bf16[256,3584]{1,0:T(8,128)(2,1)S(1)} %get-tuple-element.214.g_ref, ...), custom_call_target="tpu_custom_call" | custom-call | flops 7516192768 | bytes 14680064 | tf_op jit(solution)/shard_map/pallas_call | solution.py:325
  447.4 6.2 %collective-permute-done.79 = bf16[128,512]{1,0:T(8,128)(2,1)S(1)} collective-permute-done((bf16[128,512]{1,0:T(8,128)(2,1)S(1)}, bf16[128,512]{1,0:T(8,128)(2,1)S(1)}, u32[]{:S(2)}, u32[]{:S(2)}) %collective-permute-start.79) | collective-permute-done | bytes 131104 | tf_op jit(solution)/shard_map/ppermute | solution.py:35
  455.5 5.7 %collective-permute-done.84 = f32[128,512]{1,0:T(8,128)S(1)} collective-permute-done((f32[128,512]{1,0:T(8,128)S(1)}, f32[128,512]{1,0:T(8,128)S(1)}, u32[]{:S(2)}, u32[]{:S(2)}) %collective-permute-start.84) | collective-permute-done | bytes 262176 | tf_op jit(solution)/shard_map/ppermute | solution.py:27
  (254 shorter events, 197.8 us)
Async XLA Ops:
  7.2 105.8 %all-gather.2.cloned.1.call-start = ((), (), s32[]{:S(2)}) async-start(), calls=%async_computation | async-start | bytes 2621440 | tf_op jit(solution)/shard_map/all_gather | solution.py:352
  8.2 12.7 %collective-permute-start.3 = (bf16[128,512]{1,0:T(8,128)(2,1)S(1)}, bf16[128,512]{1,0:T(8,128)(2,1)S(1)}, u32[]{:S(2)}, u32[]{:S(2)}) collective-permute-start(bf16[128,512]{1,0:T(8,128)(2,1)S(1)} %bitcast_convert_fusion), channel_id=1, source_target_pairs={{0,24},{1,25},{2,26},{3,27},{8,0},{9,1},{10,2},{11,3},{16,8},{17,9... | collective-permute-start | bytes 393224 | tf_op jit(solution)/shard_map/ppermute | solution.py:45
  13.7 13.3 %collective-permute-start.1 = (bf16[128,512]{1,0:T(8,128)(2,1)S(1)}, bf16[128,512]{1,0:T(8,128)(2,1)S(1)}, u32[]{:S(2)}, u32[]{:S(2)}) collective-permute-start(bf16[128,512]{1,0:T(8,128)(2,1)S(1)} %bitcast_convert_fusion), channel_id=1, source_target_pairs={{0,26},{1,27},{2,24},{3,25},{8,2},{9,3},{10,0},{11,1},{16,10},{17,... | collective-permute-start | bytes 393224 | tf_op jit(solution)/shard_map/ppermute | solution.py:45
  17.2 9.9 %collective-permute-start.2 = (bf16[128,512]{1,0:T(8,128)(2,1)S(1)}, bf16[128,512]{1,0:T(8,128)(2,1)S(1)}, u32[]{:S(2)}, u32[]{:S(2)}) collective-permute-start(bf16[128,512]{1,0:T(8,128)(2,1)S(1)} %bitcast_convert_fusion), channel_id=1, source_target_pairs={{0,27},{1,26},{2,25},{3,24},{8,3},{9,2},{10,1},{11,0},{16,11},{17,... | collective-permute-start | bytes 393224 | tf_op jit(solution)/shard_map/ppermute | solution.py:45
  52.9 15.2 %collective-permute-start.8 = (bf16[128,512]{1,0:T(8,128)(2,1)S(1)}, bf16[128,512]{1,0:T(8,128)(2,1)S(1)}, u32[]{:S(2)}, u32[]{:S(2)}) collective-permute-start(bf16[128,512]{1,0:T(8,128)(2,1)S(1)} %get-tuple-element.122), channel_id=1, source_target_pairs={{0,1},{1,0},{2,3},{3,2},{4,5},{5,4},{6,7},{7,6},{8,9},{9,8},{10,11... | collective-permute-start | bytes 393224 | tf_op jit(solution)/shard_map/ppermute | solution.py:35
  55.1 18.8 %collective-permute-start.7 = (bf16[128,512]{1,0:T(8,128)(2,1)S(1)}, bf16[128,512]{1,0:T(8,128)(2,1)S(1)}, u32[]{:S(2)}, u32[]{:S(2)}) collective-permute-start(bf16[128,512]{1,0:T(8,128)(2,1)S(1)} %get-tuple-element.117), channel_id=1, source_target_pairs={{0,2},{1,3},{2,0},{3,1},{4,6},{5,7},{6,4},{7,5},{8,10},{9,11},{10,... | collective-permute-start | bytes 393224 | tf_op jit(solution)/shard_map/ppermute | solution.py:35
  56.9 18.9 %collective-permute-start.6 = (bf16[128,512]{1,0:T(8,128)(2,1)S(1)}, bf16[128,512]{1,0:T(8,128)(2,1)S(1)}, u32[]{:S(2)}, u32[]{:S(2)}) collective-permute-start(bf16[128,512]{1,0:T(8,128)(2,1)S(1)} %get-tuple-element.116), channel_id=1, source_target_pairs={{0,3},{1,2},{2,1},{3,0},{4,7},{5,6},{6,5},{7,4},{8,11},{9,10},{10,... | collective-permute-start | bytes 393224 | tf_op jit(solution)/shard_map/ppermute | solution.py:35
  77.2 12.4 %collective-permute-start.10 = (f32[5,128]{1,0:T(8,128)S(1)}, f32[5,128]{1,0:T(8,128)S(1)}, u32[]{:S(2)}, u32[]{:S(2)}) collective-permute-start(f32[5,128]{1,0:T(8,128)S(1)} %fusion.34), channel_id=1, source_target_pairs={{0,1},{1,0},{2,3},{3,2},{4,5},{5,4},{6,7},{7,6},{8,9},{9,8},{10,11... | collective-permute-start | bytes 7688 | tf_op jit(solution)/shard_map/ppermute | solution.py:35
  96.0 11.3 %collective-permute-start.15 = (bf16[128,512]{1,0:T(8,128)(2,1)S(1)}, bf16[128,512]{1,0:T(8,128)(2,1)S(1)}, u32[]{:S(2)}, u32[]{:S(2)}) collective-permute-start(bf16[128,512]{1,0:T(8,128)(2,1)S(1)} %get-tuple-element.242), channel_id=1, source_target_pairs={{0,24},{1,25},{2,26},{3,27},{8,0},{9,1},{10,2},{11,3},{16,8},{17,9... | collective-permute-start | bytes 393224 | tf_op jit(solution)/shard_map/ppermute | solution.py:45
  98.3 18.6 %collective-permute-start.13 = (bf16[128,512]{1,0:T(8,128)(2,1)S(1)}, bf16[128,512]{1,0:T(8,128)(2,1)S(1)}, u32[]{:S(2)}, u32[]{:S(2)}) collective-permute-start(bf16[128,512]{1,0:T(8,128)(2,1)S(1)} %get-tuple-element.242), channel_id=1, source_target_pairs={{0,26},{1,27},{2,24},{3,25},{8,2},{9,3},{10,0},{11,1},{16,10},{17,... | collective-permute-start | bytes 393224 | tf_op jit(solution)/shard_map/ppermute | solution.py:45
  104.4 12.5 %collective-permute-start.14 = (bf16[128,512]{1,0:T(8,128)(2,1)S(1)}, bf16[128,512]{1,0:T(8,128)(2,1)S(1)}, u32[]{:S(2)}, u32[]{:S(2)}) collective-permute-start(bf16[128,512]{1,0:T(8,128)(2,1)S(1)} %get-tuple-element.242), channel_id=1, source_target_pairs={{0,27},{1,26},{2,25},{3,24},{8,3},{9,2},{10,1},{11,0},{16,11},{17,... | collective-permute-start | bytes 393224 | tf_op jit(solution)/shard_map/ppermute | solution.py:45
  135.6 11.5 %collective-permute-start.12 = (f32[128,512]{1,0:T(8,128)S(1)}, f32[128,512]{1,0:T(8,128)S(1)}, u32[]{:S(2)}, u32[]{:S(2)}) collective-permute-start(f32[128,512]{1,0:T(8,128)S(1)} %get-tuple-element.243), channel_id=1, source_target_pairs={{0,24},{8,0},{16,8},{24,16},{1,25},{9,1},{17,9},{25,17},{2,26},{10... | collective-permute-start | bytes 786440 | tf_op jit(solution)/shard_map/ppermute | solution.py:27
  143.0 11.9 %collective-permute-start.19 = (bf16[128,512]{1,0:T(8,128)(2,1)S(1)}, bf16[128,512]{1,0:T(8,128)(2,1)S(1)}, u32[]{:S(2)}, u32[]{:S(2)}) collective-permute-start(bf16[128,512]{1,0:T(8,128)(2,1)S(1)} %get-tuple-element.131), channel_id=1, source_target_pairs={{0,2},{1,3},{2,0},{3,1},{4,6},{5,7},{6,4},{7,5},{8,10},{9,11},{10,... | collective-permute-start | bytes 393224 | tf_op jit(solution)/shard_map/ppermute | solution.py:35
  143.2 11.7 %collective-permute-start.18 = (bf16[128,512]{1,0:T(8,128)(2,1)S(1)}, bf16[128,512]{1,0:T(8,128)(2,1)S(1)}, u32[]{:S(2)}, u32[]{:S(2)}) collective-permute-start(bf16[128,512]{1,0:T(8,128)(2,1)S(1)} %get-tuple-element.130), channel_id=1, source_target_pairs={{0,3},{1,2},{2,1},{3,0},{4,7},{5,6},{6,5},{7,4},{8,11},{9,10},{10,... | collective-permute-start | bytes 393224 | tf_op jit(solution)/shard_map/ppermute | solution.py:35
  155.0 15.7 %collective-permute-start.27 = (bf16[128,512]{1,0:T(8,128)(2,1)S(1)}, bf16[128,512]{1,0:T(8,128)(2,1)S(1)}, u32[]{:S(2)}, u32[]{:S(2)}) collective-permute-start(bf16[128,512]{1,0:T(8,128)(2,1)S(1)} %get-tuple-element.238), channel_id=1, source_target_pairs={{0,24},{1,25},{2,26},{3,27},{8,0},{9,1},{10,2},{11,3},{16,8},{17,9... | collective-permute-start | bytes 393224 | tf_op jit(solution)/shard_map/ppermute | solution.py:45
  158.2 12.6 %collective-permute-start.28 = (bf16[128,512]{1,0:T(8,128)(2,1)S(1)}, bf16[128,512]{1,0:T(8,128)(2,1)S(1)}, u32[]{:S(2)}, u32[]{:S(2)}) collective-permute-start(bf16[128,512]{1,0:T(8,128)(2,1)S(1)} %get-tuple-element.238), channel_id=1, source_target_pairs={{0,25},{1,24},{2,27},{3,26},{8,1},{9,0},{10,3},{11,2},{16,9},{17,8... | collective-permute-start | bytes 393224 | tf_op jit(solution)/shard_map/ppermute | solution.py:45
  168.0 11.1 %collective-permute-start.25 = (bf16[128,512]{1,0:T(8,128)(2,1)S(1)}, bf16[128,512]{1,0:T(8,128)(2,1)S(1)}, u32[]{:S(2)}, u32[]{:S(2)}) collective-permute-start(bf16[128,512]{1,0:T(8,128)(2,1)S(1)} %get-tuple-element.238), channel_id=1, source_target_pairs={{0,26},{1,27},{2,24},{3,25},{8,2},{9,3},{10,0},{11,1},{16,10},{17,... | collective-permute-start | bytes 393224 | tf_op jit(solution)/shard_map/ppermute | solution.py:45
  168.0 11.0 %collective-permute-start.26 = (bf16[128,512]{1,0:T(8,128)(2,1)S(1)}, bf16[128,512]{1,0:T(8,128)(2,1)S(1)}, u32[]{:S(2)}, u32[]{:S(2)}) collective-permute-start(bf16[128,512]{1,0:T(8,128)(2,1)S(1)} %get-tuple-element.238), channel_id=1, source_target_pairs={{0,27},{1,26},{2,25},{3,24},{8,3},{9,2},{10,1},{11,0},{16,11},{17,... | collective-permute-start | bytes 393224 | tf_op jit(solution)/shard_map/ppermute | solution.py:45
  197.8 12.9 %collective-permute-start.24 = (f32[128,512]{1,0:T(8,128)S(1)}, f32[128,512]{1,0:T(8,128)S(1)}, u32[]{:S(2)}, u32[]{:S(2)}) collective-permute-start(f32[128,512]{1,0:T(8,128)S(1)} %get-tuple-element.239), channel_id=1, source_target_pairs={{0,24},{8,0},{16,8},{24,16},{1,25},{9,1},{17,9},{25,17},{2,26},{10... | collective-permute-start | bytes 786440 | tf_op jit(solution)/shard_map/ppermute | solution.py:27
  206.8 12.3 %collective-permute-start.31 = (bf16[128,512]{1,0:T(8,128)(2,1)S(1)}, bf16[128,512]{1,0:T(8,128)(2,1)S(1)}, u32[]{:S(2)}, u32[]{:S(2)}) collective-permute-start(bf16[128,512]{1,0:T(8,128)(2,1)S(1)} %get-tuple-element.147), channel_id=1, source_target_pairs={{0,2},{1,3},{2,0},{3,1},{4,6},{5,7},{6,4},{7,5},{8,10},{9,11},{10,... | collective-permute-start | bytes 393224 | tf_op jit(solution)/shard_map/ppermute | solution.py:35
  219.3 11.6 %collective-permute-start.39 = (bf16[128,512]{1,0:T(8,128)(2,1)S(1)}, bf16[128,512]{1,0:T(8,128)(2,1)S(1)}, u32[]{:S(2)}, u32[]{:S(2)}) collective-permute-start(bf16[128,512]{1,0:T(8,128)(2,1)S(1)} %get-tuple-element.234), channel_id=1, source_target_pairs={{0,24},{1,25},{2,26},{3,27},{8,0},{9,1},{10,2},{11,3},{16,8},{17,9... | collective-permute-start | bytes 393224 | tf_op jit(solution)/shard_map/ppermute | solution.py:45
  220.2 10.8 %collective-permute-start.40 = (bf16[128,512]{1,0:T(8,128)(2,1)S(1)}, bf16[128,512]{1,0:T(8,128)(2,1)S(1)}, u32[]{:S(2)}, u32[]{:S(2)}) collective-permute-start(bf16[128,512]{1,0:T(8,128)(2,1)S(1)} %get-tuple-element.234), channel_id=1, source_target_pairs={{0,25},{1,24},{2,27},{3,26},{8,1},{9,0},{10,3},{11,2},{16,9},{17,8... | collective-permute-start | bytes 393224 | tf_op jit(solution)/shard_map/ppermute | solution.py:45
  225.8 11.4 %collective-permute-start.37 = (bf16[128,512]{1,0:T(8,128)(2,1)S(1)}, bf16[128,512]{1,0:T(8,128)(2,1)S(1)}, u32[]{:S(2)}, u32[]{:S(2)}) collective-permute-start(bf16[128,512]{1,0:T(8,128)(2,1)S(1)} %get-tuple-element.234), channel_id=1, source_target_pairs={{0,26},{1,27},{2,24},{3,25},{8,2},{9,3},{10,0},{11,1},{16,10},{17,... | collective-permute-start | bytes 393224 | tf_op jit(solution)/shard_map/ppermute | solution.py:45
  227.5 9.8 %collective-permute-start.38 = (bf16[128,512]{1,0:T(8,128)(2,1)S(1)}, bf16[128,512]{1,0:T(8,128)(2,1)S(1)}, u32[]{:S(2)}, u32[]{:S(2)}) collective-permute-start(bf16[128,512]{1,0:T(8,128)(2,1)S(1)} %get-tuple-element.234), channel_id=1, source_target_pairs={{0,27},{1,26},{2,25},{3,24},{8,3},{9,2},{10,1},{11,0},{16,11},{17,... | collective-permute-start | bytes 393224 | tf_op jit(solution)/shard_map/ppermute | solution.py:45
  256.0 13.0 %collective-permute-start.36 = (f32[128,512]{1,0:T(8,128)S(1)}, f32[128,512]{1,0:T(8,128)S(1)}, u32[]{:S(2)}, u32[]{:S(2)}) collective-permute-start(f32[128,512]{1,0:T(8,128)S(1)} %get-tuple-element.235), channel_id=1, source_target_pairs={{0,24},{8,0},{16,8},{24,16},{1,25},{9,1},{17,9},{25,17},{2,26},{10... | collective-permute-start | bytes 786440 | tf_op jit(solution)/shard_map/ppermute | solution.py:27
  264.6 12.3 %collective-permute-start.43 = (bf16[128,512]{1,0:T(8,128)(2,1)S(1)}, bf16[128,512]{1,0:T(8,128)(2,1)S(1)}, u32[]{:S(2)}, u32[]{:S(2)}) collective-permute-start(bf16[128,512]{1,0:T(8,128)(2,1)S(1)} %get-tuple-element.163), channel_id=1, source_target_pairs={{0,2},{1,3},{2,0},{3,1},{4,6},{5,7},{6,4},{7,5},{8,10},{9,11},{10,... | collective-permute-start | bytes 393224 | tf_op jit(solution)/shard_map/ppermute | solution.py:35
  266.7 10.3 %collective-permute-start.42 = (bf16[128,512]{1,0:T(8,128)(2,1)S(1)}, bf16[128,512]{1,0:T(8,128)(2,1)S(1)}, u32[]{:S(2)}, u32[]{:S(2)}) collective-permute-start(bf16[128,512]{1,0:T(8,128)(2,1)S(1)} %get-tuple-element.162), channel_id=1, source_target_pairs={{0,3},{1,2},{2,1},{3,0},{4,7},{5,6},{6,5},{7,4},{8,11},{9,10},{10,... | collective-permute-start | bytes 393224 | tf_op jit(solution)/shard_map/ppermute | solution.py:35
  277.2 11.6 %collective-permute-start.51 = (bf16[128,512]{1,0:T(8,128)(2,1)S(1)}, bf16[128,512]{1,0:T(8,128)(2,1)S(1)}, u32[]{:S(2)}, u32[]{:S(2)}) collective-permute-start(bf16[128,512]{1,0:T(8,128)(2,1)S(1)} %get-tuple-element.230), channel_id=1, source_target_pairs={{0,24},{1,25},{2,26},{3,27},{8,0},{9,1},{10,2},{11,3},{16,8},{17,9... | collective-permute-start | bytes 393224 | tf_op jit(solution)/shard_map/ppermute | solution.py:45
  278.3 10.5 %collective-permute-start.52 = (bf16[128,512]{1,0:T(8,128)(2,1)S(1)}, bf16[128,512]{1,0:T(8,128)(2,1)S(1)}, u32[]{:S(2)}, u32[]{:S(2)}) collective-permute-start(bf16[128,512]{1,0:T(8,128)(2,1)S(1)} %get-tuple-element.230), channel_id=1, source_target_pairs={{0,25},{1,24},{2,27},{3,26},{8,1},{9,0},{10,3},{11,2},{16,9},{17,8... | collective-permute-start | bytes 393224 | tf_op jit(solution)/shard_map/ppermute | solution.py:45
  285.9 10.5 %collective-permute-start.49 = (bf16[128,512]{1,0:T(8,128)(2,1)S(1)}, bf16[128,512]{1,0:T(8,128)(2,1)S(1)}, u32[]{:S(2)}, u32[]{:S(2)}) collective-permute-start(bf16[128,512]{1,0:T(8,128)(2,1)S(1)} %get-tuple-element.230), channel_id=1, source_target_pairs={{0,26},{1,27},{2,24},{3,25},{8,2},{9,3},{10,0},{11,1},{16,10},{17,... | collective-permute-start | bytes 393224 | tf_op jit(solution)/shard_map/ppermute | solution.py:45
  286.5 9.9 %collective-permute-start.50 = (bf16[128,512]{1,0:T(8,128)(2,1)S(1)}, bf16[128,512]{1,0:T(8,128)(2,1)S(1)}, u32[]{:S(2)}, u32[]{:S(2)}) collective-permute-start(bf16[128,512]{1,0:T(8,128)(2,1)S(1)} %get-tuple-element.230), channel_id=1, source_target_pairs={{0,27},{1,26},{2,25},{3,24},{8,3},{9,2},{10,1},{11,0},{16,11},{17,... | collective-permute-start | bytes 393224 | tf_op jit(solution)/shard_map/ppermute | solution.py:45
  315.2 13.0 %collective-permute-start.48 = (f32[128,512]{1,0:T(8,128)S(1)}, f32[128,512]{1,0:T(8,128)S(1)}, u32[]{:S(2)}, u32[]{:S(2)}) collective-permute-start(f32[128,512]{1,0:T(8,128)S(1)} %get-tuple-element.231), channel_id=1, source_target_pairs={{0,24},{8,0},{16,8},{24,16},{1,25},{9,1},{17,9},{25,17},{2,26},{10... | collective-permute-start | bytes 786440 | tf_op jit(solution)/shard_map/ppermute | solution.py:27
  323.8 12.3 %collective-permute-start.55 = (bf16[128,512]{1,0:T(8,128)(2,1)S(1)}, bf16[128,512]{1,0:T(8,128)(2,1)S(1)}, u32[]{:S(2)}, u32[]{:S(2)}) collective-permute-start(bf16[128,512]{1,0:T(8,128)(2,1)S(1)} %get-tuple-element.179), channel_id=1, source_target_pairs={{0,2},{1,3},{2,0},{3,1},{4,6},{5,7},{6,4},{7,5},{8,10},{9,11},{10,... | collective-permute-start | bytes 393224 | tf_op jit(solution)/shard_map/ppermute | solution.py:35
  326.3 9.9 %collective-permute-start.54 = (bf16[128,512]{1,0:T(8,128)(2,1)S(1)}, bf16[128,512]{1,0:T(8,128)(2,1)S(1)}, u32[]{:S(2)}, u32[]{:S(2)}) collective-permute-start(bf16[128,512]{1,0:T(8,128)(2,1)S(1)} %get-tuple-element.178), channel_id=1, source_target_pairs={{0,3},{1,2},{2,1},{3,0},{4,7},{5,6},{6,5},{7,4},{8,11},{9,10},{10,... | collective-permute-start | bytes 393224 | tf_op jit(solution)/shard_map/ppermute | solution.py:35
  336.3 11.6 %collective-permute-start.63 = (bf16[128,512]{1,0:T(8,128)(2,1)S(1)}, bf16[128,512]{1,0:T(8,128)(2,1)S(1)}, u32[]{:S(2)}, u32[]{:S(2)}) collective-permute-start(bf16[128,512]{1,0:T(8,128)(2,1)S(1)} %get-tuple-element.226), channel_id=1, source_target_pairs={{0,24},{1,25},{2,26},{3,27},{8,0},{9,1},{10,2},{11,3},{16,8},{17,9... | collective-permute-start | bytes 393224 | tf_op jit(solution)/shard_map/ppermute | solution.py:45
  337.2 10.8 %collective-permute-start.64 = (bf16[128,512]{1,0:T(8,128)(2,1)S(1)}, bf16[128,512]{1,0:T(8,128)(2,1)S(1)}, u32[]{:S(2)}, u32[]{:S(2)}) collective-permute-start(bf16[128,512]{1,0:T(8,128)(2,1)S(1)} %get-tuple-element.226), channel_id=1, source_target_pairs={{0,25},{1,24},{2,27},{3,26},{8,1},{9,0},{10,3},{11,2},{16,9},{17,8... | collective-permute-start | bytes 393224 | tf_op jit(solution)/shard_map/ppermute | solution.py:45
  343.1 11.0 %collective-permute-start.61 = (bf16[128,512]{1,0:T(8,128)(2,1)S(1)}, bf16[128,512]{1,0:T(8,128)(2,1)S(1)}, u32[]{:S(2)}, u32[]{:S(2)}) collective-permute-start(bf16[128,512]{1,0:T(8,128)(2,1)S(1)} %get-tuple-element.226), channel_id=1, source_target_pairs={{0,26},{1,27},{2,24},{3,25},{8,2},{9,3},{10,0},{11,1},{16,10},{17,... | collective-permute-start | bytes 393224 | tf_op jit(solution)/shard_map/ppermute | solution.py:45
  344.3 9.8 %collective-permute-start.62 = (bf16[128,512]{1,0:T(8,128)(2,1)S(1)}, bf16[128,512]{1,0:T(8,128)(2,1)S(1)}, u32[]{:S(2)}, u32[]{:S(2)}) collective-permute-start(bf16[128,512]{1,0:T(8,128)(2,1)S(1)} %get-tuple-element.226), channel_id=1, source_target_pairs={{0,27},{1,26},{2,25},{3,24},{8,3},{9,2},{10,1},{11,0},{16,11},{17,... | collective-permute-start | bytes 393224 | tf_op jit(solution)/shard_map/ppermute | solution.py:45
  372.9 13.0 %collective-permute-start.60 = (f32[128,512]{1,0:T(8,128)S(1)}, f32[128,512]{1,0:T(8,128)S(1)}, u32[]{:S(2)}, u32[]{:S(2)}) collective-permute-start(f32[128,512]{1,0:T(8,128)S(1)} %get-tuple-element.227), channel_id=1, source_target_pairs={{0,24},{8,0},{16,8},{24,16},{1,25},{9,1},{17,9},{25,17},{2,26},{10... | collective-permute-start | bytes 786440 | tf_op jit(solution)/shard_map/ppermute | solution.py:27
  381.5 12.3 %collective-permute-start.67 = (bf16[128,512]{1,0:T(8,128)(2,1)S(1)}, bf16[128,512]{1,0:T(8,128)(2,1)S(1)}, u32[]{:S(2)}, u32[]{:S(2)}) collective-permute-start(bf16[128,512]{1,0:T(8,128)(2,1)S(1)} %get-tuple-element.195), channel_id=1, source_target_pairs={{0,2},{1,3},{2,0},{3,1},{4,6},{5,7},{6,4},{7,5},{8,10},{9,11},{10,... | collective-permute-start | bytes 393224 | tf_op jit(solution)/shard_map/ppermute | solution.py:35
  383.7 10.1 %collective-permute-start.66 = (bf16[128,512]{1,0:T(8,128)(2,1)S(1)}, bf16[128,512]{1,0:T(8,128)(2,1)S(1)}, u32[]{:S(2)}, u32[]{:S(2)}) collective-permute-start(bf16[128,512]{1,0:T(8,128)(2,1)S(1)} %get-tuple-element.194), channel_id=1, source_target_pairs={{0,3},{1,2},{2,1},{3,0},{4,7},{5,6},{6,5},{7,4},{8,11},{9,10},{10,... | collective-permute-start | bytes 393224 | tf_op jit(solution)/shard_map/ppermute | solution.py:35
  394.7 11.6 %collective-permute-start.75 = (bf16[128,512]{1,0:T(8,128)(2,1)S(1)}, bf16[128,512]{1,0:T(8,128)(2,1)S(1)}, u32[]{:S(2)}, u32[]{:S(2)}) collective-permute-start(bf16[128,512]{1,0:T(8,128)(2,1)S(1)} %get-tuple-element.222), channel_id=1, source_target_pairs={{0,24},{1,25},{2,26},{3,27},{8,0},{9,1},{10,2},{11,3},{16,8},{17,9... | collective-permute-start | bytes 393224 | tf_op jit(solution)/shard_map/ppermute | solution.py:45
  395.8 10.5 %collective-permute-start.76 = (bf16[128,512]{1,0:T(8,128)(2,1)S(1)}, bf16[128,512]{1,0:T(8,128)(2,1)S(1)}, u32[]{:S(2)}, u32[]{:S(2)}) collective-permute-start(bf16[128,512]{1,0:T(8,128)(2,1)S(1)} %get-tuple-element.222), channel_id=1, source_target_pairs={{0,25},{1,24},{2,27},{3,26},{8,1},{9,0},{10,3},{11,2},{16,9},{17,8... | collective-permute-start | bytes 393224 | tf_op jit(solution)/shard_map/ppermute | solution.py:45
  403.1 10.6 %collective-permute-start.73 = (bf16[128,512]{1,0:T(8,128)(2,1)S(1)}, bf16[128,512]{1,0:T(8,128)(2,1)S(1)}, u32[]{:S(2)}, u32[]{:S(2)}) collective-permute-start(bf16[128,512]{1,0:T(8,128)(2,1)S(1)} %get-tuple-element.222), channel_id=1, source_target_pairs={{0,26},{1,27},{2,24},{3,25},{8,2},{9,3},{10,0},{11,1},{16,10},{17,... | collective-permute-start | bytes 393224 | tf_op jit(solution)/shard_map/ppermute | solution.py:45
  403.9 9.8 %collective-permute-start.74 = (bf16[128,512]{1,0:T(8,128)(2,1)S(1)}, bf16[128,512]{1,0:T(8,128)(2,1)S(1)}, u32[]{:S(2)}, u32[]{:S(2)}) collective-permute-start(bf16[128,512]{1,0:T(8,128)(2,1)S(1)} %get-tuple-element.222), channel_id=1, source_target_pairs={{0,27},{1,26},{2,25},{3,24},{8,3},{9,2},{10,1},{11,0},{16,11},{17,... | collective-permute-start | bytes 393224 | tf_op jit(solution)/shard_map/ppermute | solution.py:45
  432.5 13.6 %collective-permute-start.72 = (f32[128,512]{1,0:T(8,128)}, f32[128,512]{1,0:T(8,128)}, u32[]{:S(2)}, u32[]{:S(2)}) collective-permute-start(f32[128,512]{1,0:T(8,128)} %get-tuple-element.223), channel_id=1, source_target_pairs={{0,24},{8,0},{16,8},{24,16},{1,25},{9,1},{17,9},{25,17},{2,26},{10... | collective-permute-start | bytes 786440 | tf_op jit(solution)/shard_map/ppermute | solution.py:27
  441.1 12.4 %collective-permute-start.79 = (bf16[128,512]{1,0:T(8,128)(2,1)S(1)}, bf16[128,512]{1,0:T(8,128)(2,1)S(1)}, u32[]{:S(2)}, u32[]{:S(2)}) collective-permute-start(bf16[128,512]{1,0:T(8,128)(2,1)S(1)} %get-tuple-element.211), channel_id=1, source_target_pairs={{0,2},{1,3},{2,0},{3,1},{4,6},{5,7},{6,4},{7,5},{8,10},{9,11},{10,... | collective-permute-start | bytes 393224 | tf_op jit(solution)/shard_map/ppermute | solution.py:35
  443.6 10.0 %collective-permute-start.78 = (bf16[128,512]{1,0:T(8,128)(2,1)S(1)}, bf16[128,512]{1,0:T(8,128)(2,1)S(1)}, u32[]{:S(2)}, u32[]{:S(2)}) collective-permute-start(bf16[128,512]{1,0:T(8,128)(2,1)S(1)} %get-tuple-element.210), channel_id=1, source_target_pairs={{0,3},{1,2},{2,1},{3,0},{4,7},{5,6},{6,5},{7,4},{8,11},{9,10},{10,... | collective-permute-start | bytes 393224 | tf_op jit(solution)/shard_map/ppermute | solution.py:35
  (61 other events, 583.3 us)
Sparse Core Ops, SparseCore 0:
  34.1 58.1 all-gather.1

commit v4 on v3

--- a/solution.py
+++ b/solution.py
@@ -128,12 +128,16 @@
         )
 
 
+def down_tile(width):
+    return 896 if width % 896 == 0 else 512
+
+
 def near_down(pieces, wd):
     half = len(pieces)
     rows, chunk = pieces[0].shape
     width = wd.shape[0]
     span = half * chunk
-    tile, depth = 512, 3
+    tile, depth = down_tile(width), 3
     return pl.pallas_call(
         functools.partial(near_down_kernel, tile, half),
         in_specs=[VMEM] * half + [HBM],
@@ -194,7 +198,7 @@
     rows = pieces[0].shape[0]
     width, span = weights.shape
     return pl.pallas_call(
-        functools.partial(far_down_kernel, 512, half, far),
+        functools.partial(far_down_kernel, down_tile(width), half, far),
         in_specs=[VMEM] * (half + 2) + [HBM, HBM],
         out_specs=[VMEM] * 3,
         out_shape=[jax.ShapeDtypeStruct((rows, width), jnp.bfloat16)]
@@ -290,7 +294,7 @@
     outs, bufs = refs[: len(dests)], refs[len(dests) :]
 
     def gradients():
-        block = 512
+        block = 256
 
         @pl.loop(0, gate.shape[1] // block)
         def _(b):
@@ -359,6 +363,8 @@
     carry = cotangent[0]
     for step in range(2 * sections - 1):
         gy = carry.astype(jnp.bfloat16)
+        if step == 0:
+            gy, sumsq_all = lax.optimization_barrier((gy, sumsq_all))
         near_pieces = [spread(gy, j) for j in range(half)]
         far_pieces = [spread(gy, j) for j in range(half, cols)]
         carry = rotate(carry)

time: 481 us -> 473 us (0.983)
  Pallas kernels: 180 us -> 169 us
    pallas_call x7, Pallas kernels: 39.6 us -> 32.1 us  [near_down(): pl.pallas_call(functools.partial(near_down_kernel, tile, half), in_specs=...]
    ppermute x28, waiting for transfers between devices: 10.6 us -> 15.6 us  [spread(): return lax.ppermute(x, ('section', 'col'), pairs)]
  transfers between devices with their start and end apart: 89 -> 89, of which waited for: 44 -> 43; matrix products, arithmetic and copies ran while one was open for 1% -> 0% of each run, Pallas kernels for 17% -> 16%
where the time goes in v4:
time: 473 us
  Pallas kernels  169 us (36%)
  starting transfers between devices  150 us (32%)
  waiting for transfers between devices  124 us (26%)
  between operations  14.7 us (3%)
  other arithmetic  8.97 us (2%)
  local copies, waits for them, and re-layouts  5.59 us (1%)
    ppermute x52, waiting for transfers between devices, swapped(): lax.ppermute(x, axis, [(i, i ^ by) for i in range(lax.axis_size(axis))])  102 us
    pallas_call x14, Pallas kernels, up_call(): pl.pallas_call(functools.partial(kernel, summed, dests, near), in_specs=[...  89.4 us
    ppermute x52, starting transfers between devices, swapped(): lax.ppermute(x, axis, [(i, i ^ by) for i in range(lax.axis_size(axis))])  77.5 us
    ppermute x28, starting transfers between devices, spread(): return lax.ppermute(x, ('section', 'col'), pairs)  56.7 us
    pallas_call x7, Pallas kernels, near_down(): pl.pallas_call(functools.partial(near_down_kernel, tile, half), in_specs=...  32.1 us
    pallas_call x7, Pallas kernels, bring(): pl.pallas_call(functools.partial(bring_kernel, step, lax.axis_size('col')...  27 us
    pallas_call x7, Pallas kernels, far_down(): pl.pallas_call(functools.partial(far_down_kernel, down_tile(width), half,...  20.5 us
    ppermute x8, starting transfers between devices, shifted(): lax.ppermute(x, axis, [(i, (i + by) % devices) for i in range(devices)])  16.1 us
  transfers between devices with their start and end apart: 89, of which 43 were waited for; matrix products, arithmetic and copies ran while one was open for 0% of the time, Pallas kernels for 16%

profile of v4, /device:TPU:0, one launch (start us, length us, event | category | flops | bytes accessed | tf_op | source)
XLA Modules:
  0.0 472.6 jit_solution(14052805277456822064)
XLA Ops:
  10.2 3.9 collective-permute-start.3
  15.7 3.5 collective-permute-start.1
  19.2 3.7 shard_map.114
  22.9 4.6 shard_map.113.refs_2_
  40.1 7.6 %shard_map.116 = (bf16[128,3584]{1,0:T(8,128)(2,1)S(1)}, bf16[128,3584]{1,0:T(8,128)(2,1)S(1)}, bf16[256,3584]{1,0:T(8,128)(2,1)S(1)}, bf16[256,3584]{1,0:T(8,12...) custom-call(bf16[128,3584]{1,0:T(8,128)(2,1)S(1)} %get-tuple-element.115.ga, ...), custom_call_target="tpu_custom_call" | custom-call | flops 7516192768 | bytes 14680064 | tf_op jit(solution)/shard_map/pallas_call | solution.py:329
  47.7 6.7 %shard_map.117 = (bf16[128,512]{1,0:T(8,128)(2,1)S(1)}, bf16[128,512]{1,0:T(8,128)(2,1)S(1)}) custom-call(bf16[128,3584]{1,0:T(8,128)(2,1)S(1)} %get-tuple-element.121.gate, bf16[128,3584]{1,0:T(8,128)(2,1)S(1)} %get-tuple-element.122.upper, bf16[256,3584]{1,0:T(8,128)(2,1)S(1)} %get-tuple-element.123.g_ref, bf16[256,3584]{1,0:T(8,128)(2,1)S(1)} %get-tuple-element.124.u_ref, ...), custom_call_target="tpu_custom_call" | custom-call | flops 7516192768 | bytes 14680064 | tf_op jit(solution)/shard_map/pallas_call | solution.py:329
  59.2 11.2 %collective-permute-done.8 = bf16[128,512]{1,0:T(8,128)(2,1)S(1)} collective-permute-done((bf16[128,512]{1,0:T(8,128)(2,1)S(1)}, bf16[128,512]{1,0:T(8,128)(2,1)S(1)}, u32[]{:S(2)}, u32[]{:S(2)}) %collective-permute-start.8) | collective-permute-done | bytes 131104 | tf_op jit(solution)/shard_map/ppermute | solution.py:35
  73.5 3.8 collective-permute-done.6
  78.7 9.7 %collective-permute-start.10 = (f32[5,128]{1,0:T(8,128)S(1)}, f32[5,128]{1,0:T(8,128)S(1)}, u32[]{:S(2)}, u32[]{:S(2)}) collective-permute-start(f32[5,128]{1,0:T(8,128)S(1)} %fusion.34), channel_id=1, source_target_pairs={{0,1},{1,0},{2,3},{3,2},{4,5},{5,4},{6,7},{7,6},{8,9},{9,8},{10,11... | collective-permute-start | bytes 7688 | tf_op jit(solution)/shard_map/ppermute | solution.py:35
  90.7 3.2 collective-permute-start.11
  99.9 5.1 %collective-permute-start.13 = (bf16[128,512]{1,0:T(8,128)(2,1)S(1)}, bf16[128,512]{1,0:T(8,128)(2,1)S(1)}, u32[]{:S(2)}, u32[]{:S(2)}) collective-permute-start(bf16[128,512]{1,0:T(8,128)(2,1)S(1)} %get-tuple-element.246), channel_id=1, source_target_pairs={{0,26},{1,27},{2,24},{3,25},{8,2},{9,3},{10,0},{11,1},{16,10},{17,... | collective-permute-start | bytes 393224 | tf_op jit(solution)/shard_map/ppermute | solution.py:45
  107.3 4.6 shard_map.118.refs_2_
  111.9 3.9 shard_map.119
  121.3 6.4 %shard_map.121 = (bf16[128,3584]{1,0:T(8,128)(2,1)S(1)}, bf16[128,3584]{1,0:T(8,128)(2,1)S(1)}, bf16[256,3584]{1,0:T(8,128)(2,1)S(1)}, bf16[256,3584]{1,0:T(8,12...) custom-call(bf16[128,3584]{1,0:T(8,128)(2,1)S(1)} %get-tuple-element.129.ga, ...), custom_call_target="tpu_custom_call" | custom-call | flops 7516192768 | bytes 14680064 | tf_op jit(solution)/shard_map/pallas_call | solution.py:329
  127.7 6.1 %shard_map.122 = (f32[128,128]{1,0:T(8,128)S(1)}, bf16[128,512]{1,0:T(8,128)(2,1)S(1)}, bf16[128,512]{1,0:T(8,128)(2,1)S(1)}) custom-call(bf16[128,3584]{1,0:T(8,128)(2,1)S(1)} %get-tuple-element.136.gate, bf16[128,3584]{1,0:T(8,128)(2,1)S(1)} %get-tuple-element.137.upper, bf16[256,3584]{1,0:T(8,128)(2,1)S(1)} %get-tuple-element.138.g_ref, ...), custom_call_target="tpu_custom_call" | custom-call | flops 7516192768 | bytes 14680064 | tf_op jit(solution)/shard_map/pallas_call | solution.py:329
  136.8 3.2 collective-permute-done.22
  148.8 7.0 %collective-permute-done.19 = bf16[128,512]{1,0:T(8,128)(2,1)S(1)} collective-permute-done((bf16[128,512]{1,0:T(8,128)(2,1)S(1)}, bf16[128,512]{1,0:T(8,128)(2,1)S(1)}, u32[]{:S(2)}, u32[]{:S(2)}) %collective-permute-start.19) | collective-permute-done | bytes 131104 | tf_op jit(solution)/shard_map/ppermute | solution.py:35
  160.2 3.9 shard_map.124
  167.7 4.6 shard_map.123.refs_2_
  180.7 6.4 %shard_map.126 = (bf16[128,3584]{1,0:T(8,128)(2,1)S(1)}, bf16[128,3584]{1,0:T(8,128)(2,1)S(1)}, bf16[256,3584]{1,0:T(8,128)(2,1)S(1)}, bf16[256,3584]{1,0:T(8,12...) custom-call(bf16[128,3584]{1,0:T(8,128)(2,1)S(1)} %get-tuple-element.145.ga, ...), custom_call_target="tpu_custom_call" | custom-call | flops 7516192768 | bytes 14680064 | tf_op jit(solution)/shard_map/pallas_call | solution.py:329
  187.1 6.1 %shard_map.127 = (f32[128,128]{1,0:T(8,128)S(1)}, bf16[128,512]{1,0:T(8,128)(2,1)S(1)}, bf16[128,512]{1,0:T(8,128)(2,1)S(1)}) custom-call(bf16[128,3584]{1,0:T(8,128)(2,1)S(1)} %get-tuple-element.152.gate, bf16[128,3584]{1,0:T(8,128)(2,1)S(1)} %get-tuple-element.153.upper, bf16[256,3584]{1,0:T(8,128)(2,1)S(1)} %get-tuple-element.154.g_ref, ...), custom_call_target="tpu_custom_call" | custom-call | flops 7516192768 | bytes 14680064 | tf_op jit(solution)/shard_map/pallas_call | solution.py:329
  208.0 6.1 %collective-permute-done.31 = bf16[128,512]{1,0:T(8,128)(2,1)S(1)} collective-permute-done((bf16[128,512]{1,0:T(8,128)(2,1)S(1)}, bf16[128,512]{1,0:T(8,128)(2,1)S(1)}, u32[]{:S(2)}, u32[]{:S(2)}) %collective-permute-start.31) | collective-permute-done | bytes 131104 | tf_op jit(solution)/shard_map/ppermute | solution.py:35
  215.4 4.2 collective-permute-start.40
  219.6 3.9 shard_map.129
  226.5 4.6 shard_map.128.refs_2_
  231.1 3.4 collective-permute-done.37.refs_0_
  240.0 6.4 %shard_map.131 = (bf16[128,3584]{1,0:T(8,128)(2,1)S(1)}, bf16[128,3584]{1,0:T(8,128)(2,1)S(1)}, bf16[256,3584]{1,0:T(8,128)(2,1)S(1)}, bf16[256,3584]{1,0:T(8,12...) custom-call(bf16[128,3584]{1,0:T(8,128)(2,1)S(1)} %get-tuple-element.161.ga, ...), custom_call_target="tpu_custom_call" | custom-call | flops 7516192768 | bytes 14680064 | tf_op jit(solution)/shard_map/pallas_call | solution.py:329
  246.4 6.1 %shard_map.132 = (f32[128,128]{1,0:T(8,128)S(1)}, bf16[128,512]{1,0:T(8,128)(2,1)S(1)}, bf16[128,512]{1,0:T(8,128)(2,1)S(1)}) custom-call(bf16[128,3584]{1,0:T(8,128)(2,1)S(1)} %get-tuple-element.168.gate, bf16[128,3584]{1,0:T(8,128)(2,1)S(1)} %get-tuple-element.169.upper, bf16[256,3584]{1,0:T(8,128)(2,1)S(1)} %get-tuple-element.170.g_ref, ...), custom_call_target="tpu_custom_call" | custom-call | flops 7516192768 | bytes 14680064 | tf_op jit(solution)/shard_map/pallas_call | solution.py:329
  267.5 6.3 %collective-permute-done.43 = bf16[128,512]{1,0:T(8,128)(2,1)S(1)} collective-permute-done((bf16[128,512]{1,0:T(8,128)(2,1)S(1)}, bf16[128,512]{1,0:T(8,128)(2,1)S(1)}, u32[]{:S(2)}, u32[]{:S(2)}) %collective-permute-start.43) | collective-permute-done | bytes 131104 | tf_op jit(solution)/shard_map/ppermute | solution.py:35
  277.0 3.9 shard_map.134
  281.3 4.3 collective-permute-start.50
  285.6 4.6 shard_map.133.refs_2_
  296.9 6.4 %shard_map.136 = (bf16[128,3584]{1,0:T(8,128)(2,1)S(1)}, bf16[128,3584]{1,0:T(8,128)(2,1)S(1)}, bf16[256,3584]{1,0:T(8,128)(2,1)S(1)}, bf16[256,3584]{1,0:T(8,12...) custom-call(bf16[128,3584]{1,0:T(8,128)(2,1)S(1)} %get-tuple-element.177.ga, ...), custom_call_target="tpu_custom_call" | custom-call | flops 7516192768 | bytes 14680064 | tf_op jit(solution)/shard_map/pallas_call | solution.py:329
  303.3 6.1 %shard_map.137 = (f32[128,128]{1,0:T(8,128)S(1)}, bf16[128,512]{1,0:T(8,128)(2,1)S(1)}, bf16[128,512]{1,0:T(8,128)(2,1)S(1)}) custom-call(bf16[128,3584]{1,0:T(8,128)(2,1)S(1)} %get-tuple-element.184.gate, bf16[128,3584]{1,0:T(8,128)(2,1)S(1)} %get-tuple-element.185.upper, bf16[256,3584]{1,0:T(8,128)(2,1)S(1)} %get-tuple-element.186.g_ref, ...), custom_call_target="tpu_custom_call" | custom-call | flops 7516192768 | bytes 14680064 | tf_op jit(solution)/shard_map/pallas_call | solution.py:329
  324.4 6.1 %collective-permute-done.55 = bf16[128,512]{1,0:T(8,128)(2,1)S(1)} collective-permute-done((bf16[128,512]{1,0:T(8,128)(2,1)S(1)}, bf16[128,512]{1,0:T(8,128)(2,1)S(1)}, u32[]{:S(2)}, u32[]{:S(2)}) %collective-permute-start.55) | collective-permute-done | bytes 131104 | tf_op jit(solution)/shard_map/ppermute | solution.py:35
  331.6 4.1 collective-permute-start.64
  335.7 3.9 shard_map.139
  342.5 4.6 shard_map.138.refs_2_
  355.6 6.4 %shard_map.141 = (bf16[128,3584]{1,0:T(8,128)(2,1)S(1)}, bf16[128,3584]{1,0:T(8,128)(2,1)S(1)}, bf16[256,3584]{1,0:T(8,128)(2,1)S(1)}, bf16[256,3584]{1,0:T(8,12...) custom-call(bf16[128,3584]{1,0:T(8,128)(2,1)S(1)} %get-tuple-element.193.ga, ...), custom_call_target="tpu_custom_call" | custom-call | flops 7516192768 | bytes 14680064 | tf_op jit(solution)/shard_map/pallas_call | solution.py:329
  362.1 6.1 %shard_map.142 = (f32[128,128]{1,0:T(8,128)S(1)}, bf16[128,512]{1,0:T(8,128)(2,1)S(1)}, bf16[128,512]{1,0:T(8,128)(2,1)S(1)}) custom-call(bf16[128,3584]{1,0:T(8,128)(2,1)S(1)} %get-tuple-element.200.gate, bf16[128,3584]{1,0:T(8,128)(2,1)S(1)} %get-tuple-element.201.upper, bf16[256,3584]{1,0:T(8,128)(2,1)S(1)} %get-tuple-element.202.g_ref, ...), custom_call_target="tpu_custom_call" | custom-call | flops 7516192768 | bytes 14680064 | tf_op jit(solution)/shard_map/pallas_call | solution.py:329
  383.2 6.2 %collective-permute-done.67 = bf16[128,512]{1,0:T(8,128)(2,1)S(1)} collective-permute-done((bf16[128,512]{1,0:T(8,128)(2,1)S(1)}, bf16[128,512]{1,0:T(8,128)(2,1)S(1)}, u32[]{:S(2)}, u32[]{:S(2)}) %collective-permute-start.67) | collective-permute-done | bytes 131104 | tf_op jit(solution)/shard_map/ppermute | solution.py:35
  392.9 3.9 shard_map.144
  397.8 3.4 collective-permute-start.74
  401.2 4.6 shard_map.143.refs_2_
  412.9 6.4 %shard_map.146 = (bf16[128,3584]{1,0:T(8,128)(2,1)S(1)}, bf16[128,3584]{1,0:T(8,128)(2,1)S(1)}, bf16[256,3584]{1,0:T(8,128)(2,1)S(1)}, bf16[256,3584]{1,0:T(8,12...) custom-call(bf16[128,3584]{1,0:T(8,128)(2,1)S(1)} %get-tuple-element.209.ga, ...), custom_call_target="tpu_custom_call" | custom-call | flops 7516192768 | bytes 14680064 | tf_op jit(solution)/shard_map/pallas_call | solution.py:329
  419.4 6.2 %shard_map.147 = (f32[128,128]{1,0:T(8,128)S(1)}, bf16[128,512]{1,0:T(8,128)(2,1)S(1)}, bf16[128,512]{1,0:T(8,128)(2,1)S(1)}) custom-call(bf16[128,3584]{1,0:T(8,128)(2,1)S(1)} %get-tuple-element.216.gate, bf16[128,3584]{1,0:T(8,128)(2,1)S(1)} %get-tuple-element.217.upper, bf16[256,3584]{1,0:T(8,128)(2,1)S(1)} %get-tuple-element.218.g_ref, ...), custom_call_target="tpu_custom_call" | custom-call | flops 7516192768 | bytes 14680064 | tf_op jit(solution)/shard_map/pallas_call | solution.py:329
  440.5 6.2 %collective-permute-done.79 = bf16[128,512]{1,0:T(8,128)(2,1)S(1)} collective-permute-done((bf16[128,512]{1,0:T(8,128)(2,1)S(1)}, bf16[128,512]{1,0:T(8,128)(2,1)S(1)}, u32[]{:S(2)}, u32[]{:S(2)}) %collective-permute-start.79) | collective-permute-done | bytes 131104 | tf_op jit(solution)/shard_map/ppermute | solution.py:35
  447.8 5.6 %collective-permute-done.84 = f32[128,512]{1,0:T(8,128)S(1)} collective-permute-done((f32[128,512]{1,0:T(8,128)S(1)}, f32[128,512]{1,0:T(8,128)S(1)}, u32[]{:S(2)}, u32[]{:S(2)}) %collective-permute-start.84) | collective-permute-done | bytes 262176 | tf_op jit(solution)/shard_map/ppermute | solution.py:27
  (248 shorter events, 203.0 us)
Async XLA Ops:
  7.2 104.7 %all-gather.2.cloned.1.call-start = ((), (), s32[]{:S(2)}) async-start(), calls=%async_computation | async-start | bytes 2621440 | tf_op jit(solution)/shard_map/all_gather | solution.py:356
  10.2 12.7 %collective-permute-start.3 = (bf16[128,512]{1,0:T(8,128)(2,1)S(1)}, bf16[128,512]{1,0:T(8,128)(2,1)S(1)}, u32[]{:S(2)}, u32[]{:S(2)}) collective-permute-start(bf16[128,512]{1,0:T(8,128)(2,1)S(1)} %bitcast_convert_fusion), channel_id=1, source_target_pairs={{0,24},{1,25},{2,26},{3,27},{8,0},{9,1},{10,2},{11,3},{16,8},{17,9... | collective-permute-start | bytes 393224 | tf_op jit(solution)/shard_map/ppermute | solution.py:45
  15.7 13.3 %collective-permute-start.1 = (bf16[128,512]{1,0:T(8,128)(2,1)S(1)}, bf16[128,512]{1,0:T(8,128)(2,1)S(1)}, u32[]{:S(2)}, u32[]{:S(2)}) collective-permute-start(bf16[128,512]{1,0:T(8,128)(2,1)S(1)} %bitcast_convert_fusion), channel_id=1, source_target_pairs={{0,26},{1,27},{2,24},{3,25},{8,2},{9,3},{10,0},{11,1},{16,10},{17,... | collective-permute-start | bytes 393224 | tf_op jit(solution)/shard_map/ppermute | solution.py:45
  19.1 9.9 %collective-permute-start.2 = (bf16[128,512]{1,0:T(8,128)(2,1)S(1)}, bf16[128,512]{1,0:T(8,128)(2,1)S(1)}, u32[]{:S(2)}, u32[]{:S(2)}) collective-permute-start(bf16[128,512]{1,0:T(8,128)(2,1)S(1)} %bitcast_convert_fusion), channel_id=1, source_target_pairs={{0,27},{1,26},{2,25},{3,24},{8,3},{9,2},{10,1},{11,0},{16,11},{17,... | collective-permute-start | bytes 393224 | tf_op jit(solution)/shard_map/ppermute | solution.py:45
  54.4 15.9 %collective-permute-start.8 = (bf16[128,512]{1,0:T(8,128)(2,1)S(1)}, bf16[128,512]{1,0:T(8,128)(2,1)S(1)}, u32[]{:S(2)}, u32[]{:S(2)}) collective-permute-start(bf16[128,512]{1,0:T(8,128)(2,1)S(1)} %get-tuple-element.125), channel_id=1, source_target_pairs={{0,1},{1,0},{2,3},{3,2},{4,5},{5,4},{6,7},{7,6},{8,9},{9,8},{10,11... | collective-permute-start | bytes 393224 | tf_op jit(solution)/shard_map/ppermute | solution.py:35
  56.7 16.8 %collective-permute-start.7 = (bf16[128,512]{1,0:T(8,128)(2,1)S(1)}, bf16[128,512]{1,0:T(8,128)(2,1)S(1)}, u32[]{:S(2)}, u32[]{:S(2)}) collective-permute-start(bf16[128,512]{1,0:T(8,128)(2,1)S(1)} %get-tuple-element.120), channel_id=1, source_target_pairs={{0,2},{1,3},{2,0},{3,1},{4,6},{5,7},{6,4},{7,5},{8,10},{9,11},{10,... | collective-permute-start | bytes 393224 | tf_op jit(solution)/shard_map/ppermute | solution.py:35
  57.8 19.5 %collective-permute-start.6 = (bf16[128,512]{1,0:T(8,128)(2,1)S(1)}, bf16[128,512]{1,0:T(8,128)(2,1)S(1)}, u32[]{:S(2)}, u32[]{:S(2)}) collective-permute-start(bf16[128,512]{1,0:T(8,128)(2,1)S(1)} %get-tuple-element.119), channel_id=1, source_target_pairs={{0,3},{1,2},{2,1},{3,0},{4,7},{5,6},{6,5},{7,4},{8,11},{9,10},{10,... | collective-permute-start | bytes 393224 | tf_op jit(solution)/shard_map/ppermute | solution.py:35
  78.7 12.0 %collective-permute-start.10 = (f32[5,128]{1,0:T(8,128)S(1)}, f32[5,128]{1,0:T(8,128)S(1)}, u32[]{:S(2)}, u32[]{:S(2)}) collective-permute-start(f32[5,128]{1,0:T(8,128)S(1)} %fusion.34), channel_id=1, source_target_pairs={{0,1},{1,0},{2,3},{3,2},{4,5},{5,4},{6,7},{7,6},{8,9},{9,8},{10,11... | collective-permute-start | bytes 7688 | tf_op jit(solution)/shard_map/ppermute | solution.py:35
  99.9 15.9 %collective-permute-start.13 = (bf16[128,512]{1,0:T(8,128)(2,1)S(1)}, bf16[128,512]{1,0:T(8,128)(2,1)S(1)}, u32[]{:S(2)}, u32[]{:S(2)}) collective-permute-start(bf16[128,512]{1,0:T(8,128)(2,1)S(1)} %get-tuple-element.246), channel_id=1, source_target_pairs={{0,26},{1,27},{2,24},{3,25},{8,2},{9,3},{10,0},{11,1},{16,10},{17,... | collective-permute-start | bytes 393224 | tf_op jit(solution)/shard_map/ppermute | solution.py:45
  105.0 10.8 %collective-permute-start.14 = (bf16[128,512]{1,0:T(8,128)(2,1)S(1)}, bf16[128,512]{1,0:T(8,128)(2,1)S(1)}, u32[]{:S(2)}, u32[]{:S(2)}) collective-permute-start(bf16[128,512]{1,0:T(8,128)(2,1)S(1)} %get-tuple-element.246), channel_id=1, source_target_pairs={{0,27},{1,26},{2,25},{3,24},{8,3},{9,2},{10,1},{11,0},{16,11},{17,... | collective-permute-start | bytes 393224 | tf_op jit(solution)/shard_map/ppermute | solution.py:45
  134.1 13.2 %collective-permute-start.12 = (f32[128,512]{1,0:T(8,128)S(1)}, f32[128,512]{1,0:T(8,128)S(1)}, u32[]{:S(2)}, u32[]{:S(2)}) collective-permute-start(f32[128,512]{1,0:T(8,128)S(1)} %get-tuple-element.247), channel_id=1, source_target_pairs={{0,24},{8,0},{16,8},{24,16},{1,25},{9,1},{17,9},{25,17},{2,26},{10... | collective-permute-start | bytes 786440 | tf_op jit(solution)/shard_map/ppermute | solution.py:27
  145.0 10.9 %collective-permute-start.19 = (bf16[128,512]{1,0:T(8,128)(2,1)S(1)}, bf16[128,512]{1,0:T(8,128)(2,1)S(1)}, u32[]{:S(2)}, u32[]{:S(2)}) collective-permute-start(bf16[128,512]{1,0:T(8,128)(2,1)S(1)} %get-tuple-element.135), channel_id=1, source_target_pairs={{0,2},{1,3},{2,0},{3,1},{4,6},{5,7},{6,4},{7,5},{8,10},{9,11},{10,... | collective-permute-start | bytes 393224 | tf_op jit(solution)/shard_map/ppermute | solution.py:35
  145.0 10.9 %collective-permute-start.18 = (bf16[128,512]{1,0:T(8,128)(2,1)S(1)}, bf16[128,512]{1,0:T(8,128)(2,1)S(1)}, u32[]{:S(2)}, u32[]{:S(2)}) collective-permute-start(bf16[128,512]{1,0:T(8,128)(2,1)S(1)} %get-tuple-element.134), channel_id=1, source_target_pairs={{0,3},{1,2},{2,1},{3,0},{4,7},{5,6},{6,5},{7,4},{8,11},{9,10},{10,... | collective-permute-start | bytes 393224 | tf_op jit(solution)/shard_map/ppermute | solution.py:35
  156.1 11.6 %collective-permute-start.27 = (bf16[128,512]{1,0:T(8,128)(2,1)S(1)}, bf16[128,512]{1,0:T(8,128)(2,1)S(1)}, u32[]{:S(2)}, u32[]{:S(2)}) collective-permute-start(bf16[128,512]{1,0:T(8,128)(2,1)S(1)} %get-tuple-element.242), channel_id=1, source_target_pairs={{0,24},{1,25},{2,26},{3,27},{8,0},{9,1},{10,2},{11,3},{16,8},{17,9... | collective-permute-start | bytes 393224 | tf_op jit(solution)/shard_map/ppermute | solution.py:45
  157.1 10.6 %collective-permute-start.28 = (bf16[128,512]{1,0:T(8,128)(2,1)S(1)}, bf16[128,512]{1,0:T(8,128)(2,1)S(1)}, u32[]{:S(2)}, u32[]{:S(2)}) collective-permute-start(bf16[128,512]{1,0:T(8,128)(2,1)S(1)} %get-tuple-element.242), channel_id=1, source_target_pairs={{0,25},{1,24},{2,27},{3,26},{8,1},{9,0},{10,3},{11,2},{16,9},{17,8... | collective-permute-start | bytes 393224 | tf_op jit(solution)/shard_map/ppermute | solution.py:45
  164.1 11.1 %collective-permute-start.25 = (bf16[128,512]{1,0:T(8,128)(2,1)S(1)}, bf16[128,512]{1,0:T(8,128)(2,1)S(1)}, u32[]{:S(2)}, u32[]{:S(2)}) collective-permute-start(bf16[128,512]{1,0:T(8,128)(2,1)S(1)} %get-tuple-element.242), channel_id=1, source_target_pairs={{0,26},{1,27},{2,24},{3,25},{8,2},{9,3},{10,0},{11,1},{16,10},{17,... | collective-permute-start | bytes 393224 | tf_op jit(solution)/shard_map/ppermute | solution.py:45
  164.5 10.8 %collective-permute-start.26 = (bf16[128,512]{1,0:T(8,128)(2,1)S(1)}, bf16[128,512]{1,0:T(8,128)(2,1)S(1)}, u32[]{:S(2)}, u32[]{:S(2)}) collective-permute-start(bf16[128,512]{1,0:T(8,128)(2,1)S(1)} %get-tuple-element.242), channel_id=1, source_target_pairs={{0,27},{1,26},{2,25},{3,24},{8,3},{9,2},{10,1},{11,0},{16,11},{17,... | collective-permute-start | bytes 393224 | tf_op jit(solution)/shard_map/ppermute | solution.py:45
  193.6 12.6 %collective-permute-start.24 = (f32[128,512]{1,0:T(8,128)S(1)}, f32[128,512]{1,0:T(8,128)S(1)}, u32[]{:S(2)}, u32[]{:S(2)}) collective-permute-start(f32[128,512]{1,0:T(8,128)S(1)} %get-tuple-element.243), channel_id=1, source_target_pairs={{0,24},{8,0},{16,8},{24,16},{1,25},{9,1},{17,9},{25,17},{2,26},{10... | collective-permute-start | bytes 786440 | tf_op jit(solution)/shard_map/ppermute | solution.py:27
  201.8 12.3 %collective-permute-start.31 = (bf16[128,512]{1,0:T(8,128)(2,1)S(1)}, bf16[128,512]{1,0:T(8,128)(2,1)S(1)}, u32[]{:S(2)}, u32[]{:S(2)}) collective-permute-start(bf16[128,512]{1,0:T(8,128)(2,1)S(1)} %get-tuple-element.151), channel_id=1, source_target_pairs={{0,2},{1,3},{2,0},{3,1},{4,6},{5,7},{6,4},{7,5},{8,10},{9,11},{10,... | collective-permute-start | bytes 393224 | tf_op jit(solution)/shard_map/ppermute | solution.py:35
  204.8 9.4 %collective-permute-start.30 = (bf16[128,512]{1,0:T(8,128)(2,1)S(1)}, bf16[128,512]{1,0:T(8,128)(2,1)S(1)}, u32[]{:S(2)}, u32[]{:S(2)}) collective-permute-start(bf16[128,512]{1,0:T(8,128)(2,1)S(1)} %get-tuple-element.150), channel_id=1, source_target_pairs={{0,3},{1,2},{2,1},{3,0},{4,7},{5,6},{6,5},{7,4},{8,11},{9,10},{10,... | collective-permute-start | bytes 393224 | tf_op jit(solution)/shard_map/ppermute | solution.py:35
  214.3 12.2 %collective-permute-start.39 = (bf16[128,512]{1,0:T(8,128)(2,1)S(1)}, bf16[128,512]{1,0:T(8,128)(2,1)S(1)}, u32[]{:S(2)}, u32[]{:S(2)}) collective-permute-start(bf16[128,512]{1,0:T(8,128)(2,1)S(1)} %get-tuple-element.238), channel_id=1, source_target_pairs={{0,24},{1,25},{2,26},{3,27},{8,0},{9,1},{10,2},{11,3},{16,8},{17,9... | collective-permute-start | bytes 393224 | tf_op jit(solution)/shard_map/ppermute | solution.py:45
  215.4 11.1 %collective-permute-start.40 = (bf16[128,512]{1,0:T(8,128)(2,1)S(1)}, bf16[128,512]{1,0:T(8,128)(2,1)S(1)}, u32[]{:S(2)}, u32[]{:S(2)}) collective-permute-start(bf16[128,512]{1,0:T(8,128)(2,1)S(1)} %get-tuple-element.238), channel_id=1, source_target_pairs={{0,25},{1,24},{2,27},{3,26},{8,1},{9,0},{10,3},{11,2},{16,9},{17,8... | collective-permute-start | bytes 393224 | tf_op jit(solution)/shard_map/ppermute | solution.py:45
  223.5 11.0 %collective-permute-start.37 = (bf16[128,512]{1,0:T(8,128)(2,1)S(1)}, bf16[128,512]{1,0:T(8,128)(2,1)S(1)}, u32[]{:S(2)}, u32[]{:S(2)}) collective-permute-start(bf16[128,512]{1,0:T(8,128)(2,1)S(1)} %get-tuple-element.238), channel_id=1, source_target_pairs={{0,26},{1,27},{2,24},{3,25},{8,2},{9,3},{10,0},{11,1},{16,10},{17,... | collective-permute-start | bytes 393224 | tf_op jit(solution)/shard_map/ppermute | solution.py:45
  225.0 9.5 %collective-permute-start.38 = (bf16[128,512]{1,0:T(8,128)(2,1)S(1)}, bf16[128,512]{1,0:T(8,128)(2,1)S(1)}, u32[]{:S(2)}, u32[]{:S(2)}) collective-permute-start(bf16[128,512]{1,0:T(8,128)(2,1)S(1)} %get-tuple-element.238), channel_id=1, source_target_pairs={{0,27},{1,26},{2,25},{3,24},{8,3},{9,2},{10,1},{11,0},{16,11},{17,... | collective-permute-start | bytes 393224 | tf_op jit(solution)/shard_map/ppermute | solution.py:45
  252.8 13.0 %collective-permute-start.36 = (f32[128,512]{1,0:T(8,128)S(1)}, f32[128,512]{1,0:T(8,128)S(1)}, u32[]{:S(2)}, u32[]{:S(2)}) collective-permute-start(f32[128,512]{1,0:T(8,128)S(1)} %get-tuple-element.239), channel_id=1, source_target_pairs={{0,24},{8,0},{16,8},{24,16},{1,25},{9,1},{17,9},{25,17},{2,26},{10... | collective-permute-start | bytes 786440 | tf_op jit(solution)/shard_map/ppermute | solution.py:27
  261.4 12.3 %collective-permute-start.43 = (bf16[128,512]{1,0:T(8,128)(2,1)S(1)}, bf16[128,512]{1,0:T(8,128)(2,1)S(1)}, u32[]{:S(2)}, u32[]{:S(2)}) collective-permute-start(bf16[128,512]{1,0:T(8,128)(2,1)S(1)} %get-tuple-element.167), channel_id=1, source_target_pairs={{0,2},{1,3},{2,0},{3,1},{4,6},{5,7},{6,4},{7,5},{8,10},{9,11},{10,... | collective-permute-start | bytes 393224 | tf_op jit(solution)/shard_map/ppermute | solution.py:35
  263.7 10.1 %collective-permute-start.42 = (bf16[128,512]{1,0:T(8,128)(2,1)S(1)}, bf16[128,512]{1,0:T(8,128)(2,1)S(1)}, u32[]{:S(2)}, u32[]{:S(2)}) collective-permute-start(bf16[128,512]{1,0:T(8,128)(2,1)S(1)} %get-tuple-element.166), channel_id=1, source_target_pairs={{0,3},{1,2},{2,1},{3,0},{4,7},{5,6},{6,5},{7,4},{8,11},{9,10},{10,... | collective-permute-start | bytes 393224 | tf_op jit(solution)/shard_map/ppermute | solution.py:35
  274.0 11.6 %collective-permute-start.51 = (bf16[128,512]{1,0:T(8,128)(2,1)S(1)}, bf16[128,512]{1,0:T(8,128)(2,1)S(1)}, u32[]{:S(2)}, u32[]{:S(2)}) collective-permute-start(bf16[128,512]{1,0:T(8,128)(2,1)S(1)} %get-tuple-element.234), channel_id=1, source_target_pairs={{0,24},{1,25},{2,26},{3,27},{8,0},{9,1},{10,2},{11,3},{16,8},{17,9... | collective-permute-start | bytes 393224 | tf_op jit(solution)/shard_map/ppermute | solution.py:45
  275.1 10.5 %collective-permute-start.52 = (bf16[128,512]{1,0:T(8,128)(2,1)S(1)}, bf16[128,512]{1,0:T(8,128)(2,1)S(1)}, u32[]{:S(2)}, u32[]{:S(2)}) collective-permute-start(bf16[128,512]{1,0:T(8,128)(2,1)S(1)} %get-tuple-element.234), channel_id=1, source_target_pairs={{0,25},{1,24},{2,27},{3,26},{8,1},{9,0},{10,3},{11,2},{16,9},{17,8... | collective-permute-start | bytes 393224 | tf_op jit(solution)/shard_map/ppermute | solution.py:45
  280.9 10.6 %collective-permute-start.49 = (bf16[128,512]{1,0:T(8,128)(2,1)S(1)}, bf16[128,512]{1,0:T(8,128)(2,1)S(1)}, u32[]{:S(2)}, u32[]{:S(2)}) collective-permute-start(bf16[128,512]{1,0:T(8,128)(2,1)S(1)} %get-tuple-element.234), channel_id=1, source_target_pairs={{0,26},{1,27},{2,24},{3,25},{8,2},{9,3},{10,0},{11,1},{16,10},{17,... | collective-permute-start | bytes 393224 | tf_op jit(solution)/shard_map/ppermute | solution.py:45
  281.3 10.1 %collective-permute-start.50 = (bf16[128,512]{1,0:T(8,128)(2,1)S(1)}, bf16[128,512]{1,0:T(8,128)(2,1)S(1)}, u32[]{:S(2)}, u32[]{:S(2)}) collective-permute-start(bf16[128,512]{1,0:T(8,128)(2,1)S(1)} %get-tuple-element.234), channel_id=1, source_target_pairs={{0,27},{1,26},{2,25},{3,24},{8,3},{9,2},{10,1},{11,0},{16,11},{17,... | collective-permute-start | bytes 393224 | tf_op jit(solution)/shard_map/ppermute | solution.py:45
  309.8 12.9 %collective-permute-start.48 = (f32[128,512]{1,0:T(8,128)S(1)}, f32[128,512]{1,0:T(8,128)S(1)}, u32[]{:S(2)}, u32[]{:S(2)}) collective-permute-start(f32[128,512]{1,0:T(8,128)S(1)} %get-tuple-element.235), channel_id=1, source_target_pairs={{0,24},{8,0},{16,8},{24,16},{1,25},{9,1},{17,9},{25,17},{2,26},{10... | collective-permute-start | bytes 786440 | tf_op jit(solution)/shard_map/ppermute | solution.py:27
  318.2 12.3 %collective-permute-start.55 = (bf16[128,512]{1,0:T(8,128)(2,1)S(1)}, bf16[128,512]{1,0:T(8,128)(2,1)S(1)}, u32[]{:S(2)}, u32[]{:S(2)}) collective-permute-start(bf16[128,512]{1,0:T(8,128)(2,1)S(1)} %get-tuple-element.183), channel_id=1, source_target_pairs={{0,2},{1,3},{2,0},{3,1},{4,6},{5,7},{6,4},{7,5},{8,10},{9,11},{10,... | collective-permute-start | bytes 393224 | tf_op jit(solution)/shard_map/ppermute | solution.py:35
  320.8 9.8 %collective-permute-start.54 = (bf16[128,512]{1,0:T(8,128)(2,1)S(1)}, bf16[128,512]{1,0:T(8,128)(2,1)S(1)}, u32[]{:S(2)}, u32[]{:S(2)}) collective-permute-start(bf16[128,512]{1,0:T(8,128)(2,1)S(1)} %get-tuple-element.182), channel_id=1, source_target_pairs={{0,3},{1,2},{2,1},{3,0},{4,7},{5,6},{6,5},{7,4},{8,11},{9,10},{10,... | collective-permute-start | bytes 393224 | tf_op jit(solution)/shard_map/ppermute | solution.py:35
  330.8 11.7 %collective-permute-start.63 = (bf16[128,512]{1,0:T(8,128)(2,1)S(1)}, bf16[128,512]{1,0:T(8,128)(2,1)S(1)}, u32[]{:S(2)}, u32[]{:S(2)}) collective-permute-start(bf16[128,512]{1,0:T(8,128)(2,1)S(1)} %get-tuple-element.230), channel_id=1, source_target_pairs={{0,24},{1,25},{2,26},{3,27},{8,0},{9,1},{10,2},{11,3},{16,8},{17,9... | collective-permute-start | bytes 393224 | tf_op jit(solution)/shard_map/ppermute | solution.py:45
  331.6 10.9 %collective-permute-start.64 = (bf16[128,512]{1,0:T(8,128)(2,1)S(1)}, bf16[128,512]{1,0:T(8,128)(2,1)S(1)}, u32[]{:S(2)}, u32[]{:S(2)}) collective-permute-start(bf16[128,512]{1,0:T(8,128)(2,1)S(1)} %get-tuple-element.230), channel_id=1, source_target_pairs={{0,25},{1,24},{2,27},{3,26},{8,1},{9,0},{10,3},{11,2},{16,9},{17,8... | collective-permute-start | bytes 393224 | tf_op jit(solution)/shard_map/ppermute | solution.py:45
  339.6 10.6 %collective-permute-start.61 = (bf16[128,512]{1,0:T(8,128)(2,1)S(1)}, bf16[128,512]{1,0:T(8,128)(2,1)S(1)}, u32[]{:S(2)}, u32[]{:S(2)}) collective-permute-start(bf16[128,512]{1,0:T(8,128)(2,1)S(1)} %get-tuple-element.230), channel_id=1, source_target_pairs={{0,26},{1,27},{2,24},{3,25},{8,2},{9,3},{10,0},{11,1},{16,10},{17,... | collective-permute-start | bytes 393224 | tf_op jit(solution)/shard_map/ppermute | solution.py:45
  340.6 9.5 %collective-permute-start.62 = (bf16[128,512]{1,0:T(8,128)(2,1)S(1)}, bf16[128,512]{1,0:T(8,128)(2,1)S(1)}, u32[]{:S(2)}, u32[]{:S(2)}) collective-permute-start(bf16[128,512]{1,0:T(8,128)(2,1)S(1)} %get-tuple-element.230), channel_id=1, source_target_pairs={{0,27},{1,26},{2,25},{3,24},{8,3},{9,2},{10,1},{11,0},{16,11},{17,... | collective-permute-start | bytes 393224 | tf_op jit(solution)/shard_map/ppermute | solution.py:45
  368.5 13.0 %collective-permute-start.60 = (f32[128,512]{1,0:T(8,128)S(1)}, f32[128,512]{1,0:T(8,128)S(1)}, u32[]{:S(2)}, u32[]{:S(2)}) collective-permute-start(f32[128,512]{1,0:T(8,128)S(1)} %get-tuple-element.231), channel_id=1, source_target_pairs={{0,24},{8,0},{16,8},{24,16},{1,25},{9,1},{17,9},{25,17},{2,26},{10... | collective-permute-start | bytes 786440 | tf_op jit(solution)/shard_map/ppermute | solution.py:27
  377.1 12.3 %collective-permute-start.67 = (bf16[128,512]{1,0:T(8,128)(2,1)S(1)}, bf16[128,512]{1,0:T(8,128)(2,1)S(1)}, u32[]{:S(2)}, u32[]{:S(2)}) collective-permute-start(bf16[128,512]{1,0:T(8,128)(2,1)S(1)} %get-tuple-element.199), channel_id=1, source_target_pairs={{0,2},{1,3},{2,0},{3,1},{4,6},{5,7},{6,4},{7,5},{8,10},{9,11},{10,... | collective-permute-start | bytes 393224 | tf_op jit(solution)/shard_map/ppermute | solution.py:35
  379.5 9.9 %collective-permute-start.66 = (bf16[128,512]{1,0:T(8,128)(2,1)S(1)}, bf16[128,512]{1,0:T(8,128)(2,1)S(1)}, u32[]{:S(2)}, u32[]{:S(2)}) collective-permute-start(bf16[128,512]{1,0:T(8,128)(2,1)S(1)} %get-tuple-element.198), channel_id=1, source_target_pairs={{0,3},{1,2},{2,1},{3,0},{4,7},{5,6},{6,5},{7,4},{8,11},{9,10},{10,... | collective-permute-start | bytes 393224 | tf_op jit(solution)/shard_map/ppermute | solution.py:35
  389.6 11.6 %collective-permute-start.75 = (bf16[128,512]{1,0:T(8,128)(2,1)S(1)}, bf16[128,512]{1,0:T(8,128)(2,1)S(1)}, u32[]{:S(2)}, u32[]{:S(2)}) collective-permute-start(bf16[128,512]{1,0:T(8,128)(2,1)S(1)} %get-tuple-element.226), channel_id=1, source_target_pairs={{0,24},{1,25},{2,26},{3,27},{8,0},{9,1},{10,2},{11,3},{16,8},{17,9... | collective-permute-start | bytes 393224 | tf_op jit(solution)/shard_map/ppermute | solution.py:45
  390.5 10.8 %collective-permute-start.76 = (bf16[128,512]{1,0:T(8,128)(2,1)S(1)}, bf16[128,512]{1,0:T(8,128)(2,1)S(1)}, u32[]{:S(2)}, u32[]{:S(2)}) collective-permute-start(bf16[128,512]{1,0:T(8,128)(2,1)S(1)} %get-tuple-element.226), channel_id=1, source_target_pairs={{0,25},{1,24},{2,27},{3,26},{8,1},{9,0},{10,3},{11,2},{16,9},{17,8... | collective-permute-start | bytes 393224 | tf_op jit(solution)/shard_map/ppermute | solution.py:45
  396.8 10.6 %collective-permute-start.73 = (bf16[128,512]{1,0:T(8,128)(2,1)S(1)}, bf16[128,512]{1,0:T(8,128)(2,1)S(1)}, u32[]{:S(2)}, u32[]{:S(2)}) collective-permute-start(bf16[128,512]{1,0:T(8,128)(2,1)S(1)} %get-tuple-element.226), channel_id=1, source_target_pairs={{0,26},{1,27},{2,24},{3,25},{8,2},{9,3},{10,0},{11,1},{16,10},{17,... | collective-permute-start | bytes 393224 | tf_op jit(solution)/shard_map/ppermute | solution.py:45
  397.8 9.6 %collective-permute-start.74 = (bf16[128,512]{1,0:T(8,128)(2,1)S(1)}, bf16[128,512]{1,0:T(8,128)(2,1)S(1)}, u32[]{:S(2)}, u32[]{:S(2)}) collective-permute-start(bf16[128,512]{1,0:T(8,128)(2,1)S(1)} %get-tuple-element.226), channel_id=1, source_target_pairs={{0,27},{1,26},{2,25},{3,24},{8,3},{9,2},{10,1},{11,0},{16,11},{17,... | collective-permute-start | bytes 393224 | tf_op jit(solution)/shard_map/ppermute | solution.py:45
  425.8 12.9 %collective-permute-start.72 = (f32[128,512]{1,0:T(8,128)S(1)}, f32[128,512]{1,0:T(8,128)S(1)}, u32[]{:S(2)}, u32[]{:S(2)}) collective-permute-start(f32[128,512]{1,0:T(8,128)S(1)} %get-tuple-element.227), channel_id=1, source_target_pairs={{0,24},{8,0},{16,8},{24,16},{1,25},{9,1},{17,9},{25,17},{2,26},{10... | collective-permute-start | bytes 786440 | tf_op jit(solution)/shard_map/ppermute | solution.py:27
  434.4 12.3 %collective-permute-start.79 = (bf16[128,512]{1,0:T(8,128)(2,1)S(1)}, bf16[128,512]{1,0:T(8,128)(2,1)S(1)}, u32[]{:S(2)}, u32[]{:S(2)}) collective-permute-start(bf16[128,512]{1,0:T(8,128)(2,1)S(1)} %get-tuple-element.215), channel_id=1, source_target_pairs={{0,2},{1,3},{2,0},{3,1},{4,6},{5,7},{6,4},{7,5},{8,10},{9,11},{10,... | collective-permute-start | bytes 393224 | tf_op jit(solution)/shard_map/ppermute | solution.py:35
  436.8 9.9 %collective-permute-start.78 = (bf16[128,512]{1,0:T(8,128)(2,1)S(1)}, bf16[128,512]{1,0:T(8,128)(2,1)S(1)}, u32[]{:S(2)}, u32[]{:S(2)}) collective-permute-start(bf16[128,512]{1,0:T(8,128)(2,1)S(1)} %get-tuple-element.214), channel_id=1, source_target_pairs={{0,3},{1,2},{2,1},{3,0},{4,7},{5,6},{6,5},{7,4},{8,11},{9,10},{10,... | collective-permute-start | bytes 393224 | tf_op jit(solution)/shard_map/ppermute | solution.py:35
  (58 other events, 555.7 us)
Sparse Core Ops, SparseCore 0:
  34.6 57.8 all-gather.1
